TPU v7x, 32 devices: a whole 2x2x4 slice. The times are simulated.
32 devices in a mesh: dp: 8 (over z, core), ctx: 4 (over y, x).
Axes of the slice: x: 2, y: 2, z: 4, core: 2. Of those that a mesh axis runs over, the one named last changes fastest.
Arguments:
- hidden_in: bfloat16 [8, 2048, 2048], P('dp', 'ctx'), may hold values from -6 to 6
- ln_gain: bfloat16 [2048], P(('dp', 'ctx')), may hold values from 0.099609375 to 1.8984375
- ln_bias: bfloat16 [2048], P(('dp', 'ctx')), may hold values from -4 to 4
- w_qkv: bfloat16 [2048, 6144], P(('dp', 'ctx')), may hold values from -0.125 to 0.125
- b_qkv: bfloat16 [6144], P(('dp', 'ctx')), may hold values from -4 to 4
- w_out: bfloat16 [2048, 2048], P(('dp', 'ctx')), may hold values from -2 to 2
- b_out: bfloat16 [2048], P(('dp', 'ctx')), may hold values from -4 to 4
- w_up: bfloat16 [2048, 8192], P(('dp', 'ctx')), may hold values from -0.125 to 0.125
- b_up: bfloat16 [8192], P(('dp', 'ctx')), may hold values from -4 to 4
- w_down: bfloat16 [8192, 2048], P(('dp', 'ctx')), may hold values from -0.0625 to 0.0625
- b_down: bfloat16 [2048], P(('dp', 'ctx')), may hold values from -4 to 4
- segment_ids: int32 [8, 2048], P('dp'), may hold values from 0 to 3, as said below
- positions: int32 [8, 2048], P('dp', 'ctx'), may hold values from 0 to 1023, as said below
- token_order: int32 [8, 2048], P('dp'), may hold values from 0 to 2047, as said below
- grad_out: bfloat16 [8, 2048, 2048], P('dp', 'ctx'), may hold values from -6 to 6
Outputs:
- output: bfloat16 [8, 2048, 2048], P('dp', 'ctx')
- grad_in: bfloat16 [8, 2048, 2048], P('dp', 'ctx')
- grad_ln_gain: float32 [2048], P(('dp', 'ctx'))
- grad_ln_bias: float32 [2048], P(('dp', 'ctx'))
- grad_w_qkv: float32 [2048, 6144], P(('dp', 'ctx'))
- grad_b_qkv: float32 [6144], P(('dp', 'ctx'))
- grad_w_out: float32 [2048, 2048], P(('dp', 'ctx'))
- grad_b_out: float32 [2048], P(('dp', 'ctx'))
- grad_w_up: float32 [2048, 8192], P(('dp', 'ctx'))
- grad_b_up: float32 [8192], P(('dp', 'ctx'))
- grad_w_down: float32 [8192, 2048], P(('dp', 'ctx'))
- grad_b_down: float32 [2048], P(('dp', 'ctx'))
Inputs may be any that keep to these rules, and one draw needn't show every extreme that they name: Each row's places 0 to 2047 form 4 documents of consecutive places, numbered in order of place, one of which holds exactly 1024 places; segment_ids gives the document of the place token_order assigns to each slot. `positions`: A slot's place minus the first place of its document. `token_order`: each row is a permutation of its places that moves whole runs of 128 places: slots 128 b to 128 b + 127 hold the places of one run in rising order.
All inputs are finite; a program needn't handle non-finite values.
Results may differ from a plain program's by a relative error of at most 0.0095.
Values may be sent and summed in bfloat16 or wider, within the bound.
No kernel may reach another device: no remote copies, remote signals or barrier semaphores. Data moves between devices by JAX's collectives and lax.ppermute only.
A program may use at most 512 MiB of HBM per device.

v0:
```python
import math

import jax
import jax.numpy as jnp
from jax import lax
from jax.sharding import PartitionSpec as P

HEAD = 64
ROT = 32


EPS = 1e-05
NEG = -1e30


def norm_rows(values, gain, shift):
    average = jnp.mean(values, axis=-1, keepdims=True)
    centred = values - average
    variance = jnp.mean(centred * centred, axis=-1, keepdims=True)
    return centred * lax.rsqrt(variance + EPS) * gain + shift


def angle_table(position_rows):
    half_width = ROT // 2
    frequency = 10000.0 ** (-jnp.arange(half_width, dtype=jnp.float32) * 2.0 / ROT)
    angles = position_rows.astype(jnp.float32)[..., None] * frequency
    return (jnp.cos(angles)[..., None, :], jnp.sin(angles)[..., None, :])


def rotate(values, cosine, sine_table):
    half_width = cosine.shape[-1]
    front_part = values[..., :half_width]
    back_part = values[..., half_width : 2 * half_width]
    return jnp.concatenate(
        [
            front_part * cosine - back_part * sine_table,
            back_part * cosine + front_part * sine_table,
            values[..., 2 * half_width :],
        ],
        axis=-1,
    )


def unrotate(gradient, cosine, sine_table):
    half_width = cosine.shape[-1]
    front_part = gradient[..., :half_width]
    back_part = gradient[..., half_width : 2 * half_width]
    return jnp.concatenate(
        [
            front_part * cosine + back_part * sine_table,
            back_part * cosine - front_part * sine_table,
            gradient[..., 2 * half_width :],
        ],
        axis=-1,
    )


def head_groups(tensor, group_size):
    row_count, slot_count, head_count, head_width = tensor.shape
    shaped = tensor.reshape(row_count, slot_count, head_count // group_size, group_size, head_width)
    return jnp.moveaxis(shaped, 2, 0)


def join_groups(tensor):
    group_count, row_count, slot_count, group_size, head_width = tensor.shape
    return jnp.moveaxis(tensor, 0, 2).reshape(
        row_count, slot_count, group_count * group_size, head_width
    )


def masked_scores(q_group, k_group, allowed, score_scale):
    scores = (
        jnp.einsum("btge,blge->bgtl", q_group, k_group, preferred_element_type=jnp.float32)
        * score_scale
    )
    return jnp.where(allowed[:, None], scores, NEG)


def attend(queries, keys_all, values_all, allowed, score_scale):

    def one_group(pieces):
        q_group, k_group, v_group = pieces
        scores = masked_scores(q_group, k_group, allowed, score_scale)
        row_top = jnp.max(scores, axis=-1, keepdims=True)
        weights = jnp.exp(scores - row_top)
        totals = jnp.sum(weights, axis=-1, keepdims=True)
        probabilities = (weights / totals).astype(jnp.bfloat16)
        mixed_out = jnp.einsum(
            "bgtl,blge->btge", probabilities, v_group, preferred_element_type=jnp.float32
        )
        return (mixed_out.astype(jnp.bfloat16), (row_top + jnp.log(totals))[..., 0])

    return lax.map(one_group, (queries, keys_all, values_all))


def attend_back(queries, keys_all, values_all, d_attended, log_totals, allowed, score_scale):

    def one_group(pieces):
        q_group, k_group, v_group, d_group, l_group = pieces
        scores = masked_scores(q_group, k_group, allowed, score_scale)
        probs_full = jnp.exp(scores - l_group[..., None])
        probs_low = probs_full.astype(jnp.bfloat16)
        d_probs = jnp.einsum(
            "btge,blge->bgtl", d_group, v_group, preferred_element_type=jnp.float32
        )
        inner_sum = jnp.sum(probs_full * d_probs, axis=-1, keepdims=True)
        d_scores = (probs_full * (d_probs - inner_sum)).astype(jnp.bfloat16)
        d_query = (
            jnp.einsum("bgtl,blge->btge", d_scores, k_group, preferred_element_type=jnp.float32)
            * score_scale
        )
        d_key = (
            jnp.einsum("bgtl,btge->blge", d_scores, q_group, preferred_element_type=jnp.float32)
            * score_scale
        )
        d_value = jnp.einsum(
            "bgtl,btge->blge", probs_low, d_group, preferred_element_type=jnp.float32
        )
        return (d_query, d_key, d_value)

    return lax.map(one_group, (queries, keys_all, values_all, d_attended, log_totals))


def run_forward(weights, hidden_in, positions, segment_ids, token_order, fetch):
    w_qkv, w_out, w_up, w_down, b_qkv, b_out, b_up, b_down, ln_gain, ln_bias = weights
    row_count, slot_count, feature = hidden_in.shape
    head_count = feature // HEAD
    group_size = math.gcd(head_count, 4)
    hidden_f = hidden_in.astype(jnp.float32)
    normed = norm_rows(hidden_f, ln_gain.astype(jnp.float32), ln_bias.astype(jnp.float32)).astype(
        jnp.bfloat16
    )
    qkv = jnp.einsum(
        "btd,df->btf", normed, w_qkv, preferred_element_type=jnp.float32
    ) + b_qkv.astype(jnp.float32)
    cosine, sine_table = angle_table(positions)
    queries = rotate(
        qkv[..., :feature].reshape(row_count, slot_count, head_count, HEAD), cosine, sine_table
    ).astype(jnp.bfloat16)
    keys_local = rotate(
        qkv[..., feature : 2 * feature].reshape(row_count, slot_count, head_count, HEAD),
        cosine,
        sine_table,
    ).astype(jnp.bfloat16)
    values_local = qkv[..., 2 * feature :].astype(jnp.bfloat16)
    keys_all, values_all = fetch(keys_local.reshape(row_count, slot_count, feature), values_local)
    slot_start = lax.axis_index("ctx") * slot_count
    segment_local = lax.dynamic_slice_in_dim(segment_ids, slot_start, slot_count, 1)
    order_local = lax.dynamic_slice_in_dim(token_order, slot_start, slot_count, 1)
    allowed = (segment_local[:, :, None] == segment_ids[:, None, :]) & (
        token_order[:, None, :] <= order_local[:, :, None]
    )
    keys_heads = keys_all.reshape(row_count, -1, head_count, HEAD)
    values_heads = values_all.reshape(row_count, -1, head_count, HEAD)
    mixed_out, log_totals = attend(
        head_groups(queries, group_size),
        head_groups(keys_heads, group_size),
        head_groups(values_heads, group_size),
        allowed,
        HEAD ** (-0.5),
    )
    attended = join_groups(mixed_out).reshape(row_count, slot_count, feature)
    attn_out = jnp.einsum(
        "btd,de->bte", attended, w_out, preferred_element_type=jnp.float32
    ) + b_out.astype(jnp.float32)
    up_proj = jnp.einsum(
        "btd,df->btf", normed, w_up, preferred_element_type=jnp.float32
    ) + b_up.astype(jnp.float32)
    active = jax.nn.gelu(up_proj, approximate=True).astype(jnp.bfloat16)
    mlp_out = jnp.einsum(
        "btf,fd->btd", active, w_down, preferred_element_type=jnp.float32
    ) + b_down.astype(jnp.float32)
    output = (hidden_f + attn_out + mlp_out).astype(jnp.bfloat16)
    return (
        hidden_f,
        normed,
        queries,
        keys_heads,
        values_heads,
        allowed,
        attended,
        log_totals,
        up_proj,
        active,
        output,
        cosine,
        sine_table,
        group_size,
    )


def outer_rows(left, right):

    def term(start, count):
        return jnp.einsum("btd,btf->df", left, right, preferred_element_type=jnp.float32)

    return term


def reduce_rows(term, own_rows):
    return lax.psum_scatter(
        term(jnp.int32(0), own_rows * lax.axis_size(("dp", "ctx"))),
        ("dp", "ctx"),
        scatter_dimension=0,
        tiled=True,
    )


def on_device(
    hidden_in,
    ln_gain,
    ln_bias,
    w_qkv,
    b_qkv,
    w_out,
    b_out,
    w_up,
    b_up,
    w_down,
    b_down,
    segment_ids,
    positions,
    token_order,
    grad_out,
):
    weights = (
        lax.all_gather(w_qkv, ("dp", "ctx"), axis=0, tiled=True),
        lax.all_gather(w_out, ("dp", "ctx"), axis=0, tiled=True),
        lax.all_gather(w_up, ("dp", "ctx"), axis=0, tiled=True),
        lax.all_gather(w_down, ("dp", "ctx"), axis=0, tiled=True),
        lax.all_gather(b_qkv, ("dp", "ctx"), axis=0, tiled=True),
        lax.all_gather(b_out, ("dp", "ctx"), axis=0, tiled=True),
        lax.all_gather(b_up, ("dp", "ctx"), axis=0, tiled=True),
        lax.all_gather(b_down, ("dp", "ctx"), axis=0, tiled=True),
        lax.all_gather(ln_gain, ("dp", "ctx"), axis=0, tiled=True),
        lax.all_gather(ln_bias, ("dp", "ctx"), axis=0, tiled=True),
    )

    def fetch_first(keys_local, values_local):
        return (
            lax.all_gather(keys_local, "ctx", axis=1, tiled=True),
            lax.all_gather(values_local, "ctx", axis=1, tiled=True),
        )

    state = run_forward(weights, hidden_in, positions, segment_ids, token_order, fetch_first)
    output = state[10]
    weights = (
        lax.all_gather(w_qkv, ("dp", "ctx"), axis=0, tiled=True),
        lax.all_gather(w_out, ("dp", "ctx"), axis=0, tiled=True),
        lax.all_gather(w_up, ("dp", "ctx"), axis=0, tiled=True),
        lax.all_gather(w_down, ("dp", "ctx"), axis=0, tiled=True),
        lax.all_gather(b_qkv, ("dp", "ctx"), axis=0, tiled=True),
        lax.all_gather(b_out, ("dp", "ctx"), axis=0, tiled=True),
        lax.all_gather(b_up, ("dp", "ctx"), axis=0, tiled=True),
        lax.all_gather(b_down, ("dp", "ctx"), axis=0, tiled=True),
        lax.all_gather(ln_gain, ("dp", "ctx"), axis=0, tiled=True),
        lax.all_gather(ln_bias, ("dp", "ctx"), axis=0, tiled=True),
    )

    def fetch_again(keys_local, values_local):
        return (
            lax.all_gather(keys_local, "ctx", axis=1, tiled=True),
            lax.all_gather(values_local, "ctx", axis=1, tiled=True),
        )

    state = run_forward(weights, hidden_in, positions, segment_ids, token_order, fetch_again)
    hidden_f, normed, queries, keys_heads, values_heads, allowed = (
        state[0],
        state[1],
        state[2],
        state[3],
        state[4],
        state[5],
    )
    attended, log_totals, up_proj, active = (state[6], state[7], state[8], state[9])
    cosine, sine_table, group_size = (state[11], state[12], state[13])
    w_qkv_all, w_out_all, w_up_all, w_down_all = (weights[0], weights[1], weights[2], weights[3])
    gain_all = weights[8].astype(jnp.float32)
    shift_all = weights[9].astype(jnp.float32)
    row_count, slot_count, feature = hidden_in.shape
    head_count = feature // HEAD
    grad_f = grad_out.astype(jnp.float32)
    bias_grad = jnp.sum(grad_f, axis=(0, 1))
    down_grad = reduce_rows(outer_rows(active, grad_out), w_down.shape[0])
    d_active = jnp.einsum("btd,fd->btf", grad_out, w_down_all, preferred_element_type=jnp.float32)
    gelu_back = jax.vjp(lambda pre_act: jax.nn.gelu(pre_act, approximate=True), up_proj)[1]
    d_up = gelu_back(d_active)[0].astype(jnp.bfloat16)
    up_bias_grad = jnp.sum(d_up.astype(jnp.float32), axis=(0, 1))
    up_grad = reduce_rows(outer_rows(normed, d_up), w_up.shape[0])
    d_normed = jnp.einsum("btf,df->btd", d_up, w_up_all, preferred_element_type=jnp.float32)
    out_grad = reduce_rows(outer_rows(attended, grad_out), w_out.shape[0])
    d_attended = jnp.einsum(
        "bte,de->btd", grad_out, w_out_all, preferred_element_type=jnp.float32
    ).astype(jnp.bfloat16)
    d_groups = head_groups(d_attended.reshape(row_count, slot_count, head_count, HEAD), group_size)
    d_query, d_key, d_value = attend_back(
        head_groups(queries, group_size),
        head_groups(keys_heads, group_size),
        head_groups(values_heads, group_size),
        d_groups,
        log_totals,
        allowed,
        HEAD ** (-0.5),
    )
    d_query = join_groups(d_query)
    d_key_all = join_groups(d_key).reshape(row_count, -1, feature)
    d_value_all = join_groups(d_value).reshape(row_count, -1, feature)
    d_key_own, d_value_own = (
        lax.psum_scatter(d_key_all, "ctx", scatter_dimension=1, tiled=True),
        lax.psum_scatter(d_value_all, "ctx", scatter_dimension=1, tiled=True),
    )
    d_qkv = jnp.concatenate(
        [
            unrotate(d_query, cosine, sine_table).reshape(row_count, slot_count, feature),
            unrotate(
                d_key_own.reshape(row_count, slot_count, head_count, HEAD), cosine, sine_table
            ).reshape(row_count, slot_count, feature),
            d_value_own,
        ],
        axis=-1,
    ).astype(jnp.bfloat16)
    qkv_bias_grad = jnp.sum(d_qkv.astype(jnp.float32), axis=(0, 1))
    qkv_grad = reduce_rows(outer_rows(normed, d_qkv), w_qkv.shape[0])
    d_normed = d_normed + jnp.einsum(
        "btf,df->btd", d_qkv, w_qkv_all, preferred_element_type=jnp.float32
    )
    norm_back = jax.vjp(norm_rows, hidden_f, gain_all, shift_all)[1]
    d_hidden, gain_grad, shift_grad = norm_back(d_normed)
    grad_in = (grad_f + d_hidden).astype(jnp.bfloat16)
    small = (
        lax.psum_scatter(qkv_bias_grad, ("dp", "ctx"), scatter_dimension=0, tiled=True),
        lax.psum_scatter(bias_grad, ("dp", "ctx"), scatter_dimension=0, tiled=True),
        lax.psum_scatter(up_bias_grad, ("dp", "ctx"), scatter_dimension=0, tiled=True),
        lax.psum_scatter(gain_grad, ("dp", "ctx"), scatter_dimension=0, tiled=True),
        lax.psum_scatter(shift_grad, ("dp", "ctx"), scatter_dimension=0, tiled=True),
    )
    return (
        output,
        grad_in,
        small[3],
        small[4],
        qkv_grad,
        small[0],
        out_grad,
        small[1],
        up_grad,
        small[2],
        down_grad,
        small[1],
    )


def solution(mesh):
    in_specs = (
        P("dp", "ctx", None),
        P(("dp", "ctx")),
        P(("dp", "ctx")),
        P(("dp", "ctx"), None),
        P(("dp", "ctx")),
        P(("dp", "ctx"), None),
        P(("dp", "ctx")),
        P(("dp", "ctx"), None),
        P(("dp", "ctx")),
        P(("dp", "ctx"), None),
        P(("dp", "ctx")),
        P("dp", None),
        P("dp", "ctx"),
        P("dp", None),
        P("dp", "ctx", None),
    )
    out_specs = (
        P("dp", "ctx", None),
        P("dp", "ctx", None),
        P(("dp", "ctx")),
        P(("dp", "ctx")),
        P(("dp", "ctx"), None),
        P(("dp", "ctx")),
        P(("dp", "ctx"), None),
        P(("dp", "ctx")),
        P(("dp", "ctx"), None),
        P(("dp", "ctx")),
        P(("dp", "ctx"), None),
        P(("dp", "ctx")),
    )
    return jax.shard_map(
        on_device, mesh=mesh, in_specs=in_specs, out_specs=out_specs, check_vma=False
    )
```

profile of v0, /device:TPU:0, one launch (start us, length us, event | category | flops | bytes accessed | tf_op | source)
XLA Modules:
  0.0 5174.0 jit_solution(12216584643388351475)
XLA Ops:
  13.0 44.1 all-reduce.11
  60.4 109.6 %all-gather.8.cloned.1.call-done = bf16[2048,6144]{1,0:T(8,128)(2,1)} async-done(((bf16[64,6144]{1,0:T(8,128)(2,1)}), bf16[2048,6144]{1,0:T(8,128)(2,1)}) %all-gather.8.cloned.1.call-update) | async-done | bytes 25165840 | tf_op jit(solution)/shard_map/all_gather | solution.py:227
  170.0 20.8 add_bitcast_fusion
  221.5 27.2 all-gather.14.cloned.1.call-done
  262.0 75.2 %all-gather.10.cloned.1.call-done = bf16[1,2048,2048]{2,1,0:T(8,128)(2,1)} async-done(((bf16[1,512,2048]{2,1,0:T(8,128)(2,1)}), bf16[1,2048,2048]{2,1,0:T(8,128)(2,1)}) %all-gather.10.cloned.1.call-update) | async-done | bytes 8388624 | tf_op jit(solution)/shard_map/all_gather | solution.py:242
  349.7 77.3 %all-gather.12.cloned.1.call-done = bf16[1,2048,2048]{1,2,0:T(8,128)(2,1)} async-done(((bf16[1,512,2048]{1,2,0:T(8,128)(2,1)}), bf16[1,2048,2048]{1,2,0:T(8,128)(2,1)}) %all-gather.12.cloned.1.call-update) | async-done | bytes 8388624 | tf_op jit(solution)/shard_map/all_gather | solution.py:241
  428.6 134.3 %while.40 = (s32[]{:T(128)}, bf16[8,1,512,4,64]{2,4,3,1,0:T(8,128)(2,1)}, f32[8,1,4,512]{3,2,1,0:T(4,128)S(1)}, bf16[8,1,2048,4,64]{2,4,3,1,0:T(8,128)(2,1)}, bf...) while((s32[]{:T(128)}, ...), condition=%wide.region_9.10_spmd.clone, body=%wide.region_6.9_spmd.clone.sunk | while | flops 1127348224 | bytes 57235568 | solution.py:93
  562.9 500.7 %while.41 = (s32[]{:T(128)}, f32[8,1,512,4,64]{2,4,3,1,0:T(8,128)}, f32[8,1,2048,4,64]{2,4,3,1,0:T(8,128)}, f32[8,1,2048,4,64]{2,4,3,1,0:T(8,128)}, bf16[8,1,204...) while((s32[]{:T(128)}, f32[8,1,512,4,64]{2,4,3,1,0:T(8,128)}, ...), condition=%wide.region_12.13_spmd.clone, body=%wide.region_10.12_spmd.clone.sunk | while | flops 2751068160 | bytes 189351168 | solution.py:121
  719.6 20.7 multiply_convert_fusion.5
  1065.7 66.7 %all-gather = bf16[32,1,256]{2,1,0:T(2,128)(2,1)S(1)} all-gather(bf16[1,1,256]{2,1,0:T(2,128)(2,1)S(1)} %reshape.719), channel_id=1, replica_groups=mesh['dp'=8,'ctx'=4] {'dp','ctx'}, dimensions={0}, use_global_device_ids=true | all-gather | bytes 16896 | tf_op jit(solution)/shard_map/all_gather | solution.py:233
  1134.4 27.6 fusion.138
  1162.0 34.9 convert_reduce_fusion
  1196.9 25.5 fusion.152
  1230.1 144.2 %reduce-scatter.9.cloned.1.call-done = f32[1,512,2048]{1,2,0:T(8,128)} async-done(((f32[1,2048,2048]{1,2,0:T(8,128)}), f32[1,512,2048]{1,2,0:T(8,128)}) %reduce-scatter.9.cloned.1.call-update) | async-done | bytes 4194320 | tf_op jit(solution)/shard_map/reduce_scatter | solution.py:310
  1378.1 25.8 fusion.117
  1442.1 24.0 fusion.120
  1466.1 29.6 fusion.135
  1497.3 32.4 fusion.122
  1530.6 162.6 %while.39 = (s32[]{:T(128)}, bf16[8,1,512,4,64]{2,4,3,1,0:T(8,128)(2,1)S(1)}, bf16[8,1,2048,4,64]{2,4,3,1,0:T(8,128)(2,1)}, bf16[8,1,512,4,64]{2,4,3,1,0:T(8,128...) while((s32[]{:T(128)}, ...), condition=%wide.region_5.6_spmd.clone, body=%wide.region_2.5_spmd.clone.sunk | while | flops 1102186496 | bytes 38312036 | solution.py:93
  1700.6 26.9 fusion.119
  1733.4 179.6 %reduce-scatter.13.cloned.1.call-done = f32[64,2048]{1,0:T(8,128)} async-done(((f32[2048,2048]{1,0:T(8,128)}), f32[64,2048]{1,0:T(8,128)}) %reduce-scatter.13.cloned.1.call-update) | async-done | bytes 524304 | tf_op jit(solution)/shard_map/reduce_scatter | solution.py:201
  1913.1 440.0 %reduce-scatter.11.cloned.1.call-done = f32[64,6144]{1,0:T(8,128)} async-done(((f32[2048,6144]{1,0:T(8,128)}), f32[64,6144]{1,0:T(8,128)}) %reduce-scatter.11.cloned.1.call-update) | async-done | bytes 1572880 | tf_op jit(solution)/shard_map/reduce_scatter | solution.py:201
  2353.1 1406.2 %reduce-scatter.15.cloned.1.call-done = f32[64,8192]{1,0:T(8,128)} async-done(((f32[2048,8192]{1,0:T(8,128)}), f32[64,8192]{1,0:T(8,128)}) %reduce-scatter.15.cloned.1.call-update) | async-done | bytes 2097168 | tf_op jit(solution)/shard_map/reduce_scatter | solution.py:201
  3759.3 1407.5 %reduce-scatter.17.cloned.1.call-done = f32[256,2048]{1,0:T(8,128)} async-done(((f32[8192,2048]{1,0:T(8,128)}), f32[256,2048]{1,0:T(8,128)}) %reduce-scatter.17.cloned.1.call-update) | async-done | bytes 2097168 | tf_op jit(solution)/shard_map/reduce_scatter | solution.py:201
  (377 shorter events, 902.4 us)
Async XLA Ops:
  7.2 51.9 %copy-start = (bf16[1,512,2048]{2,1,0:T(8,128)(2,1)S(1)}, bf16[1,512,2048]{2,1,0:T(8,128)(2,1)}, u32[]{:S(2)}) copy-start(bf16[1,512,2048]{2,1,0:T(8,128)(2,1)} %param.21) | copy-start | bytes 6291460
  7.2 162.8 %all-gather.8.cloned.1.call-start = ((), (), s32[]{:S(2)}) async-start(), calls=%async_computation.6 | async-start | bytes 25952256 | tf_op jit(solution)/shard_map/all_gather | solution.py:227
  7.9 240.7 %all-gather.14.cloned.1.call-start = ((), (), s32[]{:S(2)}) async-start(), calls=%async_computation.9 | async-start | bytes 8650752 | tf_op jit(solution)/shard_map/all_gather | solution.py:228
  8.7 328.6 %all-gather.10.cloned.1.call-start = ((), (), s32[]{:S(2)}) async-start(), calls=%async_computation.7 | async-start | bytes 10485760 | tf_op jit(solution)/shard_map/all_gather | solution.py:242
  57.1 133.7 %copy-start.15 = (f32[2048]{0:T(1024)}, f32[2048]{0:T(1024)S(1)}, u32[]{:S(2)}) copy-start(f32[2048]{0:T(1024)S(1)} %convert_element_type.146) | copy-start | bytes 24580
  57.1 133.7 %copy-start.21 = (f32[2048]{0:T(1024)}, f32[2048]{0:T(1024)S(1)}, u32[]{:S(2)}) copy-start(f32[2048]{0:T(1024)S(1)} %convert_element_type.147) | copy-start | bytes 24580
  59.1 131.7 %copy-start.17 = (f32[512]{0:T(512)}, f32[512]{0:T(512)S(1)}, u32[]{:S(2)}) copy-start(f32[512]{0:T(512)S(1)} %broadcast_multiply_fusion) | copy-start | bytes 6148
  60.4 130.4 %copy-start.19 = (f32[512]{0:T(512)}, f32[512]{0:T(512)S(1)}, u32[]{:S(2)}) copy-start(f32[512]{0:T(512)S(1)} %fusion.131) | copy-start | bytes 6148
  194.7 232.3 %all-gather.12.cloned.1.call-start = ((), (), s32[]{:S(2)}) async-start(), calls=%async_computation.8 | async-start | bytes 10485760 | tf_op jit(solution)/shard_map/all_gather | solution.py:241
  219.9 914.4 %all-gather.16.cloned.1.call-start = ((), (), s32[]{:S(2)}) async-start(), calls=%async_computation.10 | async-start | bytes 34603008 | tf_op jit(solution)/shard_map/all_gather | solution.py:229
  220.5 941.5 %all-gather.18.cloned.1.call-start = ((), (), s32[]{:S(2)}) async-start(), calls=%async_computation.11 | async-start | bytes 34603008 | tf_op jit(solution)/shard_map/all_gather | solution.py:230
  221.1 1001.3 %reduce-scatter.7.cloned.1.call-start = ((), (), s32[]{:S(2)}) async-start(), calls=%async_computation.12 | async-start | bytes 20971520 | tf_op jit(solution)/shard_map/reduce_scatter | solution.py:309
  1064.9 309.4 %reduce-scatter.9.cloned.1.call-start = ((), (), s32[]{:S(2)}) async-start(), calls=%async_computation.13 | async-start | bytes 20971520 | tf_op jit(solution)/shard_map/reduce_scatter | solution.py:310
  1064.9 69.4 %copy-start.1 = (bf16[1,512,2048]{2,1,0:T(8,128)(2,1)S(1)}, bf16[1,512,2048]{2,1,0:T(8,128)(2,1)}, u32[]{:S(2)}) copy-start(bf16[1,512,2048]{2,1,0:T(8,128)(2,1)} %param.21) | copy-start | bytes 6291460
  1064.9 69.4 %copy-start.16 = (f32[2048]{0:T(1024)S(1)}, f32[2048]{0:T(1024)}, u32[]{:S(2)}) copy-start(f32[2048]{0:T(1024)} %copy-done.15) | copy-start | bytes 24580
  1065.0 69.4 %copy-start.18 = (f32[512]{0:T(512)S(1)}, f32[512]{0:T(512)}, u32[]{:S(2)}) copy-start(f32[512]{0:T(512)} %copy-done.17) | copy-start | bytes 6148
  1065.0 69.4 %copy-start.20 = (f32[512]{0:T(512)S(1)}, f32[512]{0:T(512)}, u32[]{:S(2)}) copy-start(f32[512]{0:T(512)} %copy-done.19) | copy-start | bytes 6148
  1065.0 69.4 %copy-start.22 = (f32[2048]{0:T(1024)S(1)}, f32[2048]{0:T(1024)}, u32[]{:S(2)}) copy-start(f32[2048]{0:T(1024)} %copy-done.21) | copy-start | bytes 24580
  1065.6 661.9 %all-reduce.14.cloned.1.call-start = ((), (), s32[]{:S(2)}) async-start(), calls=%async_computation.18 | async-start | bytes 163840
  1428.8 484.2 %reduce-scatter.13.cloned.1.call-start = ((), (), s32[]{:S(2)}) async-start(), calls=%async_computation.15 | async-start | bytes 17301504 | tf_op jit(solution)/shard_map/reduce_scatter | solution.py:201
  1441.4 911.7 %reduce-scatter.11.cloned.1.call-start = ((), (), s32[]{:S(2)}) async-start(), calls=%async_computation.14 | async-start | bytes 51904512 | tf_op jit(solution)/shard_map/reduce_scatter | solution.py:201
  1466.0 2293.2 %reduce-scatter.15.cloned.1.call-start = ((), (), s32[]{:S(2)}) async-start(), calls=%async_computation.16 | async-start | bytes 69206016 | tf_op jit(solution)/shard_map/reduce_scatter | solution.py:201
  1495.7 3671.1 %reduce-scatter.17.cloned.1.call-start = ((), (), s32[]{:S(2)}) async-start(), calls=%async_computation.17 | async-start | bytes 69206016 | tf_op jit(solution)/shard_map/reduce_scatter | solution.py:201
  1728.3 3439.0 %copy-start.41 = (f32[64]{0:T(128)}, f32[64]{0:T(128)S(1)}, u32[]{:S(2)}) copy-start(f32[64]{0:T(128)S(1)} %dynamic-slice.3) | copy-start | bytes 772
  (63 other events, 1065.5 us)
Sparse Core Ops, SparseCore 0:
  10.9 159.0 all-gather.7
  172.8 75.7 all-gather.13
  251.0 86.1 all-gather.9
  339.5 87.4 all-gather.11
  429.8 194.8 all-gather.15
  627.3 192.9 all-gather.17
  1063.7 153.6 reduce-scatter.6
  1220.5 153.7 reduce-scatter.8
  1428.9 122.3 all-reduce.13
  1554.1 358.9 reduce-scatter.12
  1920.1 432.9 reduce-scatter.10
  2355.9 1403.3 reduce-scatter.14
  3762.2 1404.5 reduce-scatter.16
where the time goes:
time: 5180 us; the launch traced here: 5170 us
  waiting for transfers between devices  3870 us (75%)
  matrix products  870 us (17%)
  other arithmetic  234 us (5%)
  blocking collectives  111 us (2%)
  local copies, waits for them, and re-layouts  63.3 us (1%)
    reduce_scatter x4, waiting for transfers between devices, reduce_rows(): lax.psum_scatter(term(jnp.int32(0), own_rows * lax.axis_size(('dp', 'ctx'...  3430 us
    reduce_scatter x1, waiting for transfers between devices, on_device(): lax.psum_scatter(d_value_all, 'ctx', scatter_dimension=1, tiled=True)  144 us
    convert_element_type x8, other arithmetic, one_group(): d_scores = (probs_full * (d_probs - inner_sum)).astype(jnp.bfloat16)  135 us
    dot_general x16, matrix products, one_group(): jnp.einsum('bgtl,blge->btge', probabilities, v_group, preferred_element_t...  127 us
    dot_general x16, matrix products, masked_scores(): jnp.einsum('btge,blge->bgtl', q_group, k_group, preferred_element_type=jn...  111 us
    all_gather x1, waiting for transfers between devices, on_device(): lax.all_gather(w_qkv, ('dp', 'ctx'), axis=0, tiled=True)  110 us
  transfers between devices with their start and end apart: 13, of which 9 were waited for; matrix products, arithmetic and copies ran while one was open for 21% of the time, Pallas kernels for 0%

commit v1 on v0

v1 whole, which is shorter than its diff:
```python
import functools
import math

import jax
import jax.numpy as jnp
from jax import lax
from jax.experimental import pallas as pl
from jax.experimental.pallas import tpu as pltpu
from jax.sharding import PartitionSpec as P

HEAD = 64
ROT = 32
BLK = 128
DOCS = 4
EPS = 1e-05
NEG = -1e30
PAIR = 2 * HEAD
KEYS = 256
LONGEST = 1024
PAIRS = 2
LOOSE = 2
SCALE = HEAD**-0.5
ALL = ("dp", "ctx")
BF = jnp.bfloat16
F32 = jnp.float32


def partner(x):
    lane = lax.broadcasted_iota(jnp.int32, x.shape, 1) % HEAD
    return jnp.where(
        lane < ROT // 2, pltpu.roll(x, PAIR - ROT // 2, 1), pltpu.roll(x, ROT // 2, 1)
    )


def dot(a, b):
    return jnp.dot(a, b, preferred_element_type=F32)


def dot_t(a, b):
    return lax.dot_general(a, b, (((1,), (1,)), ((), ())), preferred_element_type=F32)


def aligned_rows(index, size):
    return pl.ds(pl.multiple_of(index * size, size), size)


def attention_kernel(
    place_ref,
    slot_ref,
    low_ref,
    qkv_ref,
    cot_ref,
    cos_ref,
    sin_ref,
    first_ref,
    att_ref,
    grad_ref,
    q_st,
    do_st,
    k_s,
    v_s,
    k_t,
    v_t,
    dk_s,
    dv_s,
    p_s,
    dp_s,
):
    slots = qkv_ref.shape[0]
    blocks = slots // BLK
    pairs = k_s.shape[0]
    lane_first = lax.broadcasted_iota(jnp.int32, (BLK, PAIR), 1) < HEAD
    row_first = lax.broadcasted_iota(jnp.int32, (PAIR, BLK), 0) < HEAD

    def stack(value):
        zero = jnp.zeros_like(value)
        both = [jnp.where(lane_first, value, zero), jnp.where(lane_first, zero, value)]
        return jnp.concatenate(both, axis=0).astype(BF)

    def columns(pair, which, count=3):
        start = (pair * count + which) * PAIR
        return slice(start, start + PAIR)

    def load_block(b, carry):
        rows = aligned_rows(b, BLK)
        place = place_ref[b]
        out_rows = aligned_rows(place, BLK)
        cosine = cos_ref[rows, :]
        sine = sin_ref[rows, :]
        for pair in range(pairs):
            q = qkv_ref[rows, columns(pair, 0)]
            k = qkv_ref[rows, columns(pair, 1)]
            v = qkv_ref[rows, columns(pair, 2)]
            q = (q * cosine + partner(q) * sine).astype(BF).astype(F32) * SCALE
            k = k * cosine + partner(k) * sine
            q_st[pair, aligned_rows(place, 2 * BLK), :] = stack(q)
            do = cot_ref[rows, columns(pair, 0, 1)].astype(F32)
            do_st[pair, aligned_rows(place, 2 * BLK), :] = stack(do)
            k_s[pair, out_rows, :] = k.astype(BF)
            v_s[pair, out_rows, :] = v.astype(BF)
            k_t[pair, out_rows, :] = k.T.astype(BF)
            v_t[pair, out_rows, :] = v.T.astype(BF)
        return carry

    lax.fori_loop(0, blocks, load_block, 0, unroll=LOOSE)
    dk_s[...] = jnp.zeros_like(dk_s)
    dv_s[...] = jnp.zeros_like(dv_s)

    def tiles_of(i, low, count):
        stacked = aligned_rows(i, 2 * BLK)
        first = first_ref[pl.ds(i, 1), :]
        row = lax.broadcasted_iota(jnp.int32, (KEYS, BLK), 0)
        own = i * BLK + lax.broadcasted_iota(jnp.int32, (1, BLK), 1)
        every = range(pairs)
        top = [None] * pairs
        for t in range(count):
            keys = aligned_rows(low + t, KEYS)
            part = slice(t * KEYS, (t + 1) * KEYS)
            place = (low + t) * KEYS
            allowed = row >= first - place
            if t == count - 1:
                allowed = allowed & (row <= own - place)
            allowed = jnp.concatenate([allowed, allowed], axis=1)
            for pair in every:
                s = dot_t(k_s[pair, keys, :], q_st[pair, stacked, :])
                s = jnp.where(allowed, s, NEG)
                p_s[pair, part, :] = s
                dp_s[pair, part, :] = dot_t(v_s[pair, keys, :], do_st[pair, stacked, :])
                here = jnp.max(s, axis=0, keepdims=True)
                top[pair] = here if t == 0 else jnp.maximum(top[pair], here)
        total = [0.0] * pairs
        inner = [0.0] * pairs
        for t in range(count):
            part = slice(t * KEYS, (t + 1) * KEYS)
            for pair in every:
                p = jnp.exp(p_s[pair, part, :] - top[pair])
                p_s[pair, part, :] = p
                total[pair] += jnp.sum(p, axis=0, keepdims=True)
                inner[pair] += jnp.sum(p * dp_s[pair, part, :], axis=0, keepdims=True)
        inverse = [1.0 / x for x in total]
        inner = [x * y for x, y in zip(inner, inverse)]
        out = [0.0] * pairs
        dq = [0.0] * pairs
        for t in range(count):
            part = slice(t * KEYS, (t + 1) * KEYS)
            keys = aligned_rows(low + t, KEYS)
            for pair in every:
                p = p_s[pair, part, :] * inverse[pair]
                ds = (p * (dp_s[pair, part, :] - inner[pair])).astype(BF)
                p = p.astype(BF)
                v_turned = v_t[pair, keys, :]
                k_turned = k_t[pair, keys, :]
                v_turned = jnp.concatenate([v_turned[:BLK], v_turned[BLK:]], axis=1)
                k_turned = jnp.concatenate([k_turned[:BLK], k_turned[BLK:]], axis=1)
                out[pair] += dot(v_turned, p)
                dq[pair] += dot(k_turned, ds)
                dv_s[pair, keys, :] += dot(p, do_st[pair, stacked, :])
                dk_s[pair, keys, :] += dot(ds, q_st[pair, stacked, :])
        slot_rows = aligned_rows(slot_ref[i], BLK)
        for pair in every:
            x = jnp.where(row_first, out[pair][:, :BLK], out[pair][:, BLK:]).T
            att_ref[slot_rows, columns(pair, 0, 1)] = x.astype(BF)
            x = (jnp.where(row_first, dq[pair][:, :BLK], dq[pair][:, BLK:]) * SCALE).T
            x = x * cos_ref[slot_rows, :] - partner(x) * sin_ref[slot_rows, :]
            grad_ref[slot_rows, columns(pair, 0)] = x.astype(BF)

    most = p_s.shape[1] // KEYS

    def query_block(i, carry):
        low = low_ref[i]
        count = (i * BLK) // KEYS + 1 - low
        for n in range(1, most + 1):
            pl.when(count == n)(functools.partial(tiles_of, i, low, n))
        return carry

    lax.fori_loop(0, blocks, query_block, 0)

    def store_block(b, carry):
        rows = aligned_rows(b, BLK)
        in_rows = aligned_rows(place_ref[b], BLK)
        for pair in range(pairs):
            dk = dk_s[pair, in_rows, :]
            dk = dk * cos_ref[rows, :] - partner(dk) * sin_ref[rows, :]
            grad_ref[rows, columns(pair, 1)] = dk.astype(BF)
            grad_ref[rows, columns(pair, 2)] = dv_s[pair, in_rows, :].astype(BF)
        return carry

    lax.fori_loop(0, blocks, store_block, 0, unroll=LOOSE)


def attention(qkv, cotangent, cosine, sine, first_place, block_place, slot_block):
    slots, width = qkv.shape
    groups = width // (3 * PAIR)
    pairs = math.gcd(groups, PAIRS)
    wide = pairs * PAIR
    blocks = slots // BLK
    low = first_place[:, 0] // KEYS
    once = pl.Buffered(1)
    most = min(LONGEST // KEYS + 1, slots // KEYS)
    grid_spec = pltpu.PrefetchScalarGridSpec(
        num_scalar_prefetch=3,
        grid=(groups // pairs,),
        in_specs=[
            pl.BlockSpec((slots, 3 * wide), lambda g, *_: (0, g)),
            pl.BlockSpec((slots, wide), lambda g, *_: (0, g)),
            pl.BlockSpec((slots, PAIR), lambda g, *_: (0, 0), pipeline_mode=once),
            pl.BlockSpec((slots, PAIR), lambda g, *_: (0, 0), pipeline_mode=once),
            pl.BlockSpec((blocks, BLK), lambda g, *_: (0, 0), pipeline_mode=once),
        ],
        out_specs=[
            pl.BlockSpec((slots, wide), lambda g, *_: (0, g)),
            pl.BlockSpec((slots, 3 * wide), lambda g, *_: (0, g)),
        ],
        scratch_shapes=[
            pltpu.VMEM((pairs, 2 * slots, PAIR), BF),
            pltpu.VMEM((pairs, 2 * slots, PAIR), BF),
            pltpu.VMEM((pairs, slots, PAIR), BF),
            pltpu.VMEM((pairs, slots, PAIR), BF),
            pltpu.VMEM((pairs, slots, PAIR), BF),
            pltpu.VMEM((pairs, slots, PAIR), BF),
            pltpu.VMEM((pairs, slots, PAIR), F32),
            pltpu.VMEM((pairs, slots, PAIR), F32),
            pltpu.VMEM((pairs, most * KEYS, 2 * BLK), F32),
            pltpu.VMEM((pairs, most * KEYS, 2 * BLK), F32),
        ],
    )
    tiles = groups * blocks * (blocks // 4)
    return pl.pallas_call(
        attention_kernel,
        out_shape=[
            jax.ShapeDtypeStruct((slots, groups * PAIR), BF),
            jax.ShapeDtypeStruct((slots, width), BF),
        ],
        grid_spec=grid_spec,
        compiler_params=pltpu.CompilerParams(vmem_limit_bytes=50 * 1024 * 1024),
        cost_estimate=pl.CostEstimate(
            flops=12 * tiles * 2 * BLK * BLK * PAIR * 4,
            bytes_accessed=qkv.size * 6 + cotangent.size * 4,
            transcendentals=tiles * 2 * BLK * BLK,
        ),
        name="attention",
    )(block_place, slot_block, low, qkv, cotangent, cosine, sine, first_place)


def exchange(value, axis, size, offset):
    return lax.ppermute(value, axis, [(i, i ^ offset) for i in range(size)])


def after(value, *others):
    return lax.optimization_barrier((value,) + others)[0]


def half_blocks(size):
    if size == 4:
        return [(0, 0), (0, 1), (1, 0), (2, 1), (2, 0), (3, 0), (1, 1), (3, 1)]
    return [(j, half) for j in range(size) for half in range(2)]


def gather_steps(value, size, first=None):
    half = value.shape[0] // 2
    found = {(0, 0): value[:half], (0, 1): value[half:]}
    if size != 4:
        for j in range(1, size):
            other = exchange(value, "ctx", size, j)
            found[j, 0], found[j, 1] = other[:half], other[half:]
        return found, found[1, 0]
    one = exchange(value, "ctx", size, 1)
    two = exchange(value, "ctx", size, 2)
    found[1, 0], found[1, 1] = one[:half], one[half:]
    found[2, 0], found[2, 1] = two[:half], two[half:]
    found[3, 0] = exchange(one[:half], "ctx", size, 2)
    found[3, 1] = exchange(two[half:], "ctx", size, 1)
    return found, lax.optimization_barrier((one, two))[0]


def sum_blocks(piece, size):
    if size != 4:
        total = piece(0, 2)
        for j in range(1, size):
            total = total + exchange(piece(2 * j, 2 * j + 2).astype(BF), "ctx", size, j).astype(F32)
        return total
    far = exchange(piece(4, 6).astype(BF), "ctx", size, 2).astype(F32)
    near = exchange(piece(6, 8).astype(BF), "ctx", size, 1).astype(F32)
    middle = piece(2, 4)
    own = piece(0, 2)
    half = own.shape[0] // 2
    top = exchange((middle[:half] + far[half:]).astype(BF), "ctx", size, 1)
    low = exchange((middle[half:] + near[half:]).astype(BF), "ctx", size, 2)
    top = own[:half] + far[:half] + top.astype(F32)
    low = own[half:] + near[:half] + low.astype(F32)
    return jnp.concatenate([top, low], axis=0)


def gather_small(value, devices):
    copies = jnp.broadcast_to(value, (devices,) + value.shape)
    return lax.all_to_all(copies, ALL, split_axis=0, concat_axis=0, tiled=True)


def gather_dp(value):
    return lax.all_gather(value, "dp", axis=0, tiled=True)


def scatter_dp(value):
    return lax.psum_scatter(value, "dp", scatter_dimension=0, tiled=True)


def swap_ctx(value):
    return lax.all_to_all(value, "ctx", split_axis=0, concat_axis=0, tiled=True)


def swap_ctx_steps(value, size):
    c = lax.axis_index("ctx")
    blocks = value.reshape((size, -1) + value.shape[1:])
    result = blocks
    for j in range(1, size):
        block = lax.dynamic_index_in_dim(blocks, c ^ j, 0)
        block = exchange(block, "ctx", size, j)
        result = lax.dynamic_update_slice_in_dim(result, block, c ^ j, 0)
    return result.reshape(value.shape)


def matmul(a, b):
    return jnp.dot(a, b, preferred_element_type=F32)


def matmul_t(a, b):
    return lax.dot_general(a, b, (((1,), (1,)), ((), ())), preferred_element_type=F32)


def outer(a, b):
    return lax.dot_general(a, b, (((0,), (0,)), ((), ())), preferred_element_type=F32)


def standardise(hidden):
    average = jnp.mean(hidden, axis=-1, keepdims=True)
    centred = hidden - average
    variance = jnp.mean(centred * centred, axis=-1, keepdims=True)
    scale = lax.rsqrt(variance + EPS)
    return centred * scale, scale


def gelu_pair(x):
    root = math.sqrt(2.0 / math.pi)
    t = jnp.tanh(root * (x + 0.044715 * (x * x * x)))
    value = 0.5 * x * (1.0 + t)
    slope = 0.5 * (1.0 + t) + 0.5 * x * (1.0 - t * t) * (root * (1.0 + 3 * 0.044715 * x * x))
    return value, slope


def on_device(
    hidden_in,
    ln_gain,
    ln_bias,
    w_qkv,
    b_qkv,
    w_out,
    b_out,
    w_up,
    b_up,
    w_down,
    b_down,
    segment_ids,
    positions,
    token_order,
    grad_out,
):
    N, C = lax.axis_size("dp"), lax.axis_size("ctx")
    c = lax.axis_index("ctx")
    rows, own_slots, width = hidden_in.shape
    assert rows == 1
    heads = width // HEAD
    own_heads = heads // C
    groups = own_heads // 2
    ff_block = w_down.shape[0]
    row_block = w_qkv.shape[0]
    own_ff = N * ff_block
    hidden_own = hidden_in.reshape(own_slots, width)
    grad_own = grad_out.reshape(own_slots, width)

    found, arrived = gather_steps(hidden_own, C)
    hidden_all = jnp.concatenate([found[key] for key in half_blocks(C)], axis=0)
    found, _ = gather_steps(after(grad_own, arrived), C)
    grad_all = jnp.concatenate([found[key] for key in half_blocks(C)], axis=0)

    sizes = [ln_gain.shape[0], ln_bias.shape[0], b_qkv.shape[0], b_out.shape[0]]
    sizes += [b_up.shape[0], b_down.shape[0]]
    cuts = [sum(sizes[:i]) for i in range(1, len(sizes))]
    small = jnp.concatenate([ln_gain, ln_bias, b_qkv, b_out, b_up, b_down])
    pieces = jnp.split(gather_small(small, N * C), cuts, axis=1)
    gain, shift, qkv_bias, out_bias, up_bias, down_bias = [p.reshape(-1).astype(F32) for p in pieces]
    qkv_send = w_qkv.reshape(row_block, 3, groups, 2, C, HEAD).transpose(4, 0, 2, 1, 3, 5)
    qkv_send = qkv_send.reshape(C * row_block, 3 * own_heads * HEAD)
    up_send = w_up.reshape(row_block, N, C, ff_block).transpose(2, 0, 1, 3)
    up_send = up_send.reshape(C * row_block, own_ff)
    aligned = row_block == HEAD
    if aligned:
        w_out_own = gather_dp(w_out)
    else:
        everything = lax.all_gather(w_out, ALL, axis=0, tiled=True)
        everything = everything.reshape(own_heads, C, HEAD, width)
        w_out_own = lax.dynamic_index_in_dim(everything, c, 1, keepdims=False)
        w_out_own = w_out_own.reshape(own_heads * HEAD, width)
    up_rows = swap_ctx_steps(up_send, C)
    qkv_rows = swap_ctx_steps(after(qkv_send, arrived), C)
    w_up_own = gather_dp(up_rows)
    w_qkv_own = gather_dp(qkv_rows)

    half_block = jnp.array([j for j, _ in half_blocks(C)], jnp.int32) ^ c
    half_block = 2 * half_block + jnp.array([half for _, half in half_blocks(C)], jnp.int32)
    row_order, row_ids = token_order.reshape(-1), segment_ids.reshape(-1)
    slots = row_order.shape[0]
    first = jnp.zeros_like(row_order)
    for document in range(DOCS):
        inside = row_ids == document
        first = jnp.where(inside, jnp.min(jnp.where(inside, row_order, slots)), first)
    order_all, first_all = [
        jnp.take(x.reshape(2 * C, -1), half_block, axis=0).reshape(-1) for x in (row_order, first)
    ]
    position_all = order_all - first_all
    block_place = order_all[::BLK] // BLK
    slot_block = jnp.argsort(block_place).astype(jnp.int32)
    first_place = jnp.take(first_all.reshape(-1, BLK), slot_block, axis=0)
    half = ROT // 2
    frequency = 10000.0 ** (-jnp.arange(half, dtype=F32) * 2.0 / ROT)
    angles = position_all.astype(F32)[:, None] * frequency
    cosine, sine = jnp.cos(angles), jnp.sin(angles)
    rest = jnp.zeros((slots, HEAD - ROT), F32)
    cosine = jnp.concatenate([cosine, cosine, rest + 1.0] * 2, axis=1)
    sine = jnp.concatenate([-sine, sine, rest] * 2, axis=1)

    own_bias = lax.dynamic_index_in_dim(qkv_bias.reshape(3, groups, 2, C, HEAD), c, 3, keepdims=False)
    own_bias = own_bias.transpose(1, 0, 2, 3).reshape(-1)
    hidden_all, cosine, sine, first_place, block_place, slot_block, own_bias = (
        lax.optimization_barrier(
            (hidden_all, cosine, sine, first_place, block_place, slot_block, own_bias)
        )
    )
    xhat_all, _ = standardise(hidden_all.astype(F32))
    normed = (xhat_all * gain + shift).astype(BF)
    w_down_own = gather_dp(after(w_down, arrived))
    own_up_bias = lax.dynamic_index_in_dim(up_bias.reshape(N, C, ff_block), c, 1, keepdims=False)
    up = matmul(normed, w_up_own) + own_up_bias.reshape(-1)
    value, slope = gelu_pair(up)
    active = value.astype(BF)
    down_part = outer(active, grad_all).astype(BF)
    down_grad = scatter_dp(down_part).astype(F32)

    qkv = matmul(after(normed, down_part), w_qkv_own) + own_bias
    d_attended = matmul_t(after(grad_all, down_part), w_out_own).astype(BF)
    attended, d_qkv = attention(
        qkv, d_attended, cosine, sine, first_place, block_place, slot_block
    )

    def column_grad(part, shape):
        return swap_ctx(scatter_dp(part)).reshape((C, row_block) + shape)

    qkv_part = outer(after(normed, down_grad), d_qkv).astype(BF)
    qkv_grad = column_grad(qkv_part, (groups, 3, 2, HEAD))
    qkv_grad = qkv_grad.transpose(1, 3, 2, 4, 0, 5).reshape(w_qkv.shape).astype(F32)
    out_part = outer(after(attended, qkv_part), grad_all)
    if aligned:
        out_part = out_part.astype(BF)
        out_grad = scatter_dp(out_part).astype(F32)
    else:
        spread = jnp.zeros((own_heads, C, HEAD, width), F32)
        spread = lax.dynamic_update_index_in_dim(
            spread, out_part.reshape(own_heads, HEAD, width), c, 1
        )
        out_grad = lax.psum_scatter(
            spread.reshape(heads * HEAD, width), ALL, scatter_dimension=0, tiled=True
        )

    step = own_slots // 2
    attended_then, active_then = lax.optimization_barrier((attended, active, out_part))[:2]

    def out_piece(start, stop):
        rows = slice(start * step, stop * step)
        return matmul(attended_then[rows], w_out_own) + matmul(active_then[rows], w_down_own)

    output = hidden_own.astype(F32) + sum_blocks(out_piece, C) + (out_bias + down_bias)
    output = output.astype(BF).reshape(hidden_in.shape)

    d_up = (matmul_t(after(grad_all, attended), w_down_own) * slope).astype(BF)
    up_part = outer(normed, d_up).astype(BF)
    up_grad = column_grad(up_part, (N, ff_block))
    up_grad = up_grad.transpose(1, 2, 0, 3).reshape(w_up.shape).astype(F32)

    d_qkv_then, d_up_then = lax.optimization_barrier((d_qkv, d_up, up_part))[:2]

    def normed_piece(start, stop):
        rows = slice(start * step, stop * step)
        return matmul_t(d_qkv_then[rows], w_qkv_own) + matmul_t(d_up_then[rows], w_up_own)

    d_normed = sum_blocks(normed_piece, C)
    xhat, scale = standardise(hidden_own.astype(F32))
    e = d_normed * gain
    d_hidden = e - jnp.mean(e, axis=-1, keepdims=True)
    d_hidden = (d_hidden - xhat * jnp.mean(e * xhat, axis=-1, keepdims=True)) * scale
    grad_in = (grad_own.astype(F32) + d_hidden).astype(BF).reshape(hidden_in.shape)

    devices = N * C
    gain_grad = jnp.sum(d_normed * xhat, axis=0)
    shift_grad = jnp.sum(d_normed, axis=0)
    bias_grad = jnp.sum(grad_own.astype(F32), axis=0)
    up_bias_grad = jnp.sum(d_up.astype(F32), axis=0).reshape(N, 1, ff_block)
    qkv_bias_grad = jnp.sum(d_qkv.astype(F32), axis=0).reshape(groups, 3, 2, HEAD)
    qkv_bias_grad = qkv_bias_grad.transpose(1, 0, 2, 3)[:, :, :, None, :]
    mine = jnp.arange(C) == c
    up_bias_grad = jnp.where(mine[None, :, None], up_bias_grad, 0.0)
    qkv_bias_grad = jnp.where(mine[None, None, None, :, None], qkv_bias_grad, 0.0)
    small = [gain_grad, shift_grad, qkv_bias_grad, bias_grad, up_bias_grad]
    small = jnp.concatenate([s.reshape(devices, -1) for s in small], axis=1)
    small = lax.all_to_all(small, ALL, split_axis=0, concat_axis=0, tiled=True)
    small = jnp.split(jnp.sum(small, axis=0), cuts[:4])

    return (
        output,
        grad_in,
        small[0],
        small[1],
        qkv_grad,
        small[2],
        out_grad,
        small[3],
        up_grad,
        small[4],
        down_grad,
        small[3],
    )


def solution(mesh):
    both = P(("dp", "ctx"))
    matrix = P(("dp", "ctx"), None)
    slots = P("dp", "ctx", None)
    in_specs = (
        slots,
        both,
        both,
        matrix,
        both,
        matrix,
        both,
        matrix,
        both,
        matrix,
        both,
        P("dp", None),
        P("dp", "ctx"),
        P("dp", None),
        slots,
    )
    out_specs = (
        slots,
        slots,
        both,
        both,
        matrix,
        both,
        matrix,
        both,
        matrix,
        both,
        matrix,
        both,
    )
    return jax.shard_map(
        on_device, mesh=mesh, in_specs=in_specs, out_specs=out_specs, check_vma=False
    )
```

time: 5180 us -> 784 us (0.15)
  waiting for transfers between devices: 3870 us -> 206 us
  matrix products: 870 us -> 277 us
  other arithmetic: 234 us -> 67.6 us
  blocking collectives: 111 us -> 0 us
  Pallas kernels: 0 us -> 63.2 us
  starting transfers between devices: 0.78 us -> 54.1 us
    reduce_scatter x6 -> x4, waiting for transfers between devices: 3580 us -> 0.01 us  [scatter_dp(): return lax.psum_scatter(value, 'dp', scatter_dimension=0, tiled=True)]
    dot_general x76 -> x24, matrix products: 786 us -> 277 us  [the longest x10 111 us: matmul_t(): lax.dot_general(a, b, (((1,), (1,)), ((), ())), preferred_element_type=F32)]
    all_gather x6 -> x4, waiting for transfers between devices: 289 us -> 0.02 us  [gather_dp(): return lax.all_gather(value, 'dp', axis=0, tiled=True)]
    ppermute x0 -> x22, waiting for transfers between devices: none -> 169 us  [exchange(): return lax.ppermute(value, axis, [(i, i ^ offset) for i in range(size)])]
    convert_element_type x15 -> x14, other arithmetic: 135 us -> 27.8 us  [the longest x1 6.29 us: on_device(): (grad_own.astype(F32) + d_hidden).astype(BF).reshape(hidden_in.shape)]
    sub x8 -> x0, matrix products: 83.8 us -> none  [one_group(): weights = jnp.exp(scores - row_top)]
    all_gather x1 -> x0, blocking collectives: 66.7 us -> none  [on_device(): lax.all_gather(b_up, ('dp', 'ctx'), axis=0, tiled=True)]
    pallas_call x0 -> x1, Pallas kernels: none -> 63.2 us  [attention(): pl.pallas_call(attention_kernel, out_shape=[jax.ShapeDtypeStruct((slots,...]
  transfers between devices with their start and end apart: 13 -> 34, of which waited for: 9 -> 15; matrix products, arithmetic and copies ran while one was open for 21% -> 53% of each run, Pallas kernels for 0% -> 8%
where the time goes in v1:
time: 784 us; the launch traced here: 774 us
  matrix products  277 us (35%)
  waiting for transfers between devices  206 us (26%)
  local copies, waits for them, and re-layouts  90.6 us (12%)
  other arithmetic  67.6 us (9%)
  Pallas kernels  63.2 us (8%)
  starting transfers between devices  54.1 us (7%)
  between operations  15.5 us (2%)
    ppermute x22, waiting for transfers between devices, exchange(): return lax.ppermute(value, axis, [(i, i ^ offset) for i in range(size)])  169 us
    dot_general x10, matrix products, matmul_t(): lax.dot_general(a, b, (((1,), (1,)), ((), ())), preferred_element_type=F32)  111 us
    dot_general x10, matrix products, matmul(): return jnp.dot(a, b, preferred_element_type=F32)  91 us
    dot_general x4, matrix products, outer(): lax.dot_general(a, b, (((0,), (0,)), ((), ())), preferred_element_type=F32)  74.6 us
    pallas_call x1, Pallas kernels, attention(): pl.pallas_call(attention_kernel, out_shape=[jax.ShapeDtypeStruct((slots,...  63.2 us
    all_to_all x1, waiting for transfers between devices, on_device(): small = lax.all_to_all(small, ALL, split_axis=0, concat_axis=0, tiled=True)  33.6 us
    ppermute x22, starting transfers between devices, exchange(): return lax.ppermute(value, axis, [(i, i ^ offset) for i in range(size)])  32.3 us
    unnamed x95, local copies, waits for them, and re-layouts  27.9 us
  transfers between devices with their start and end apart: 34, of which 15 were waited for; matrix products, arithmetic and copies ran while one was open for 53% of the time, Pallas kernels for 8%

profile of v1, /device:TPU:0, one launch (start us, length us, event | category | flops | bytes accessed | tf_op | source)
XLA Modules:
  0.0 774.0 jit_solution(6919043455013646502)
XLA Ops:
  25.3 9.9 %collective-permute-done.5 = bf16[1,64,2048]{2,1,0:T(8,128)(2,1)S(1)} collective-permute-done((bf16[1,64,2048]{2,1,0:T(8,128)(2,1)S(1)}, bf16[1,64,2048]{2,1,0:T(8,128)(2,1)S(1)}, u32[]{:S(2)}, u32[]{:S(2)}) %collective-permute-start.5) | collective-permute-done | bytes 262176 | tf_op jit(solution)/shard_map/ppermute | solution.py:246
  51.9 31.4 %collective-permute-done.1 = bf16[512,2048]{1,0:T(8,128)(2,1)} collective-permute-done((bf16[512,2048]{1,0:T(8,128)(2,1)S(1)}, bf16[512,2048]{1,0:T(8,128)(2,1)}, u32[]{:S(2)}, u32[]{:S(2)}) %collective-permute-start.1) | collective-permute-done | bytes 2097184 | tf_op jit(solution)/shard_map/ppermute | solution.py:246
  147.2 55.6 %collective-permute-done.2 = bf16[256,2048]{1,0:T(8,128)(2,1)} collective-permute-done((bf16[256,2048]{1,0:T(8,128)(2,1)}, bf16[256,2048]{1,0:T(8,128)(2,1)}, u32[]{:S(2)}, u32[]{:S(2)}) %collective-permute-start.2) | collective-permute-done | bytes 1048608 | tf_op jit(solution)/shard_map/ppermute | solution.py:246
  233.9 16.6 %collective-permute-done.9 = bf16[256,2048]{1,0:T(8,128)(2,1)S(1)} collective-permute-done((bf16[256,2048]{1,0:T(8,128)(2,1)S(1)}, bf16[256,2048]{1,0:T(8,128)(2,1)S(1)}, u32[]{:S(2)}, u32[]{:S(2)}) %collective-permute-start.9) | collective-permute-done | bytes 1048608 | tf_op jit(solution)/shard_map/ppermute | solution.py:246
  255.2 28.5 %multiply_convert_fusion = (bf16[2048,2048]{1,0:T(8,128)(2,1)S(1)}, f32[2048,2048]{1,0:T(8,128)}) fusion(f32[2048]{0:T(1024)S(1)} %bitcast.121, bf16[2048,2048]{1,0:T(8,128)(2,1)} %fusion.5, bf16[2048,2048]{1,0:T(8,128)(2,1)} %all-gather.5.cloned.1.call-done), kind=kOutput, calls=%fused_computation.24 | convolution fusion | flops 17221812224 | bytes 41951232 | tf_op jit(solution)/shard_map/dot_general | solution.py:323
  287.0 22.1 %convolution_convert_fusion.1 = bf16[2048,2048]{1,0:T(8,128)(2,1)} fusion(bf16[2048,2048]{1,0:T(8,128)(2,1)S(1)} %get-tuple-element.54, bf16[2048,2048]{1,0:T(8,128)(2,1)} %constant_dynamic-update-slice_fusion.4), kind=kOutput, calls=%fused_computation.28 | convolution fusion | flops 17184063488 | bytes 25165824 | tf_op jit(solution)/shard_map/dot_general | solution.py:331
  309.5 9.9 %convolution_convert_fusion.4.cot_ref = bf16[2048,512]{1,0:T(8,128)(2,1)} fusion(bf16[2048,2048]{1,0:T(8,128)(2,1)} %constant_dynamic-update-slice_fusion.4, bf16[512,2048]{1,0:T(8,128)(2,1)} %all-gather.9.cloned.1.call-done), kind=kOutput, calls=%fused_computation.64 | convolution fusion | flops 4296015872 | bytes 12582912 | tf_op jit(solution)/shard_map/dot_general | solution.py:327
  319.3 19.3 %convolution_add_fusion.qkv_ref = f32[2048,1536]{1,0:T(8,128)} fusion(bf16[2048,2048]{1,0:T(8,128)(2,1)} %fusion.5, bf16[2048,1536]{1,0:T(8,128)(2,1)} %all-gather.7.cloned.1.call-done, f32[1536]{0:T(1024)S(1)} %reshape.366), kind=kOutput, calls=%fused_computation.26 | convolution fusion | flops 12888047616 | bytes 27269120 | tf_op jit(solution)/shard_map/dot_general | solution.py:323
  338.6 63.2 %attention.1 = (bf16[2048,512]{1,0:T(8,128)(2,1)}, bf16[2048,1536]{1,0:T(8,128)(2,1)}) custom-call(s32[16]{0:T(128)S(1)} %copy-done.1, s32[16]{0:T(128)S(1)} %copy-done.3, s32[16]{0:T(128)S(1)} %and_select_fusion.low_ref, f32[2048,1536]{1,0:T(8,128)} %convolution_add_fusion.qkv_ref, bf16[2048,512]{1,0:T(8,128)(2,1)} %convolution_convert_fusion.4.cot_ref, ...), custom_call_target="tpu_custom_call" | custom-call | flops 51539607552 | bytes 23068672 | tf_op jit(solution)/shard_map/attention/pallas_call | solution.py:228
  401.8 34.6 %convert_reduce_fusion.1 = (f32[2048]{0:T(1024)S(1)}, bf16[2048,2048]{1,0:T(8,128)(2,1)}) fusion(f32[2048,2048]{1,0:T(8,128)} %get-tuple-element.108, f32[2048]{0:T(1024)S(1)} %bitcast.122, bf16[2048,2048]{1,0:T(8,128)(2,1)} %constant_dynamic-update-slice_fusion.4, bf16[2048,2048]{1,0:T(8,128)(2,1)} %all-gather.11.cloned.1.call-done), kind=kOutput, calls=%fused_computation.23 | convolution fusion | flops 17272141824 | bytes 41959424 | tf_op jit(solution)/shard_map/dot_general | solution.py:327
  436.4 24.0 %convolution_convert_fusion = bf16[2048,2048]{1,0:T(8,128)(2,1)} fusion(bf16[2048,2048]{1,0:T(8,128)(2,1)} %fusion.5, bf16[2048,2048]{1,0:T(8,128)(2,1)} %get-tuple-element.58), kind=kOutput, calls=%fused_computation.27 | convolution fusion | flops 17184063488 | bytes 25165824 | tf_op jit(solution)/shard_map/dot_general | solution.py:331
  469.3 7.9 %fusion.42 = f32[512,2048]{1,0:T(8,128)S(1)} fusion(bf16[2048,2048]{1,0:T(8,128)(2,1)} %all-gather.5.cloned.1.call-done, bf16[2048,2048]{1,0:T(8,128)(2,1)} %get-tuple-element.58), kind=kOutput, calls=%fused_computation.84 | convolution fusion | flops 4294967296 | bytes 14680064 | tf_op jit(solution)/shard_map/dot_general | solution.py:327
  477.2 8.1 %add_convert_fusion = bf16[512,2048]{1,0:T(8,128)(2,1)} fusion(f32[512,2048]{1,0:T(8,128)S(1)} %fusion.42, bf16[2048,1536]{1,0:T(8,128)(2,1)} %all-gather.7.cloned.1.call-done, bf16[2048,1536]{1,0:T(8,128)(2,1)} %get-tuple-element.57), kind=kOutput, calls=%fused_computation.53 | convolution fusion | flops 3223322624 | bytes 14155776 | tf_op jit(solution)/shard_map/dot_general | solution.py:327
  489.5 19.3 %convolution_convert_fusion.2 = bf16[2048,1536]{1,0:T(8,128)(2,1)} fusion(bf16[2048,2048]{1,0:T(8,128)(2,1)} %fusion.5, bf16[2048,1536]{1,0:T(8,128)(2,1)} %get-tuple-element.57), kind=kOutput, calls=%fused_computation.29 | convolution fusion | flops 12888047616 | bytes 20971520 | tf_op jit(solution)/shard_map/dot_general | solution.py:331
  508.9 8.2 %fusion.46 = f32[512,2048]{1,0:T(8,128)S(1)} fusion(bf16[2048,2048]{1,0:T(8,128)(2,1)} %all-gather.5.cloned.1.call-done, bf16[2048,2048]{1,0:T(8,128)(2,1)} %get-tuple-element.58), kind=kOutput, calls=%fused_computation.88 | convolution fusion | flops 4294967296 | bytes 14680064 | tf_op jit(solution)/shard_map/dot_general | solution.py:327
  525.2 10.6 %fusion.44 = f32[512,2048]{1,0:T(8,128)} fusion(bf16[2048,2048]{1,0:T(8,128)(2,1)} %all-gather.5.cloned.1.call-done, bf16[2048,2048]{1,0:T(8,128)(2,1)} %get-tuple-element.58), kind=kOutput, calls=%fused_computation.86 | convolution fusion | flops 4294967296 | bytes 14680064 | tf_op jit(solution)/shard_map/dot_general | solution.py:327
  543.2 10.6 %fusion.48 = f32[512,2048]{1,0:T(8,128)} fusion(bf16[2048,2048]{1,0:T(8,128)(2,1)} %all-gather.5.cloned.1.call-done, bf16[2048,2048]{1,0:T(8,128)(2,1)} %get-tuple-element.58), kind=kOutput, calls=%fused_computation.90 | convolution fusion | flops 4294967296 | bytes 14680064 | tf_op jit(solution)/shard_map/dot_general | solution.py:327
  556.0 15.5 %collective-permute-done.18 = bf16[512,2048]{1,0:T(8,128)(2,1)S(1)} collective-permute-done((bf16[512,2048]{1,0:T(8,128)(2,1)S(1)}, bf16[512,2048]{1,0:T(8,128)(2,1)S(1)}, u32[]{:S(2)}, u32[]{:S(2)}) %collective-permute-start.18) | collective-permute-done | bytes 2097184 | tf_op jit(solution)/shard_map/ppermute | solution.py:246
  582.5 14.8 %collective-permute-done.19 = bf16[256,2048]{1,0:T(8,128)(2,1)S(1)} collective-permute-done((bf16[256,2048]{1,0:T(8,128)(2,1)S(1)}, bf16[256,2048]{1,0:T(8,128)(2,1)S(1)}, u32[]{:S(2)}, u32[]{:S(2)}) %collective-permute-start.19) | collective-permute-done | bytes 1048608 | tf_op jit(solution)/shard_map/ppermute | solution.py:246
  601.1 9.2 %convolution_convert_fusion.3 = bf16[512,2048]{1,0:T(8,128)(2,1)} fusion(bf16[2048,512]{1,0:T(8,128)(2,1)S(1)} %copy-done.17, bf16[2048,2048]{1,0:T(8,128)(2,1)} %constant_dynamic-update-slice_fusion.4), kind=kOutput, calls=%fused_computation.63 | convolution fusion | flops 4296015872 | bytes 12582912 | tf_op jit(solution)/shard_map/dot_general | solution.py:331
  610.3 8.0 %fusion.50 = f32[512,2048]{1,0:T(8,128)S(1)} fusion(bf16[2048,2048]{1,0:T(8,128)(2,1)} %all-gather.11.cloned.1.call-done, bf16[2048,2048]{1,0:T(8,128)(2,1)} %copy-done.34), kind=kOutput, calls=%fused_computation.92 | convolution fusion | flops 4294967296 | bytes 14680064 | tf_op jit(solution)/shard_map/dot_general | solution.py:323
  637.1 8.2 %all-to-all-start.1 = ((f32[32,1,640]{2,1,0:T(1,128)}), f32[32,1,640]{2,1,0:T(1,128)S(1)}, u32[]{:S(2)}, u32[]{:S(2)}) async-start(f32[32,1,640]{2,1,0:T(1,128)} %all_to_all.26), calls=%async_computation.2 | async-start | bytes 163840 | tf_op jit(solution)/shard_map/all_to_all | solution.py:513
  645.4 33.6 %all-to-all-done.1 = f32[32,1,640]{2,1,0:T(1,128)S(1)} async-done(((f32[32,1,640]{2,1,0:T(1,128)}), f32[32,1,640]{2,1,0:T(1,128)S(1)}, u32[]{:S(2)}, u32[]{:S(2)}) %all-to-all-start.1) | async-done | bytes 81952 | tf_op jit(solution)/shard_map/all_to_all | solution.py:513
  680.8 7.7 fusion.52
  (288 shorter events, 281.7 us)
Async XLA Ops:
  7.2 248.0 %all-gather.5.cloned.1.call-start = ((), (), s32[]{:S(2)}) async-start(), calls=%async_computation.8 | async-start | bytes 9437184 | tf_op jit(solution)/shard_map/all_gather | solution.py:300
  36.3 273.2 %all-gather.9.cloned.1.call-start = ((), (), s32[]{:S(2)}) async-start(), calls=%async_computation.10 | async-start | bytes 2359296 | tf_op jit(solution)/shard_map/all_gather | solution.py:300
  37.0 282.3 %all-gather.7.cloned.1.call-start = ((), (), s32[]{:S(2)}) async-start(), calls=%async_computation.9 | async-start | bytes 7077888 | tf_op jit(solution)/shard_map/all_gather | solution.py:300
  37.1 46.2 %collective-permute-start.1 = (bf16[512,2048]{1,0:T(8,128)(2,1)S(1)}, bf16[512,2048]{1,0:T(8,128)(2,1)}, u32[]{:S(2)}, u32[]{:S(2)}) collective-permute-start(bf16[512,2048]{1,0:T(8,128)(2,1)S(1)} %bitcast.91), channel_id=1, source_target_pairs={{0,2},{1,3},{2,0},{3,1},{4,6},{5,7},{6,4},{7,5},{8,10},{9,11},{10,... | collective-permute-start | bytes 6291464 | tf_op jit(solution)/shard_map/ppermute | solution.py:246
  38.6 46.1 %collective-permute-start = (bf16[512,2048]{1,0:T(8,128)(2,1)S(1)}, bf16[512,2048]{1,0:T(8,128)(2,1)}, u32[]{:S(2)}, u32[]{:S(2)}) collective-permute-start(bf16[512,2048]{1,0:T(8,128)(2,1)S(1)} %bitcast.92), channel_id=1, source_target_pairs={{0,1},{1,0},{2,3},{3,2},{4,5},{5,4},{6,7},{7,6},{8,9},{9,8},{10,11... | collective-permute-start | bytes 6291464 | tf_op jit(solution)/shard_map/ppermute | solution.py:246
  101.8 29.8 %all-to-all-start = ((bf16[32,2,352]{2,1,0:T(2,128)(2,1)}), bf16[32,2,352]{2,1,0:T(2,128)(2,1)S(1)}, u32[]{:S(2)}, u32[]{:S(2)}) async-start(bf16[32,2,352]{2,1,0:T(2,128)(2,1)} %reshape.433), calls=%async_computation | async-start | bytes 98304 | tf_op jit(solution)/shard_map/all_to_all | solution.py:296
  106.9 294.9 %all-gather.11.cloned.1.call-start = ((), (), s32[]{:S(2)}) async-start(), calls=%async_computation.12 | async-start | bytes 9437184 | tf_op jit(solution)/shard_map/all_gather | solution.py:300
  132.2 95.5 %collective-permute-start.8 = (bf16[512,2048]{1,0:T(8,128)(2,1)}, bf16[512,2048]{1,0:T(8,128)(2,1)}, u32[]{:S(2)}, u32[]{:S(2)}) collective-permute-start(bf16[512,2048]{1,0:T(8,128)(2,1)} %bitcast.93), channel_id=1, source_target_pairs={{0,2},{1,3},{2,0},{3,1},{4,6},{5,7},{6,4},{7,5},{8,10},{9,11},{10,... | collective-permute-start | bytes 6291464 | tf_op jit(solution)/shard_map/ppermute | solution.py:246
  134.0 89.5 %collective-permute-start.7 = (bf16[512,2048]{1,0:T(8,128)(2,1)}, bf16[512,2048]{1,0:T(8,128)(2,1)}, u32[]{:S(2)}, u32[]{:S(2)}) collective-permute-start(bf16[512,2048]{1,0:T(8,128)(2,1)} %bitcast.94), channel_id=1, source_target_pairs={{0,1},{1,0},{2,3},{3,2},{4,5},{5,4},{6,7},{7,6},{8,9},{9,8},{10,11... | collective-permute-start | bytes 6291464 | tf_op jit(solution)/shard_map/ppermute | solution.py:246
  138.3 64.5 %collective-permute-start.2 = (bf16[256,2048]{1,0:T(8,128)(2,1)}, bf16[256,2048]{1,0:T(8,128)(2,1)}, u32[]{:S(2)}, u32[]{:S(2)}) collective-permute-start(bf16[256,2048]{1,0:T(8,128)(2,1)} %get-tuple-element.89), channel_id=1, source_target_pairs={{0,2},{1,3},{2,0},{3,1},{4,6},{5,7},{6,4},{7,5},{8,10},{9,11},{10,... | collective-permute-start | bytes 3145736 | tf_op jit(solution)/shard_map/ppermute | solution.py:246
  141.2 66.2 %collective-permute-start.3 = (bf16[256,2048]{1,0:T(8,128)(2,1)S(1)}, bf16[256,2048]{1,0:T(8,128)(2,1)}, u32[]{:S(2)}, u32[]{:S(2)}) collective-permute-start(bf16[256,2048]{1,0:T(8,128)(2,1)S(1)} %get-tuple-element.87), channel_id=1, source_target_pairs={{0,1},{1,0},{2,3},{3,2},{4,5},{5,4},{6,7},{7,6},{8,9},{9,8},{10,11... | collective-permute-start | bytes 3145736 | tf_op jit(solution)/shard_map/ppermute | solution.py:246
  141.5 345.2 %reduce-scatter.5.cloned.1.call-start = ((), (), s32[]{:S(2)}) async-start(), calls=%async_computation.11 | async-start | bytes 9437184 | tf_op jit(solution)/shard_map/reduce_scatter | solution.py:304
  226.0 24.5 %collective-permute-start.9 = (bf16[256,2048]{1,0:T(8,128)(2,1)S(1)}, bf16[256,2048]{1,0:T(8,128)(2,1)S(1)}, u32[]{:S(2)}, u32[]{:S(2)}) collective-permute-start(bf16[256,2048]{1,0:T(8,128)(2,1)S(1)} %get-tuple-element.85), channel_id=1, source_target_pairs={{0,2},{1,3},{2,0},{3,1},{4,6},{5,7},{6,4},{7,5},{8,10},{9,11},{10,... | collective-permute-start | bytes 3145736 | tf_op jit(solution)/shard_map/ppermute | solution.py:246
  309.2 383.6 %reduce-scatter.11.cloned.1.call-start = ((), (), s32[]{:S(2)}) async-start(), calls=%async_computation.15 | async-start | bytes 9437184 | tf_op jit(solution)/shard_map/reduce_scatter | solution.py:304
  460.4 280.5 %reduce-scatter.7.cloned.1.call-start = ((), (), s32[]{:S(2)}) async-start(), calls=%async_computation.13 | async-start | bytes 7077888 | tf_op jit(solution)/shard_map/reduce_scatter | solution.py:304
  485.3 68.6 %collective-permute-start.20 = (bf16[512,2048]{1,0:T(8,128)(2,1)}, bf16[512,2048]{1,0:T(8,128)(2,1)}, u32[]{:S(2)}, u32[]{:S(2)}) collective-permute-start(bf16[512,2048]{1,0:T(8,128)(2,1)} %add_convert_fusion), channel_id=1, source_target_pairs={{0,1},{1,0},{2,3},{3,2},{4,5},{5,4},{6,7},{7,6},{8,9},{9,8},{10,11... | collective-permute-start | bytes 6291464 | tf_op jit(solution)/shard_map/ppermute | solution.py:246
  524.0 47.5 %collective-permute-start.18 = (bf16[512,2048]{1,0:T(8,128)(2,1)S(1)}, bf16[512,2048]{1,0:T(8,128)(2,1)S(1)}, u32[]{:S(2)}, u32[]{:S(2)}) collective-permute-start(bf16[512,2048]{1,0:T(8,128)(2,1)S(1)} %add_convert_fusion.1), channel_id=1, source_target_pairs={{0,2},{1,3},{2,0},{3,1},{4,6},{5,7},{6,4},{7,5},{8,10},{9,11},{10,... | collective-permute-start | bytes 6291464 | tf_op jit(solution)/shard_map/ppermute | solution.py:246
  620.9 75.9 %collective-permute-start.16 = (bf16[512,2048]{1,0:T(8,128)(2,1)}, bf16[512,2048]{1,0:T(8,128)(2,1)}, u32[]{:S(2)}, u32[]{:S(2)}) collective-permute-start(bf16[512,2048]{1,0:T(8,128)(2,1)} %add_convert_fusion.2), channel_id=1, source_target_pairs={{0,1},{1,0},{2,3},{3,2},{4,5},{5,4},{6,7},{7,6},{8,9},{9,8},{10,11... | collective-permute-start | bytes 6291464 | tf_op jit(solution)/shard_map/ppermute | solution.py:246
  632.2 66.9 %collective-permute-start.14 = (bf16[512,2048]{1,0:T(8,128)(2,1)}, bf16[512,2048]{1,0:T(8,128)(2,1)}, u32[]{:S(2)}, u32[]{:S(2)}) collective-permute-start(bf16[512,2048]{1,0:T(8,128)(2,1)} %add_convert_fusion.3), channel_id=1, source_target_pairs={{0,2},{1,3},{2,0},{3,1},{4,6},{5,7},{6,4},{7,5},{8,10},{9,11},{10,... | collective-permute-start | bytes 6291464 | tf_op jit(solution)/shard_map/ppermute | solution.py:246
  637.1 41.8 %all-to-all-start.1 = ((f32[32,1,640]{2,1,0:T(1,128)}), f32[32,1,640]{2,1,0:T(1,128)S(1)}, u32[]{:S(2)}, u32[]{:S(2)}) async-start(f32[32,1,640]{2,1,0:T(1,128)} %all_to_all.26), calls=%async_computation.2 | async-start | bytes 163840 | tf_op jit(solution)/shard_map/all_to_all | solution.py:513
  645.3 105.7 %reduce-scatter.9.cloned.1.call-start = ((), (), s32[]{:S(2)}) async-start(), calls=%async_computation.14 | async-start | bytes 2359296 | tf_op jit(solution)/shard_map/reduce_scatter | solution.py:304
  692.8 27.3 %all-to-all-start.3 = ((bf16[4,64,2048]{2,1,0:T(8,128)(2,1)}), bf16[4,64,2048]{2,1,0:T(8,128)(2,1)S(1)}, u32[]{:S(2)}, u32[]{:S(2)}) async-start(bf16[4,64,2048]{2,1,0:T(8,128)(2,1)} %bitcast.110), calls=%async_computation.7 | async-start | bytes 2097152 | tf_op jit(solution)/shard_map/all_to_all | solution.py:308
  706.1 27.2 %collective-permute-start.15 = (bf16[256,2048]{1,0:T(8,128)(2,1)}, bf16[256,2048]{1,0:T(8,128)(2,1)}, u32[]{:S(2)}, u32[]{:S(2)}) collective-permute-start(bf16[256,2048]{1,0:T(8,128)(2,1)} %get-tuple-element.79), channel_id=1, source_target_pairs={{0,1},{1,0},{2,3},{3,2},{4,5},{5,4},{6,7},{7,6},{8,9},{9,8},{10,11... | collective-permute-start | bytes 3145736 | tf_op jit(solution)/shard_map/ppermute | solution.py:246
  708.1 25.2 %collective-permute-start.17 = (bf16[256,2048]{1,0:T(8,128)(2,1)}, bf16[256,2048]{1,0:T(8,128)(2,1)}, u32[]{:S(2)}, u32[]{:S(2)}) collective-permute-start(bf16[256,2048]{1,0:T(8,128)(2,1)} %get-tuple-element.80), channel_id=1, source_target_pairs={{0,2},{1,3},{2,0},{3,1},{4,6},{5,7},{6,4},{7,5},{8,10},{9,11},{10,... | collective-permute-start | bytes 3145736 | tf_op jit(solution)/shard_map/ppermute | solution.py:246
  (49 other events, 1166.9 us)
Sparse Core Ops, SparseCore 0:
  36.4 84.2 all-gather.4
  122.3 27.5 all-gather.8
  152.1 64.2 all-gather.6
  217.8 80.6 all-gather.10
  309.3 90.2 reduce-scatter.4
  460.5 97.7 reduce-scatter.10
  560.6 68.1 reduce-scatter.6
  680.9 41.7 reduce-scatter.8

commit v2 on v1

--- a/solution.py
+++ b/solution.py
@@ -234,12 +234,107 @@
         grid_spec=grid_spec,
         compiler_params=pltpu.CompilerParams(vmem_limit_bytes=50 * 1024 * 1024),
         cost_estimate=pl.CostEstimate(
-            flops=12 * tiles * 2 * BLK * BLK * PAIR * 4,
-            bytes_accessed=qkv.size * 6 + cotangent.size * 4,
-            transcendentals=tiles * 2 * BLK * BLK,
+            flops=tiles * 2 * BLK * BLK * PAIR,
+            bytes_accessed=qkv.size,
+            transcendentals=0,
         ),
         name="attention",
     )(block_place, slot_block, low, qkv, cotangent, cosine, sine, first_place)
+
+
+def pick_rows(found, order, rows):
+    arrays, places = [], []
+    for key in order:
+        array, start = found[key]
+        held = [i for i, known in enumerate(arrays) if known is array]
+        if not held:
+            arrays.append(array)
+            held = [len(arrays) - 1]
+        places.append((held[0], start // rows))
+    return arrays, places
+
+
+def join_blocks(found, order, rows, gain=None, shift=None):
+    arrays, places = pick_rows(found, order, rows)
+    width = arrays[0].shape[1]
+    norm = gain is not None
+
+    def kernel(*refs):
+        out = refs[-1]
+        step = pl.program_id(0)
+        for number, (which, block) in enumerate(places):
+
+            @pl.when(step == number)
+            def _(ref=refs[which], block=block):
+                x = ref[block * rows : (block + 1) * rows, :]
+                if norm:
+                    x, _ = standardise(x.astype(F32))
+                    x = (x * refs[-3][...] + refs[-2][...]).astype(BF)
+                out[...] = x
+
+    once = pl.Buffered(1)
+    in_specs = [pl.BlockSpec(a.shape, lambda i: (0, 0), pipeline_mode=once) for a in arrays]
+    extra = []
+    if norm:
+        extra = [gain[None, :], shift[None, :]]
+        in_specs += [pl.BlockSpec((1, width), lambda i: (0, 0), pipeline_mode=once)] * 2
+    size = len(order) * rows * width
+    return pl.pallas_call(
+        kernel,
+        grid=(len(order),),
+        in_specs=in_specs,
+        out_specs=pl.BlockSpec((rows, width), lambda i: (i, 0)),
+        out_shape=jax.ShapeDtypeStruct((len(order) * rows, width), BF),
+        compiler_params=pltpu.CompilerParams(vmem_limit_bytes=40 * 1024 * 1024),
+        cost_estimate=pl.CostEstimate(
+            flops=size * (10 if norm else 1), bytes_accessed=4 * size, transcendentals=0
+        ),
+        name="norm_rows" if norm else "join_rows",
+    )(*arrays, *extra)
+
+
+def deal_columns(matrix, chunks):
+    rows = matrix.shape[0]
+    width = sum(stop - start for start, stop in chunks[0])
+
+    def kernel(x_ref, o_ref):
+        x = x_ref[...].astype(F32)
+        for target, parts in enumerate(chunks):
+            part = jnp.concatenate([x[:, start:stop] for start, stop in parts], axis=1)
+            o_ref[target] = part.astype(BF)
+
+    return pl.pallas_call(
+        kernel,
+        out_shape=jax.ShapeDtypeStruct((len(chunks), rows, width), BF),
+        cost_estimate=pl.CostEstimate(
+            flops=matrix.size, bytes_accessed=4 * matrix.size, transcendentals=0
+        ),
+        name="deal_columns",
+    )(matrix)
+
+
+def collect_columns(blocks, chunks):
+    order = []
+    for source, parts in enumerate(chunks):
+        place = 0
+        for start, stop in parts:
+            order.append((start, source, place, place + stop - start))
+            place += stop - start
+    order.sort()
+    width = blocks.shape[0] * blocks.shape[2]
+
+    def kernel(x_ref, o_ref):
+        x = [x_ref[source].astype(F32) for source in range(len(chunks))]
+        o_ref[...] = jnp.concatenate([x[i][:, low:high] for _, i, low, high in order], axis=1)
+
+    return pl.pallas_call(
+        kernel,
+        out_shape=jax.ShapeDtypeStruct((blocks.shape[1], width), F32),
+        cost_estimate=pl.CostEstimate(
+            flops=blocks.size, bytes_accessed=6 * blocks.size, transcendentals=0
+        ),
+        name="collect_columns",
+    )(blocks)
 
 
 def exchange(value, axis, size, offset):
@@ -256,39 +351,62 @@
     return [(j, half) for j in range(size) for half in range(2)]
 
 
-def gather_steps(value, size, first=None):
+def split_halves(value, j, found):
     half = value.shape[0] // 2
-    found = {(0, 0): value[:half], (0, 1): value[half:]}
+    found[j, 0], found[j, 1] = (value, 0), (value, half)
+
+
+def gather_two(first, second, size, wait):
+    send = functools.partial(exchange, axis="ctx", size=size)
+    half = first.shape[0] // 2
+    left, right = {}, {}
+    split_halves(first, 0, left)
+    split_halves(second, 0, right)
     if size != 4:
         for j in range(1, size):
-            other = exchange(value, "ctx", size, j)
-            found[j, 0], found[j, 1] = other[:half], other[half:]
-        return found, found[1, 0]
-    one = exchange(value, "ctx", size, 1)
-    two = exchange(value, "ctx", size, 2)
-    found[1, 0], found[1, 1] = one[:half], one[half:]
-    found[2, 0], found[2, 1] = two[:half], two[half:]
-    found[3, 0] = exchange(one[:half], "ctx", size, 2)
-    found[3, 1] = exchange(two[half:], "ctx", size, 1)
-    return found, lax.optimization_barrier((one, two))[0]
-
-
-def sum_blocks(piece, size):
+            split_halves(send(first, offset=j), j, left)
+        for j in range(1, size):
+            split_halves(send(second, offset=j), j, right)
+        return left, right, first
+    one, two = send(first, offset=1), send(first, offset=2)
+    split_halves(one, 1, left)
+    split_halves(two, 2, left)
+    one, two, second = lax.optimization_barrier((one, two, second) + wait)[:3]
+    near = send(jnp.concatenate([two[half:], second], axis=0), offset=1)
+    far = send(jnp.concatenate([one[:half], second], axis=0), offset=2)
+    left[3, 0], left[3, 1] = (far, 0), (near, 0)
+    right[1, 0], right[1, 1] = (near, half), (near, 2 * half)
+    right[2, 0], right[2, 1] = (far, half), (far, 2 * half)
+    right[3, 0] = (send(near[half : 2 * half], offset=2), 0)
+    right[3, 1] = (send(far[2 * half :], offset=1), 0)
+    return left, right, one
+
+
+def sum_cut(size):
+    return 4 if size == 4 else 2
+
+
+def sum_blocks(away, size):
+    away = away.astype(BF)
     if size != 4:
-        total = piece(0, 2)
-        for j in range(1, size):
-            total = total + exchange(piece(2 * j, 2 * j + 2).astype(BF), "ctx", size, j).astype(F32)
-        return total
-    far = exchange(piece(4, 6).astype(BF), "ctx", size, 2).astype(F32)
-    near = exchange(piece(6, 8).astype(BF), "ctx", size, 1).astype(F32)
-    middle = piece(2, 4)
-    own = piece(0, 2)
-    half = own.shape[0] // 2
-    top = exchange((middle[:half] + far[half:]).astype(BF), "ctx", size, 1)
-    low = exchange((middle[half:] + near[half:]).astype(BF), "ctx", size, 2)
-    top = own[:half] + far[:half] + top.astype(F32)
-    low = own[half:] + near[:half] + low.astype(F32)
-    return jnp.concatenate([top, low], axis=0)
+        blocks = away.reshape(size - 1, -1, away.shape[1])
+        arrived = tuple(exchange(blocks[j - 1], "ctx", size, j) for j in range(1, size))
+        return arrived, lambda own: sum([x.astype(F32) for x in arrived], own)
+    half = away.shape[0] // 4
+    arrived = (
+        exchange(away[: 2 * half], "ctx", size, 2),
+        exchange(away[2 * half :], "ctx", size, 1),
+    )
+
+    def finish(own):
+        far, near = arrived[0].astype(F32), arrived[1].astype(F32)
+        top = exchange((own[2 * half : 3 * half] + far[half:]).astype(BF), "ctx", size, 1)
+        low = exchange((own[3 * half :] + near[half:]).astype(BF), "ctx", size, 2)
+        top = own[:half] + far[:half] + top.astype(F32)
+        low = own[half : 2 * half] + near[:half] + low.astype(F32)
+        return jnp.concatenate([top, low], axis=0)
+
+    return arrived, finish
 
 
 def gather_small(value, devices):
@@ -306,17 +424,6 @@
 
 def swap_ctx(value):
     return lax.all_to_all(value, "ctx", split_axis=0, concat_axis=0, tiled=True)
-
-
-def swap_ctx_steps(value, size):
-    c = lax.axis_index("ctx")
-    blocks = value.reshape((size, -1) + value.shape[1:])
-    result = blocks
-    for j in range(1, size):
-        block = lax.dynamic_index_in_dim(blocks, c ^ j, 0)
-        block = exchange(block, "ctx", size, j)
-        result = lax.dynamic_update_slice_in_dim(result, block, c ^ j, 0)
-    return result.reshape(value.shape)
 
 
 def matmul(a, b):
@@ -377,21 +484,27 @@
     hidden_own = hidden_in.reshape(own_slots, width)
     grad_own = grad_out.reshape(own_slots, width)
 
-    found, arrived = gather_steps(hidden_own, C)
-    hidden_all = jnp.concatenate([found[key] for key in half_blocks(C)], axis=0)
-    found, _ = gather_steps(after(grad_own, arrived), C)
-    grad_all = jnp.concatenate([found[key] for key in half_blocks(C)], axis=0)
 
     sizes = [ln_gain.shape[0], ln_bias.shape[0], b_qkv.shape[0], b_out.shape[0]]
     sizes += [b_up.shape[0], b_down.shape[0]]
     cuts = [sum(sizes[:i]) for i in range(1, len(sizes))]
     small = jnp.concatenate([ln_gain, ln_bias, b_qkv, b_out, b_up, b_down])
-    pieces = jnp.split(gather_small(small, N * C), cuts, axis=1)
+    small = gather_small(small, N * C)
+    hidden_parts, grad_parts, arrived = gather_two(hidden_own, grad_own, C, (small,))
+    pieces = jnp.split(small, cuts, axis=1)
     gain, shift, qkv_bias, out_bias, up_bias, down_bias = [p.reshape(-1).astype(F32) for p in pieces]
-    qkv_send = w_qkv.reshape(row_block, 3, groups, 2, C, HEAD).transpose(4, 0, 2, 1, 3, 5)
-    qkv_send = qkv_send.reshape(C * row_block, 3 * own_heads * HEAD)
-    up_send = w_up.reshape(row_block, N, C, ff_block).transpose(2, 0, 1, 3)
-    up_send = up_send.reshape(C * row_block, own_ff)
+    qkv_chunks = [
+        [
+            (part * width + (i * C + t) * HEAD, part * width + (i * C + t + 1) * HEAD)
+            for pair in range(groups)
+            for part in range(3)
+            for i in (2 * pair, 2 * pair + 1)
+        ]
+        for t in range(C)
+    ]
+    up_chunks = [
+        [((i * C + t) * ff_block, (i * C + t + 1) * ff_block) for i in range(N)] for t in range(C)
+    ]
     aligned = row_block == HEAD
     if aligned:
         w_out_own = gather_dp(w_out)
@@ -400,8 +513,9 @@
         everything = everything.reshape(own_heads, C, HEAD, width)
         w_out_own = lax.dynamic_index_in_dim(everything, c, 1, keepdims=False)
         w_out_own = w_out_own.reshape(own_heads * HEAD, width)
-    up_rows = swap_ctx_steps(up_send, C)
-    qkv_rows = swap_ctx_steps(after(qkv_send, arrived), C)
+    up_rows = swap_ctx(deal_columns(w_up, up_chunks)).reshape(C * row_block, -1)
+    qkv_send = deal_columns(w_qkv, qkv_chunks)
+    qkv_rows = swap_ctx(after(qkv_send, arrived)).reshape(C * row_block, -1)
     w_up_own = gather_dp(up_rows)
     w_qkv_own = gather_dp(qkv_rows)
 
@@ -430,18 +544,20 @@
 
     own_bias = lax.dynamic_index_in_dim(qkv_bias.reshape(3, groups, 2, C, HEAD), c, 3, keepdims=False)
     own_bias = own_bias.transpose(1, 0, 2, 3).reshape(-1)
-    hidden_all, cosine, sine, first_place, block_place, slot_block, own_bias = (
-        lax.optimization_barrier(
-            (hidden_all, cosine, sine, first_place, block_place, slot_block, own_bias)
-        )
-    )
-    xhat_all, _ = standardise(hidden_all.astype(F32))
-    normed = (xhat_all * gain + shift).astype(BF)
+    gain, cosine, sine, first_place, block_place, slot_block, own_bias = lax.optimization_barrier(
+        (gain, cosine, sine, first_place, block_place, slot_block, own_bias)
+    )
+    step = own_slots // 2
+    normed = join_blocks(hidden_parts, half_blocks(C), step, gain, shift)
     w_down_own = gather_dp(after(w_down, arrived))
     own_up_bias = lax.dynamic_index_in_dim(up_bias.reshape(N, C, ff_block), c, 1, keepdims=False)
     up = matmul(normed, w_up_own) + own_up_bias.reshape(-1)
     value, slope = gelu_pair(up)
-    active = value.astype(BF)
+    active, slope = lax.optimization_barrier((value.astype(BF), slope))
+    if C == 4:
+        for key in ((3, 0), (3, 1)):
+            grad_parts[key] = (after(grad_parts[key][0], active), grad_parts[key][1])
+    grad_all = join_blocks(grad_parts, half_blocks(C), step)
     down_part = outer(active, grad_all).astype(BF)
     down_grad = scatter_dp(down_part).astype(F32)
 
@@ -451,13 +567,16 @@
         qkv, d_attended, cosine, sine, first_place, block_place, slot_block
     )
 
-    def column_grad(part, shape):
-        return swap_ctx(scatter_dp(part)).reshape((C, row_block) + shape)
-
-    qkv_part = outer(after(normed, down_grad), d_qkv).astype(BF)
-    qkv_grad = column_grad(qkv_part, (groups, 3, 2, HEAD))
-    qkv_grad = qkv_grad.transpose(1, 3, 2, 4, 0, 5).reshape(w_qkv.shape).astype(F32)
-    out_part = outer(after(attended, qkv_part), grad_all)
+    def column_grad(part, chunks):
+        own = scatter_dp(part)
+        return collect_columns(swap_ctx(own.reshape(C, row_block, -1)), chunks)
+
+    cut = sum_cut(C) * step
+
+    def out_rows(rows, attended):
+        return matmul(attended[rows], w_out_own) + matmul(active[rows], w_down_own)
+
+    out_part = outer(attended, after(grad_all, w_down_own))
     if aligned:
         out_part = out_part.astype(BF)
         out_grad = scatter_dp(out_part).astype(F32)
@@ -470,28 +589,29 @@
             spread.reshape(heads * HEAD, width), ALL, scatter_dimension=0, tiled=True
         )
 
-    step = own_slots // 2
-    attended_then, active_then = lax.optimization_barrier((attended, active, out_part))[:2]
-
-    def out_piece(start, stop):
-        rows = slice(start * step, stop * step)
-        return matmul(attended_then[rows], w_out_own) + matmul(active_then[rows], w_down_own)
-
-    output = hidden_own.astype(F32) + sum_blocks(out_piece, C) + (out_bias + down_bias)
+    qkv_part = outer(after(normed, down_grad, out_part), d_qkv).astype(BF)
+    qkv_grad = column_grad(qkv_part, qkv_chunks)
+
+    out_away = out_rows(slice(cut, None), after(attended, qkv_part)).astype(BF)
+    out_arrived, finish = sum_blocks(out_away, C)
+    grad_then = after(grad_all, out_away)
+    d_up = (matmul_t(grad_then, w_down_own) * slope).astype(BF)
+    up_part = outer(after(normed, *out_arrived), d_up).astype(BF)
+    up_grad = column_grad(up_part, up_chunks)
+    out_near = out_rows(slice(0, cut), after(attended, up_part))
+    out_sum = finish(out_near)
+    output = hidden_own.astype(F32) + out_sum + (out_bias + down_bias)
     output = output.astype(BF).reshape(hidden_in.shape)
 
-    d_up = (matmul_t(after(grad_all, attended), w_down_own) * slope).astype(BF)
-    up_part = outer(normed, d_up).astype(BF)
-    up_grad = column_grad(up_part, (N, ff_block))
-    up_grad = up_grad.transpose(1, 2, 0, 3).reshape(w_up.shape).astype(F32)
-
     d_qkv_then, d_up_then = lax.optimization_barrier((d_qkv, d_up, up_part))[:2]
 
-    def normed_piece(start, stop):
-        rows = slice(start * step, stop * step)
+    def normed_rows(rows):
         return matmul_t(d_qkv_then[rows], w_qkv_own) + matmul_t(d_up_then[rows], w_up_own)
 
-    d_normed = sum_blocks(normed_piece, C)
+    d_away = normed_rows(slice(cut, None)).astype(BF)
+    d_near = normed_rows(slice(0, cut))
+    d_normed = sum_blocks(d_away, C)[1](after(d_near, qkv_grad))
+    d_normed = after(d_normed, up_grad)
     xhat, scale = standardise(hidden_own.astype(F32))
     e = d_normed * gain
     d_hidden = e - jnp.mean(e, axis=-1, keepdims=True)
@@ -510,6 +630,7 @@
     qkv_bias_grad = jnp.where(mine[None, None, None, :, None], qkv_bias_grad, 0.0)
     small = [gain_grad, shift_grad, qkv_bias_grad, bias_grad, up_bias_grad]
     small = jnp.concatenate([s.reshape(devices, -1) for s in small], axis=1)
+    small = after(small, grad_in)
     small = lax.all_to_all(small, ALL, split_axis=0, concat_axis=0, tiled=True)
     small = jnp.split(jnp.sum(small, axis=0), cuts[:4])
 

time: 784 us -> 738 us (0.941)
  local copies, waits for them, and re-layouts: 90.6 us -> 38.8 us
  Pallas kernels: 63.2 us -> 104 us
  blocking collectives: 0 us -> 36.3 us
  waiting for transfers between devices: 206 us -> 174 us
  matrix products: 277 us -> 248 us
  starting transfers between devices: 54.1 us -> 38 us
    ppermute x22 -> x14, waiting for transfers between devices: 169 us -> 96.6 us  [exchange(): return lax.ppermute(value, axis, [(i, i ^ offset) for i in range(size)])]
    all_to_all x0 -> x2, blocking collectives: none -> 36.3 us  [swap_ctx(): return lax.all_to_all(value, 'ctx', split_axis=0, concat_axis=0, tiled=True)]
    all_to_all x1, waiting for transfers between devices: 0.01 us -> 36.2 us  [gather_small(): return lax.all_to_all(copies, ALL, split_axis=0, concat_axis=0, tiled=True)]
    pallas_call x0 -> x6, Pallas kernels: none -> 33 us  [the longest x2 23 us: join_blocks(): pl.pallas_call(kernel, grid=(len(order),), in_specs=in_specs, out_specs=p...]
    all_to_all x1, waiting for transfers between devices: 33.6 us -> 3.4 us  [on_device(): small = lax.all_to_all(small, ALL, split_axis=0, concat_axis=0, tiled=True)]
    dot_general x10 -> x6, matrix products: 111 us -> 89.1 us  [matmul_t(): lax.dot_general(a, b, (((1,), (1,)), ((), ())), preferred_element_type=F32)]
    all_to_all x2, waiting for transfers between devices: 2.79 us -> 24.8 us  [swap_ctx(): return lax.all_to_all(value, 'ctx', split_axis=0, concat_axis=0, tiled=True)]
    unnamed x95 -> x83, local copies, waits for them, and re-layouts: 27.9 us -> 7.91 us
  transfers between devices with their start and end apart: 34 -> 26, of which waited for: 15 -> 11; matrix products, arithmetic and copies ran while one was open for 53% -> 44% of each run, Pallas kernels for 8% -> 14%
where the time goes in v2:
time: 738 us; the launch traced here: 729 us
  matrix products  248 us (34%)
  waiting for transfers between devices  174 us (24%)
  Pallas kernels  104 us (14%)
  other arithmetic  73.6 us (10%)
  local copies, waits for them, and re-layouts  38.8 us (5%)
  starting transfers between devices  38 us (5%)
  blocking collectives  36.3 us (5%)
  between operations  15.3 us (2%)
    ppermute x14, waiting for transfers between devices, exchange(): return lax.ppermute(value, axis, [(i, i ^ offset) for i in range(size)])  96.6 us
    dot_general x6, matrix products, matmul_t(): lax.dot_general(a, b, (((1,), (1,)), ((), ())), preferred_element_type=F32)  89.1 us
    dot_general x6, matrix products, matmul(): return jnp.dot(a, b, preferred_element_type=F32)  84.4 us
    dot_general x4, matrix products, outer(): lax.dot_general(a, b, (((0,), (0,)), ((), ())), preferred_element_type=F32)  74.5 us
    pallas_call x1, Pallas kernels, attention(): pl.pallas_call(attention_kernel, out_shape=[jax.ShapeDtypeStruct((slots,...  71.4 us
    all_to_all x2, blocking collectives, swap_ctx(): return lax.all_to_all(value, 'ctx', split_axis=0, concat_axis=0, tiled=True)  36.3 us
    all_to_all x1, waiting for transfers between devices, gather_small(): return lax.all_to_all(copies, ALL, split_axis=0, concat_axis=0, tiled=True)  36.2 us
    all_to_all x2, waiting for transfers between devices, swap_ctx(): return lax.all_to_all(value, 'ctx', split_axis=0, concat_axis=0, tiled=True)  24.8 us
  transfers between devices with their start and end apart: 26, of which 11 were waited for; matrix products, arithmetic and copies ran while one was open for 44% of the time, Pallas kernels for 14%

profile of v2, /device:TPU:0, one launch (start us, length us, event | category | flops | bytes accessed | tf_op | source)
XLA Modules:
  0.0 728.7 jit_solution(13134923347229668204)
XLA Ops:
  9.7 20.1 %all_to_all.38 = bf16[4,64,2048]{2,1,0:T(8,128)(2,1)} all-to-all(bf16[4,64,2048]{2,1,0:T(8,128)(2,1)} %deal_columns.2), channel_id=1, replica_groups=mesh['dp'=8,'ctx'=4] {'ctx'}, dimensions={0} | all-to-all | bytes 2097152 | tf_op jit(solution)/shard_map/all_to_all | solution.py:426
  42.5 36.2 %all-to-all-done = bf16[32,2,352]{2,1,0:T(2,128)(2,1)S(1)} async-done(((bf16[32,2,352]{2,1,0:T(2,128)(2,1)}), bf16[32,2,352]{2,1,0:T(2,128)(2,1)S(1)}, u32[]{:S(2)}, u32[]{:S(2)}) %all-to-all-start) | async-done | bytes 45088 | tf_op jit(solution)/shard_map/all_to_all | solution.py:414
  78.9 16.2 %all_to_all.39 = bf16[4,64,1536]{2,1,0:T(8,128)(2,1)} all-to-all(bf16[4,64,1536]{2,1,0:T(8,128)(2,1)} %deal_columns.3), channel_id=1, replica_groups=mesh['dp'=8,'ctx'=4] {'ctx'}, dimensions={0} | all-to-all | bytes 1572864 | tf_op jit(solution)/shard_map/all_to_all | solution.py:426
  130.0 42.8 %collective-permute-done.2.refs_3_.refs_2_ = bf16[768,2048]{1,0:T(8,128)(2,1)} collective-permute-done((bf16[768,2048]{1,0:T(8,128)(2,1)}, bf16[768,2048]{1,0:T(8,128)(2,1)}, u32[]{:S(2)}, u32[]{:S(2)}) %collective-permute-start.2) | collective-permute-done | bytes 3145760 | tf_op jit(solution)/shard_map/ppermute | solution.py:341
  179.3 12.0 %norm_rows.1 = bf16[2048,2048]{1,0:T(8,128)(2,1)} custom-call(bf16[512,2048]{1,0:T(8,128)(2,1)S(1)} %bitcast.64, bf16[512,2048]{1,0:T(8,128)(2,1)} %collective-permute-done.refs_1_, bf16[512,2048]{1,0:T(8,128)(2,1)} %collective-permute-done.1.refs_2_, bf16[768,2048]{1,0:T(8,128)(2,1)} %collective-permute-done.2.refs_3_.refs_2_, ...), custom_call_target="tpu_custom_call" | custom-call | flops 41943040 | bytes 16777216 | tf_op jit(solution)/shard_map/norm_rows/pallas_call | solution.py:282
  191.2 34.2 %fusion.7 = (f32[2048,2048]{1,0:T(8,128)}, bf16[2048,2048]{1,0:T(8,128)(2,1)S(1)}) fusion(f32[2048]{0:T(1024)S(1)} %bitcast.83, bf16[2048,2048]{1,0:T(8,128)(2,1)} %norm_rows.1, bf16[2048,2048]{1,0:T(8,128)(2,1)} %all-gather.5.cloned.1.call-done), kind=kOutput, calls=%fused_computation.12 | convolution fusion | flops 17263755264 | bytes 41951232 | tf_op jit(solution)/shard_map/dot_general | solution.py:430
  225.5 11.1 %join_rows.1 = bf16[2048,2048]{1,0:T(8,128)(2,1)} custom-call(bf16[512,2048]{1,0:T(8,128)(2,1)S(1)} %bitcast.66, bf16[768,2048]{1,0:T(8,128)(2,1)} %collective-permute-done.3.refs_4_.refs_1_, bf16[768,2048]{1,0:T(8,128)(2,1)} %collective-permute-done.2.refs_3_.refs_2_, bf16[256,2048]{1,0:T(8,128)(2,1)} %collective-permute-done.4.refs_3_, ...), custom_call_target="tpu_custom_call" | custom-call | flops 4194304 | bytes 16777216 | tf_op jit(solution)/shard_map/join_rows/pallas_call | solution.py:282
  236.6 21.3 %convolution_convert_fusion.1 = bf16[2048,2048]{1,0:T(8,128)(2,1)} fusion(bf16[2048,2048]{1,0:T(8,128)(2,1)S(1)} %get-tuple-element.53, bf16[2048,2048]{1,0:T(8,128)(2,1)} %join_rows.1), kind=kOutput, calls=%fused_computation.21 | convolution fusion | flops 17184063488 | bytes 25165824 | tf_op jit(solution)/shard_map/dot_general | solution.py:438
  268.4 19.3 %convolution_add_fusion.qkv_ref = f32[2048,1536]{1,0:T(8,128)} fusion(bf16[2048,2048]{1,0:T(8,128)(2,1)} %norm_rows.1, bf16[2048,1536]{1,0:T(8,128)(2,1)} %all-gather.7.cloned.1.call-done, f32[1536]{0:T(1024)S(1)} %reshape.229), kind=kOutput, calls=%fused_computation.17 | convolution fusion | flops 12888047616 | bytes 27269120 | tf_op jit(solution)/shard_map/dot_general | solution.py:430
  287.7 71.4 %attention.1 = (bf16[2048,512]{1,0:T(8,128)(2,1)}, bf16[2048,1536]{1,0:T(8,128)(2,1)}) custom-call(s32[16]{0:T(128)S(1)} %copy-done.6, s32[16]{0:T(128)S(1)} %copy-done.8, s32[16]{0:T(128)S(1)} %and_select_fusion.low_ref, f32[2048,1536]{1,0:T(8,128)} %convolution_add_fusion.qkv_ref, bf16[2048,512]{1,0:T(8,128)(2,1)} %convolution_convert_fusion.4.cot_ref, ...), custom_call_target="tpu_custom_call" | custom-call | flops 1073741824 | bytes 3145728 | tf_op jit(solution)/shard_map/attention/pallas_call | solution.py:228
  369.2 11.7 %reduce-scatter.5.cloned.1.call-done = bf16[256,2048]{1,0:T(8,128)(2,1)} async-done(((bf16[2048,2048]{1,0:T(8,128)(2,1)}), bf16[256,2048]{1,0:T(8,128)(2,1)}) %reduce-scatter.5.cloned.1.call-update) | async-done | bytes 1048592 | tf_op jit(solution)/shard_map/reduce_scatter | solution.py:422
  383.6 19.2 %convolution_convert_fusion.2 = bf16[2048,1536]{1,0:T(8,128)(2,1)} fusion(bf16[2048,2048]{1,0:T(8,128)(2,1)} %norm_rows.1, bf16[2048,1536]{1,0:T(8,128)(2,1)} %get-tuple-element.72), kind=kOutput, calls=%fused_computation.22 | convolution fusion | flops 12888047616 | bytes 20971520 | tf_op jit(solution)/shard_map/dot_general | solution.py:438
  403.6 13.5 %fusion.27 = f32[1024,2048]{1,0:T(8,128)S(1)} fusion(bf16[2048,2048]{1,0:T(8,128)(2,1)} %all-gather.11.cloned.1.call-done, bf16[2048,2048]{1,0:T(8,128)(2,1)} %copy-done.35), kind=kOutput, calls=%fused_computation.48 | convolution fusion | flops 8589934592 | bytes 20971520 | tf_op jit(solution)/shard_map/dot_general | solution.py:430
  424.6 25.7 %convert_reduce_fusion = (f32[2048]{0:T(1024)S(1)}, bf16[2048,2048]{1,0:T(8,128)(2,1)}) fusion(f32[2048,2048]{1,0:T(8,128)} %get-tuple-element.70, bf16[2048,2048]{1,0:T(8,128)(2,1)} %join_rows.1, bf16[2048,2048]{1,0:T(8,128)(2,1)} %all-gather.11.cloned.1.call-done), kind=kOutput, calls=%fused_computation.13 | convolution fusion | flops 17196644352 | bytes 41951232 | tf_op jit(solution)/shard_map/dot_general | solution.py:434
  450.3 16.8 %collective-permute-done.6 = bf16[512,2048]{1,0:T(8,128)(2,1)} collective-permute-done((bf16[512,2048]{1,0:T(8,128)(2,1)}, bf16[512,2048]{1,0:T(8,128)(2,1)}, u32[]{:S(2)}, u32[]{:S(2)}) %collective-permute-start.6) | collective-permute-done | bytes 2097184 | tf_op jit(solution)/shard_map/ppermute | solution.py:341
  468.3 24.0 %convolution_convert_fusion = bf16[2048,2048]{1,0:T(8,128)(2,1)} fusion(bf16[2048,2048]{1,0:T(8,128)(2,1)} %norm_rows.1, bf16[2048,2048]{1,0:T(8,128)(2,1)} %get-tuple-element.73), kind=kOutput, calls=%fused_computation.20 | convolution fusion | flops 17184063488 | bytes 25165824 | tf_op jit(solution)/shard_map/dot_general | solution.py:438
  494.0 12.5 %fusion.25 = f32[1024,2048]{1,0:T(8,128)S(1)} fusion(bf16[2048,2048]{1,0:T(8,128)(2,1)} %all-gather.11.cloned.1.call-done, bf16[2048,2048]{1,0:T(8,128)(2,1)} %copy-done.35), kind=kOutput, calls=%fused_computation.46 | convolution fusion | flops 8589934592 | bytes 20971520 | tf_op jit(solution)/shard_map/dot_general | solution.py:430
  506.6 14.5 %fusion.21 = f32[1024,2048]{1,0:T(8,128)} fusion(bf16[2048,2048]{1,0:T(8,128)(2,1)} %all-gather.5.cloned.1.call-done, bf16[2048,2048]{1,0:T(8,128)(2,1)} %get-tuple-element.73), kind=kOutput, calls=%fused_computation.42 | convolution fusion | flops 8589934592 | bytes 20971520 | tf_op jit(solution)/shard_map/dot_general | solution.py:434
  521.1 11.3 %add_convert_fusion = bf16[1024,2048]{1,0:T(8,128)(2,1)S(1)} fusion(f32[1024,2048]{1,0:T(8,128)} %fusion.21, bf16[2048,1536]{1,0:T(8,128)(2,1)} %all-gather.7.cloned.1.call-done, bf16[2048,1536]{1,0:T(8,128)(2,1)} %get-tuple-element.72), kind=kOutput, calls=%fused_computation.18 | convolution fusion | flops 6446645248 | bytes 22020096 | tf_op jit(solution)/shard_map/dot_general | solution.py:434
  546.7 14.6 %fusion.23 = f32[1024,2048]{1,0:T(8,128)} fusion(bf16[2048,2048]{1,0:T(8,128)(2,1)} %all-gather.5.cloned.1.call-done, bf16[2048,2048]{1,0:T(8,128)(2,1)} %get-tuple-element.73), kind=kOutput, calls=%fused_computation.44 | convolution fusion | flops 8589934592 | bytes 20971520 | tf_op jit(solution)/shard_map/dot_general | solution.py:434
  565.0 13.0 %convolution_add_fusion.2 = f32[1024,2048]{1,0:T(8,128)} fusion(f32[1024,2048]{1,0:T(8,128)} %fusion.23, bf16[2048,1536]{1,0:T(8,128)(2,1)} %all-gather.7.cloned.1.call-done, bf16[2048,1536]{1,0:T(8,128)(2,1)} %get-tuple-element.72), kind=kOutput, calls=%fused_computation.51 | convolution fusion | flops 6444548096 | bytes 26214400 | tf_op jit(solution)/shard_map/dot_general | solution.py:434
  585.2 24.8 %all-to-all-done.3.x_ref = bf16[4,64,1536]{2,1,0:T(8,128)(2,1)S(1)} async-done(((bf16[4,64,1536]{2,1,0:T(8,128)(2,1)}), bf16[4,64,1536]{2,1,0:T(8,128)(2,1)S(1)}, u32[]{:S(2)}, u32[]{:S(2)}) %all-to-all-start.3) | async-done | bytes 786464 | tf_op jit(solution)/shard_map/all_to_all | solution.py:426
  645.0 16.6 %collective-permute-done.9 = bf16[256,2048]{1,0:T(8,128)(2,1)} collective-permute-done((bf16[256,2048]{1,0:T(8,128)(2,1)S(1)}, bf16[256,2048]{1,0:T(8,128)(2,1)}, u32[]{:S(2)}, u32[]{:S(2)}) %collective-permute-start.9) | collective-permute-done | bytes 1048608 | tf_op jit(solution)/shard_map/ppermute | solution.py:341
  669.6 13.7 %collective-permute-done.13 = bf16[256,2048]{1,0:T(8,128)(2,1)} collective-permute-done((bf16[256,2048]{1,0:T(8,128)(2,1)}, bf16[256,2048]{1,0:T(8,128)(2,1)}, u32[]{:S(2)}, u32[]{:S(2)}) %collective-permute-start.13) | collective-permute-done | bytes 1048608 | tf_op jit(solution)/shard_map/ppermute | solution.py:341
  (238 shorter events, 196.8 us)
Async XLA Ops:
  7.3 184.0 %all-gather.5.cloned.1.call-start = ((), (), s32[]{:S(2)}) async-start(), calls=%async_computation.10 | async-start | bytes 9437184 | tf_op jit(solution)/shard_map/all_gather | solution.py:418
  29.9 228.6 %all-gather.9.cloned.1.call-start = ((), (), s32[]{:S(2)}) async-start(), calls=%async_computation.12 | async-start | bytes 2359296 | tf_op jit(solution)/shard_map/all_gather | solution.py:418
  30.6 48.2 %collective-permute-start = (bf16[512,2048]{1,0:T(8,128)(2,1)S(1)}, bf16[512,2048]{1,0:T(8,128)(2,1)}, u32[]{:S(2)}, u32[]{:S(2)}) collective-permute-start(bf16[512,2048]{1,0:T(8,128)(2,1)S(1)} %bitcast.62), channel_id=1, source_target_pairs={{0,1},{1,0},{2,3},{3,2},{4,5},{5,4},{6,7},{7,6},{8,9},{9,8},{10,11... | collective-permute-start | bytes 6291464 | tf_op jit(solution)/shard_map/ppermute | solution.py:341
  31.6 47.3 %collective-permute-start.1 = (bf16[512,2048]{1,0:T(8,128)(2,1)S(1)}, bf16[512,2048]{1,0:T(8,128)(2,1)}, u32[]{:S(2)}, u32[]{:S(2)}) collective-permute-start(bf16[512,2048]{1,0:T(8,128)(2,1)S(1)} %bitcast.63), channel_id=1, source_target_pairs={{0,2},{1,3},{2,0},{3,1},{4,6},{5,7},{6,4},{7,5},{8,10},{9,11},{10,... | collective-permute-start | bytes 6291464 | tf_op jit(solution)/shard_map/ppermute | solution.py:341
  34.2 44.6 %all-to-all-start = ((bf16[32,2,352]{2,1,0:T(2,128)(2,1)}), bf16[32,2,352]{2,1,0:T(2,128)(2,1)S(1)}, u32[]{:S(2)}, u32[]{:S(2)}) async-start(bf16[32,2,352]{2,1,0:T(2,128)(2,1)} %reshape.293), calls=%async_computation | async-start | bytes 98304 | tf_op jit(solution)/shard_map/all_to_all | solution.py:414
  40.1 228.2 %all-gather.7.cloned.1.call-start = ((), (), s32[]{:S(2)}) async-start(), calls=%async_computation.11 | async-start | bytes 7077888 | tf_op jit(solution)/shard_map/all_gather | solution.py:418
  95.1 264.0 %all-gather.11.cloned.1.call-start = ((), (), s32[]{:S(2)}) async-start(), calls=%async_computation.14 | async-start | bytes 9437184 | tf_op jit(solution)/shard_map/all_gather | solution.py:418
  95.7 285.1 %reduce-scatter.5.cloned.1.call-start = ((), (), s32[]{:S(2)}) async-start(), calls=%async_computation.13 | async-start | bytes 9437184 | tf_op jit(solution)/shard_map/reduce_scatter | solution.py:422
  103.5 69.3 %collective-permute-start.2 = (bf16[768,2048]{1,0:T(8,128)(2,1)}, bf16[768,2048]{1,0:T(8,128)(2,1)}, u32[]{:S(2)}, u32[]{:S(2)}) collective-permute-start(bf16[768,2048]{1,0:T(8,128)(2,1)} %get-tuple-element.101), channel_id=1, source_target_pairs={{0,2},{1,3},{2,0},{3,1},{4,6},{5,7},{6,4},{7,5},{8,10},{9,11},{10,... | collective-permute-start | bytes 9437192 | tf_op jit(solution)/shard_map/ppermute | solution.py:341
  104.4 72.0 %collective-permute-start.3 = (bf16[768,2048]{1,0:T(8,128)(2,1)}, bf16[768,2048]{1,0:T(8,128)(2,1)}, u32[]{:S(2)}, u32[]{:S(2)}) collective-permute-start(bf16[768,2048]{1,0:T(8,128)(2,1)} %get-tuple-element.100), channel_id=1, source_target_pairs={{0,1},{1,0},{2,3},{3,2},{4,5},{5,4},{6,7},{7,6},{8,9},{9,8},{10,11... | collective-permute-start | bytes 9437192 | tf_op jit(solution)/shard_map/ppermute | solution.py:341
  175.1 50.4 %collective-permute-start.5 = (bf16[256,2048]{1,0:T(8,128)(2,1)}, bf16[256,2048]{1,0:T(8,128)(2,1)}, u32[]{:S(2)}, u32[]{:S(2)}) collective-permute-start(bf16[256,2048]{1,0:T(8,128)(2,1)} %slice.143), channel_id=1, source_target_pairs={{0,1},{1,0},{2,3},{3,2},{4,5},{5,4},{6,7},{7,6},{8,9},{9,8},{10,11... | collective-permute-start | bytes 3145736 | tf_op jit(solution)/shard_map/ppermute | solution.py:341
  178.7 46.8 %collective-permute-start.4 = (bf16[256,2048]{1,0:T(8,128)(2,1)}, bf16[256,2048]{1,0:T(8,128)(2,1)}, u32[]{:S(2)}, u32[]{:S(2)}) collective-permute-start(bf16[256,2048]{1,0:T(8,128)(2,1)} %slice.142), channel_id=1, source_target_pairs={{0,2},{1,3},{2,0},{3,1},{4,6},{5,7},{6,4},{7,5},{8,10},{9,11},{10,... | collective-permute-start | bytes 3145736 | tf_op jit(solution)/shard_map/ppermute | solution.py:341
  257.9 303.4 %reduce-scatter.7.cloned.1.call-start = ((), (), s32[]{:S(2)}) async-start(), calls=%async_computation.15 | async-start | bytes 7077888 | tf_op jit(solution)/shard_map/reduce_scatter | solution.py:422
  402.8 240.3 %reduce-scatter.11.cloned.1.call-start = ((), (), s32[]{:S(2)}) async-start(), calls=%async_computation.17 | async-start | bytes 2359296 | tf_op jit(solution)/shard_map/reduce_scatter | solution.py:422
  403.6 262.5 %reduce-scatter.9.cloned.1.call-start = ((), (), s32[]{:S(2)}) async-start(), calls=%async_computation.16 | async-start | bytes 9437184 | tf_op jit(solution)/shard_map/reduce_scatter | solution.py:422
  422.1 45.1 %collective-permute-start.6 = (bf16[512,2048]{1,0:T(8,128)(2,1)}, bf16[512,2048]{1,0:T(8,128)(2,1)}, u32[]{:S(2)}, u32[]{:S(2)}) collective-permute-start(bf16[512,2048]{1,0:T(8,128)(2,1)} %get-tuple-element.96), channel_id=1, source_target_pairs={{0,2},{1,3},{2,0},{3,1},{4,6},{5,7},{6,4},{7,5},{8,10},{9,11},{10,... | collective-permute-start | bytes 6291464 | tf_op jit(solution)/shard_map/ppermute | solution.py:341
  423.2 45.2 %collective-permute-start.7 = (bf16[512,2048]{1,0:T(8,128)(2,1)}, bf16[512,2048]{1,0:T(8,128)(2,1)}, u32[]{:S(2)}, u32[]{:S(2)}) collective-permute-start(bf16[512,2048]{1,0:T(8,128)(2,1)} %get-tuple-element.97), channel_id=1, source_target_pairs={{0,1},{1,0},{2,3},{3,2},{4,5},{5,4},{6,7},{7,6},{8,9},{9,8},{10,11... | collective-permute-start | bytes 6291464 | tf_op jit(solution)/shard_map/ppermute | solution.py:341
  534.7 46.4 %collective-permute-start.10 = (bf16[512,2048]{1,0:T(8,128)(2,1)}, bf16[512,2048]{1,0:T(8,128)(2,1)}, u32[]{:S(2)}, u32[]{:S(2)}) collective-permute-start(bf16[512,2048]{1,0:T(8,128)(2,1)} %get-tuple-element.94), channel_id=1, source_target_pairs={{0,2},{1,3},{2,0},{3,1},{4,6},{5,7},{6,4},{7,5},{8,10},{9,11},{10,... | collective-permute-start | bytes 6291464 | tf_op jit(solution)/shard_map/ppermute | solution.py:341
  535.3 97.8 %collective-permute-start.12 = (bf16[512,2048]{1,0:T(8,128)(2,1)}, bf16[512,2048]{1,0:T(8,128)(2,1)}, u32[]{:S(2)}, u32[]{:S(2)}) collective-permute-start(bf16[512,2048]{1,0:T(8,128)(2,1)} %get-tuple-element.95), channel_id=1, source_target_pairs={{0,1},{1,0},{2,3},{3,2},{4,5},{5,4},{6,7},{7,6},{8,9},{9,8},{10,11... | collective-permute-start | bytes 6291464 | tf_op jit(solution)/shard_map/ppermute | solution.py:341
  545.9 79.5 %collective-permute-start.8 = (bf16[256,2048]{1,0:T(8,128)(2,1)}, bf16[256,2048]{1,0:T(8,128)(2,1)}, u32[]{:S(2)}, u32[]{:S(2)}) collective-permute-start(bf16[256,2048]{1,0:T(8,128)(2,1)} %fusion.39), channel_id=1, source_target_pairs={{0,1},{1,0},{2,3},{3,2},{4,5},{5,4},{6,7},{7,6},{8,9},{9,8},{10,11... | collective-permute-start | bytes 3145736 | tf_op jit(solution)/shard_map/ppermute | solution.py:341
  561.3 48.7 %all-to-all-start.3 = ((bf16[4,64,1536]{2,1,0:T(8,128)(2,1)}), bf16[4,64,1536]{2,1,0:T(8,128)(2,1)S(1)}, u32[]{:S(2)}, u32[]{:S(2)}) async-start(bf16[4,64,1536]{2,1,0:T(8,128)(2,1)} %bitcast.73), calls=%async_computation.5 | async-start | bytes 1572864 | tf_op jit(solution)/shard_map/all_to_all | solution.py:426
  632.6 29.0 %collective-permute-start.9 = (bf16[256,2048]{1,0:T(8,128)(2,1)S(1)}, bf16[256,2048]{1,0:T(8,128)(2,1)}, u32[]{:S(2)}, u32[]{:S(2)}) collective-permute-start(bf16[256,2048]{1,0:T(8,128)(2,1)S(1)} %get-tuple-element.93), channel_id=1, source_target_pairs={{0,2},{1,3},{2,0},{3,1},{4,6},{5,7},{6,4},{7,5},{8,10},{9,11},{10,... | collective-permute-start | bytes 3145736 | tf_op jit(solution)/shard_map/ppermute | solution.py:341
  641.8 41.5 %collective-permute-start.13 = (bf16[256,2048]{1,0:T(8,128)(2,1)}, bf16[256,2048]{1,0:T(8,128)(2,1)}, u32[]{:S(2)}, u32[]{:S(2)}) collective-permute-start(bf16[256,2048]{1,0:T(8,128)(2,1)} %get-tuple-element.91), channel_id=1, source_target_pairs={{0,2},{1,3},{2,0},{3,1},{4,6},{5,7},{6,4},{7,5},{8,10},{9,11},{10,... | collective-permute-start | bytes 3145736 | tf_op jit(solution)/shard_map/ppermute | solution.py:341
  666.0 22.8 %all-to-all-start.4 = ((bf16[4,64,2048]{2,1,0:T(8,128)(2,1)}), bf16[4,64,2048]{2,1,0:T(8,128)(2,1)S(1)}, u32[]{:S(2)}, u32[]{:S(2)}) async-start(bf16[4,64,2048]{2,1,0:T(8,128)(2,1)} %bitcast.72), calls=%async_computation.7 | async-start | bytes 2097152 | tf_op jit(solution)/shard_map/all_to_all | solution.py:426
  (40 other events, 862.8 us)
Sparse Core Ops, SparseCore 0:
  30.0 82.9 all-gather.4
  114.6 27.7 all-gather.8
  144.0 64.2 all-gather.6
  209.7 80.6 all-gather.10
  292.6 88.1 reduce-scatter.4
  402.9 68.1 reduce-scatter.6
  473.4 34.1 reduce-scatter.10
  509.9 88.2 reduce-scatter.8

commit v3 on v2

--- a/solution.py
+++ b/solution.py
@@ -19,6 +19,7 @@
 LONGEST = 1024
 PAIRS = 2
 LOOSE = 2
+FRACTION = 5.0
 SCALE = HEAD**-0.5
 ALL = ("dp", "ctx")
 BF = jnp.bfloat16
@@ -254,10 +255,9 @@
     return arrays, places
 
 
-def join_blocks(found, order, rows, gain=None, shift=None):
+def norm_blocks(found, order, rows, gain, shift):
     arrays, places = pick_rows(found, order, rows)
     width = arrays[0].shape[1]
-    norm = gain is not None
 
     def kernel(*refs):
         out = refs[-1]
@@ -267,17 +267,12 @@
             @pl.when(step == number)
             def _(ref=refs[which], block=block):
                 x = ref[block * rows : (block + 1) * rows, :]
-                if norm:
-                    x, _ = standardise(x.astype(F32))
-                    x = (x * refs[-3][...] + refs[-2][...]).astype(BF)
-                out[...] = x
+                x, _ = standardise(x.astype(F32))
+                out[...] = (x * refs[-3][...] + refs[-2][...]).astype(BF)
 
     once = pl.Buffered(1)
     in_specs = [pl.BlockSpec(a.shape, lambda i: (0, 0), pipeline_mode=once) for a in arrays]
-    extra = []
-    if norm:
-        extra = [gain[None, :], shift[None, :]]
-        in_specs += [pl.BlockSpec((1, width), lambda i: (0, 0), pipeline_mode=once)] * 2
+    in_specs += [pl.BlockSpec((1, width), lambda i: (0, 0), pipeline_mode=once)] * 2
     size = len(order) * rows * width
     return pl.pallas_call(
         kernel,
@@ -286,31 +281,58 @@
         out_specs=pl.BlockSpec((rows, width), lambda i: (i, 0)),
         out_shape=jax.ShapeDtypeStruct((len(order) * rows, width), BF),
         compiler_params=pltpu.CompilerParams(vmem_limit_bytes=40 * 1024 * 1024),
-        cost_estimate=pl.CostEstimate(
-            flops=size * (10 if norm else 1), bytes_accessed=4 * size, transcendentals=0
-        ),
-        name="norm_rows" if norm else "join_rows",
-    )(*arrays, *extra)
-
-
-def deal_columns(matrix, chunks):
-    rows = matrix.shape[0]
-    width = sum(stop - start for start, stop in chunks[0])
-
-    def kernel(x_ref, o_ref):
-        x = x_ref[...].astype(F32)
-        for target, parts in enumerate(chunks):
-            part = jnp.concatenate([x[:, start:stop] for start, stop in parts], axis=1)
-            o_ref[target] = part.astype(BF)
-
+        cost_estimate=pl.CostEstimate(flops=size * 10, bytes_accessed=4 * size, transcendentals=0),
+        name="norm_rows",
+    )(*arrays, gain[None, :], shift[None, :])
+
+
+def join_blocks(found, order, rows):
+    arrays, places = pick_rows(found, order, rows)
+    width = arrays[0].shape[1]
+
+    def kernel(*refs):
+        out, arrived = refs[-2], refs[-1]
+        copies = []
+        for number, (which, block) in enumerate(places):
+            source = refs[which].at[pl.ds(block * rows, rows), :]
+            target = out.at[pl.ds(number * rows, rows), :]
+            copies.append(pltpu.make_async_copy(source, target, arrived.at[number]))
+        for copy in copies:
+            copy.start()
+        for copy in copies:
+            copy.wait()
+
+    size = len(order) * rows * width
     return pl.pallas_call(
         kernel,
-        out_shape=jax.ShapeDtypeStruct((len(chunks), rows, width), BF),
-        cost_estimate=pl.CostEstimate(
-            flops=matrix.size, bytes_accessed=4 * matrix.size, transcendentals=0
-        ),
+        in_specs=[pl.BlockSpec(memory_space=pl.ANY)] * len(arrays),
+        out_specs=pl.BlockSpec(memory_space=pl.ANY),
+        out_shape=jax.ShapeDtypeStruct((len(order) * rows, width), BF),
+        scratch_shapes=[pltpu.SemaphoreType.DMA((len(order),))],
+        cost_estimate=pl.CostEstimate(flops=size, bytes_accessed=4 * size, transcendentals=0),
+        name="join_rows",
+    )(*arrays)
+
+
+def deal_columns(matrices, chunks):
+    rows = matrices[0].shape[0]
+    width = sum(stop - start for parts in chunks for start, stop in parts[0])
+    size = rows * width * len(chunks[0])
+
+    def kernel(*refs):
+        values = [ref[...].astype(F32) for ref in refs[:-1]]
+        for target in range(len(chunks[0])):
+            part = [
+                x[:, start:stop] for x, parts in zip(values, chunks) for start, stop in parts[target]
+            ]
+            refs[-1][target] = jnp.concatenate(part, axis=1).astype(BF)
+
+    return pl.pallas_call(
+        kernel,
+        out_shape=jax.ShapeDtypeStruct((len(chunks[0]), rows, width), BF),
+        cost_estimate=pl.CostEstimate(flops=size, bytes_accessed=4 * size, transcendentals=0),
         name="deal_columns",
-    )(matrix)
+    )(*matrices)
 
 
 def collect_columns(blocks, chunks):
@@ -391,7 +413,7 @@
     if size != 4:
         blocks = away.reshape(size - 1, -1, away.shape[1])
         arrived = tuple(exchange(blocks[j - 1], "ctx", size, j) for j in range(1, size))
-        return arrived, lambda own: sum([x.astype(F32) for x in arrived], own)
+        return arrived, lambda own: (sum([x.astype(F32) for x in arrived], own), arrived)
     half = away.shape[0] // 4
     arrived = (
         exchange(away[: 2 * half], "ctx", size, 2),
@@ -402,9 +424,10 @@
         far, near = arrived[0].astype(F32), arrived[1].astype(F32)
         top = exchange((own[2 * half : 3 * half] + far[half:]).astype(BF), "ctx", size, 1)
         low = exchange((own[3 * half :] + near[half:]).astype(BF), "ctx", size, 2)
+        last = (top, low)
         top = own[:half] + far[:half] + top.astype(F32)
         low = own[half : 2 * half] + near[:half] + low.astype(F32)
-        return jnp.concatenate([top, low], axis=0)
+        return jnp.concatenate([top, low], axis=0), last
 
     return arrived, finish
 
@@ -436,6 +459,74 @@
 
 def outer(a, b):
     return lax.dot_general(a, b, (((0,), (0,)), ((), ())), preferred_element_type=F32)
+
+
+CONTRACT = {"nn": ((1,), (0,)), "nt": ((1,), (1,)), "tn": ((0,), (0,))}
+
+
+def tile_of(size):
+    return next(t for t in (1024, 768, 512, 384, 256, 128, size) if size % t == 0)
+
+
+def product(kind, pairs, outs=(BF,), finish=None, extras=(), row_range=None):
+    a, b = pairs[0]
+    rows = a.shape[1] if kind == "tn" else a.shape[0]
+    columns = b.shape[0] if kind == "nt" else b.shape[1]
+    low, high = row_range or (0, rows)
+    tall, wide = tile_of(high - low), tile_of(columns)
+    skip = low // tall
+    in_specs, operands = [], []
+    for a, b in pairs:
+        if kind == "tn":
+            in_specs.append(pl.BlockSpec((a.shape[0], tall), lambda j, i: (0, i + skip)))
+        else:
+            in_specs.append(pl.BlockSpec((tall, a.shape[1]), lambda j, i: (i + skip, 0)))
+        if kind == "nt":
+            in_specs.append(pl.BlockSpec((wide, b.shape[1]), lambda j, i: (j, 0)))
+        else:
+            in_specs.append(pl.BlockSpec((b.shape[0], wide), lambda j, i: (0, j)))
+        operands += [a, b]
+    for extra in extras:
+        if extra.shape[0] == 1:
+            in_specs.append(pl.BlockSpec((1, wide), lambda j, i: (0, j)))
+        else:
+            in_specs.append(pl.BlockSpec((tall, wide), lambda j, i: (i + skip, j)))
+        operands.append(extra)
+    count, chunk = len(pairs), min(256, wide)
+    depth = sum(a.shape[0] if kind == "tn" else a.shape[1] for a, _ in pairs)
+
+    def kernel(*refs):
+        for start in range(0, wide, chunk):
+            part = slice(start, start + chunk)
+            total = None
+            for p in range(count):
+                right = refs[2 * p + 1]
+                right = right[part, :] if kind == "nt" else right[:, part]
+                term = lax.dot_general(
+                    refs[2 * p][...], right, (CONTRACT[kind], ((), ())), preferred_element_type=F32
+                )
+                total = term if total is None else total + term
+            more = [refs[2 * count + n][:, part] for n in range(len(extras))]
+            results = finish(total, *more) if finish else (total,)
+            for ref, value in zip(refs[-len(outs) :], results):
+                ref[:, part] = value.astype(ref.dtype)
+
+    shape = (high - low, columns)
+    result = pl.pallas_call(
+        kernel,
+        grid=(columns // wide, (high - low) // tall),
+        in_specs=in_specs,
+        out_specs=[pl.BlockSpec((tall, wide), lambda j, i: (i, j))] * len(outs),
+        out_shape=[jax.ShapeDtypeStruct(shape, dtype) for dtype in outs],
+        compiler_params=pltpu.CompilerParams(vmem_limit_bytes=56 * 1024 * 1024),
+        cost_estimate=pl.CostEstimate(
+            flops=int(2 * FRACTION * shape[0] * shape[1] * depth),
+            bytes_accessed=shape[0] * shape[1],
+            transcendentals=0,
+        ),
+        name="product_" + kind,
+    )(*operands)
+    return result if len(outs) > 1 else result[0]
 
 
 def standardise(hidden):
@@ -447,10 +538,11 @@
 
 
 def gelu_pair(x):
-    root = math.sqrt(2.0 / math.pi)
-    t = jnp.tanh(root * (x + 0.044715 * (x * x * x)))
-    value = 0.5 * x * (1.0 + t)
-    slope = 0.5 * (1.0 + t) + 0.5 * x * (1.0 - t * t) * (root * (1.0 + 3 * 0.044715 * x * x))
+    root, cubic = math.sqrt(2.0 / math.pi), 0.044715
+    square = x * x
+    gate = 0.5 + 0.5 * jnp.tanh(x * (root + (root * cubic) * square))
+    value = x * gate
+    slope = gate + value * (1.0 - gate) * (2.0 * root + (6.0 * root * cubic) * square)
     return value, slope
 
 
@@ -513,9 +605,9 @@
         everything = everything.reshape(own_heads, C, HEAD, width)
         w_out_own = lax.dynamic_index_in_dim(everything, c, 1, keepdims=False)
         w_out_own = w_out_own.reshape(own_heads * HEAD, width)
-    up_rows = swap_ctx(deal_columns(w_up, up_chunks)).reshape(C * row_block, -1)
-    qkv_send = deal_columns(w_qkv, qkv_chunks)
-    qkv_rows = swap_ctx(after(qkv_send, arrived)).reshape(C * row_block, -1)
+    both_rows = swap_ctx(deal_columns((w_up, w_qkv), (up_chunks, qkv_chunks)))
+    both_rows = both_rows.reshape(C * row_block, -1)
+    up_rows, qkv_rows = both_rows[:, :own_ff], both_rows[:, own_ff:]
     w_up_own = gather_dp(up_rows)
     w_qkv_own = gather_dp(qkv_rows)
 
@@ -548,10 +640,10 @@
         (gain, cosine, sine, first_place, block_place, slot_block, own_bias)
     )
     step = own_slots // 2
-    normed = join_blocks(hidden_parts, half_blocks(C), step, gain, shift)
+    normed = norm_blocks(hidden_parts, half_blocks(C), step, gain, shift)
     w_down_own = gather_dp(after(w_down, arrived))
     own_up_bias = lax.dynamic_index_in_dim(up_bias.reshape(N, C, ff_block), c, 1, keepdims=False)
-    up = matmul(normed, w_up_own) + own_up_bias.reshape(-1)
+    up = matmul(after(normed, w_out_own), w_up_own) + own_up_bias.reshape(-1)
     value, slope = gelu_pair(up)
     active, slope = lax.optimization_barrier((value.astype(BF), slope))
     if C == 4:
@@ -594,24 +686,24 @@
 
     out_away = out_rows(slice(cut, None), after(attended, qkv_part)).astype(BF)
     out_arrived, finish = sum_blocks(out_away, C)
-    grad_then = after(grad_all, out_away)
+    out_near = out_rows(slice(0, cut), after(attended, out_away))
+    grad_then = after(grad_all, out_near)
     d_up = (matmul_t(grad_then, w_down_own) * slope).astype(BF)
-    up_part = outer(after(normed, *out_arrived), d_up).astype(BF)
+    up_part = outer(normed, d_up).astype(BF)
     up_grad = column_grad(up_part, up_chunks)
-    out_near = out_rows(slice(0, cut), after(attended, up_part))
-    out_sum = finish(out_near)
+    out_sum, out_last = finish(after(out_near, d_up))
     output = hidden_own.astype(F32) + out_sum + (out_bias + down_bias)
     output = output.astype(BF).reshape(hidden_in.shape)
 
-    d_qkv_then, d_up_then = lax.optimization_barrier((d_qkv, d_up, up_part))[:2]
-
-    def normed_rows(rows):
-        return matmul_t(d_qkv_then[rows], w_qkv_own) + matmul_t(d_up_then[rows], w_up_own)
-
-    d_away = normed_rows(slice(cut, None)).astype(BF)
-    d_near = normed_rows(slice(0, cut))
-    d_normed = sum_blocks(d_away, C)[1](after(d_near, qkv_grad))
-    d_normed = after(d_normed, up_grad)
+    d_qkv_then, d_up_then = lax.optimization_barrier((d_qkv, d_up, up_part, qkv_grad) + out_last)[:2]
+
+    def normed_rows(row_range, dtype):
+        pairs = [(d_qkv_then, w_qkv_own), (d_up_then, w_up_own)]
+        return product("nt", pairs, (dtype,), row_range=row_range)
+
+    d_away = normed_rows((cut, slots), BF)
+    d_near = normed_rows((0, cut), F32)
+    d_normed, _ = sum_blocks(d_away, C)[1](d_near)
     xhat, scale = standardise(hidden_own.astype(F32))
     e = d_normed * gain
     d_hidden = e - jnp.mean(e, axis=-1, keepdims=True)

time: 738 us -> 982 us (1.33)
  Pallas kernels: 104 us -> 396 us
  matrix products: 248 us -> 202 us
  waiting for transfers between devices: 174 us -> 129 us
  blocking collectives: 36.3 us -> 72.2 us
    pallas_call x4 -> x5, Pallas kernels: 27.8 us -> 316 us  [the longest x1 255 us: join_blocks(): pl.pallas_call(kernel, in_specs=[pl.BlockSpec(memory_space=pl.ANY)] * len...]
    dot_general x6 -> x2, matrix products: 89.1 us -> 36.3 us  [matmul_t(): lax.dot_general(a, b, (((1,), (1,)), ((), ())), preferred_element_type=F32)]
    all_to_all x0 -> x1, blocking collectives: none -> 44.3 us  [gather_small(): return lax.all_to_all(copies, ALL, split_axis=0, concat_axis=0, tiled=True)]
    all_to_all x1 -> x0, waiting for transfers between devices: 36.2 us -> none  [gather_small(): return lax.all_to_all(copies, ALL, split_axis=0, concat_axis=0, tiled=True)]
    all_to_all x1, starting transfers between devices: 10 us -> 22 us  [on_device(): small = lax.all_to_all(small, ALL, split_axis=0, concat_axis=0, tiled=True)]
    reduce_scatter x4, waiting for transfers between devices: 11.7 us -> 0.04 us  [scatter_dp(): return lax.psum_scatter(value, 'dp', scatter_dimension=0, tiled=True)]
    all_to_all x2, waiting for transfers between devices: 24.8 us -> 14.4 us  [swap_ctx(): return lax.all_to_all(value, 'ctx', split_axis=0, concat_axis=0, tiled=True)]
    all_to_all x2 -> x1, blocking collectives: 36.3 us -> 27.9 us  [swap_ctx(): return lax.all_to_all(value, 'ctx', split_axis=0, concat_axis=0, tiled=True)]
  transfers between devices with their start and end apart: 26 -> 25, of which waited for: 11 -> 10; matrix products, arithmetic and copies ran while one was open for 44% -> 29% of each run, Pallas kernels for 14% -> 41%
where the time goes in v3:
time: 982 us; the launch traced here: 967 us
  Pallas kernels  396 us (40%)
  matrix products  202 us (21%)
  waiting for transfers between devices  129 us (13%)
  blocking collectives  72.2 us (7%)
  other arithmetic  65.1 us (7%)
  local copies, waits for them, and re-layouts  44.2 us (5%)
  starting transfers between devices  43.8 us (4%)
  between operations  15.2 us (2%)
    pallas_call x1, Pallas kernels, join_blocks(): pl.pallas_call(kernel, in_specs=[pl.BlockSpec(memory_space=pl.ANY)] * len...  255 us
    ppermute x14, waiting for transfers between devices, exchange(): return lax.ppermute(value, axis, [(i, i ^ offset) for i in range(size)])  106 us
    dot_general x6, matrix products, matmul(): return jnp.dot(a, b, preferred_element_type=F32)  90.6 us
    dot_general x4, matrix products, outer(): lax.dot_general(a, b, (((0,), (0,)), ((), ())), preferred_element_type=F32)  74.9 us
    pallas_call x1, Pallas kernels, attention(): pl.pallas_call(attention_kernel, out_shape=[jax.ShapeDtypeStruct((slots,...  74.2 us
    pallas_call x2, Pallas kernels, product(): pl.pallas_call(kernel, grid=(columns // wide, (high - low) // tall), in_s...  45.9 us
    all_to_all x1, blocking collectives, gather_small(): return lax.all_to_all(copies, ALL, split_axis=0, concat_axis=0, tiled=True)  44.3 us
    dot_general x2, matrix products, matmul_t(): lax.dot_general(a, b, (((1,), (1,)), ((), ())), preferred_element_type=F32)  36.3 us
  transfers between devices with their start and end apart: 25, of which 10 were waited for; matrix products, arithmetic and copies ran while one was open for 29% of the time, Pallas kernels for 41%

profile of v3, /device:TPU:0, one launch (start us, length us, event | category | flops | bytes accessed | tf_op | source)
XLA Modules:
  0.0 967.3 jit_solution(5534077590184363454)
XLA Ops:
  11.0 27.9 %all_to_all.33 = bf16[4,64,3584]{2,1,0:T(8,128)(2,1)S(1)} all-to-all(bf16[4,64,3584]{2,1,0:T(8,128)(2,1)} %deal_columns.1), channel_id=1, replica_groups=mesh['dp'=8,'ctx'=4] {'ctx'}, dimensions={0} | all-to-all | bytes 3670016 | tf_op jit(solution)/shard_map/all_to_all | solution.py:449
  46.8 44.3 %all_to_all.34 = bf16[32,2,352]{2,1,0:T(2,128)(2,1)S(1)} all-to-all(bf16[32,2,352]{2,1,0:T(2,128)(2,1)S(1)} %reshape.386), channel_id=1, replica_groups=mesh['dp'=8,'ctx'=4] {'dp','ctx'}, dimensions={0} | all-to-all | bytes 90112 | tf_op jit(solution)/shard_map/all_to_all | solution.py:437
  126.3 43.4 %collective-permute-done.2.refs_3_.refs_2_ = bf16[768,2048]{1,0:T(8,128)(2,1)} collective-permute-done((bf16[768,2048]{1,0:T(8,128)(2,1)}, bf16[768,2048]{1,0:T(8,128)(2,1)}, u32[]{:S(2)}, u32[]{:S(2)}) %collective-permute-start.2) | collective-permute-done | bytes 3145760 | tf_op jit(solution)/shard_map/ppermute | solution.py:363
  170.0 12.0 %norm_rows.1 = bf16[2048,2048]{1,0:T(8,128)(2,1)} custom-call(bf16[512,2048]{1,0:T(8,128)(2,1)S(1)} %bitcast.57, bf16[512,2048]{1,0:T(8,128)(2,1)} %collective-permute-done.refs_1_, bf16[512,2048]{1,0:T(8,128)(2,1)} %collective-permute-done.1.refs_2_, bf16[768,2048]{1,0:T(8,128)(2,1)} %collective-permute-done.2.refs_3_.refs_2_, ...), custom_call_target="tpu_custom_call" | custom-call | flops 41943040 | bytes 16777216 | tf_op jit(solution)/shard_map/norm_rows/pallas_call | solution.py:277
  188.9 32.2 %multiply_add_fusion = (f32[2048,2048]{1,0:T(8,128)}, bf16[2048,2048]{1,0:T(8,128)(2,1)}) fusion(f32[2048]{0:T(1024)S(1)} %bitcast.80, bf16[2048,2048]{1,0:T(8,128)(2,1)} %norm_rows.1, bf16[2048,2048]{1,0:T(8,128)(2,1)} %all-gather.7.cloned.1.call-done.refs_3_), kind=kOutput, calls=%fused_computation.5 | convolution fusion | flops 17242783744 | bytes 41951232 | tf_op jit(solution)/shard_map/dot_general | solution.py:453
  221.1 255.3 %join_rows.1 = bf16[2048,2048]{1,0:T(8,128)(2,1)} custom-call(bf16[512,2048]{1,0:T(8,128)(2,1)} %bitcast.61, bf16[768,2048]{1,0:T(8,128)(2,1)} %collective-permute-done.3.refs_4_.refs_1_, bf16[768,2048]{1,0:T(8,128)(2,1)} %collective-permute-done.2.refs_3_.refs_2_, bf16[256,2048]{1,0:T(8,128)(2,1)} %collective-permute-done.4.refs_3_, ...), custom_call_target="tpu_custom_call" | custom-call | flops 4194304 | bytes 16777216 | tf_op jit(solution)/shard_map/join_rows/pallas_call | solution.py:306
  476.4 23.7 %convolution_convert_fusion.1 = bf16[2048,2048]{1,0:T(8,128)(2,1)} fusion(bf16[2048,2048]{1,0:T(8,128)(2,1)} %get-tuple-element.52, bf16[2048,2048]{1,0:T(8,128)(2,1)} %join_rows.1), kind=kOutput, calls=%fused_computation.13 | convolution fusion | flops 17184063488 | bytes 25165824 | tf_op jit(solution)/shard_map/dot_general | solution.py:461
  510.6 19.3 %convolution_add_fusion.qkv_ref = f32[2048,1536]{1,0:T(8,128)} fusion(bf16[2048,2048]{1,0:T(8,128)(2,1)} %norm_rows.1, bf16[2048,1536]{1,0:T(8,128)(2,1)} %all-gather.9.cloned.1.call-done.refs_1_, f32[1536]{0:T(1024)S(1)} %reshape.325), kind=kOutput, calls=%fused_computation.10 | convolution fusion | flops 12888047616 | bytes 27269120 | tf_op jit(solution)/shard_map/dot_general | solution.py:453
  530.0 74.2 %attention.1 = (bf16[2048,512]{1,0:T(8,128)(2,1)}, bf16[2048,1536]{1,0:T(8,128)(2,1)}) custom-call(s32[16]{0:T(128)S(1)} %copy-done.4, s32[16]{0:T(128)S(1)} %copy-done.6, s32[16]{0:T(128)S(1)} %and_select_fusion.low_ref, f32[2048,1536]{1,0:T(8,128)} %convolution_add_fusion.qkv_ref, bf16[2048,512]{1,0:T(8,128)(2,1)} %convolution_convert_fusion.4.cot_ref, ...), custom_call_target="tpu_custom_call" | custom-call | flops 1073741824 | bytes 3145728 | tf_op jit(solution)/shard_map/attention/pallas_call | solution.py:229
  604.2 9.9 %convolution_convert_fusion.3 = bf16[512,2048]{1,0:T(8,128)(2,1)} fusion(bf16[2048,512]{1,0:T(8,128)(2,1)} %get-tuple-element.66, bf16[2048,2048]{1,0:T(8,128)(2,1)} %join_rows.1), kind=kOutput, calls=%fused_computation.46 | convolution fusion | flops 4296015872 | bytes 12582912 | tf_op jit(solution)/shard_map/dot_general | solution.py:461
  614.1 14.4 %fusion.20 = f32[1024,2048]{1,0:T(8,128)} fusion(bf16[2048,2048]{1,0:T(8,128)(2,1)} %all-gather.11.cloned.1.call-done, bf16[2048,2048]{1,0:T(8,128)(2,1)} %get-tuple-element.52), kind=kOutput, calls=%fused_computation.40 | convolution fusion | flops 8589934592 | bytes 20971520 | tf_op jit(solution)/shard_map/dot_general | solution.py:453
  631.4 19.2 %convolution_convert_fusion.2 = bf16[2048,1536]{1,0:T(8,128)(2,1)} fusion(bf16[2048,2048]{1,0:T(8,128)(2,1)} %norm_rows.1, bf16[2048,1536]{1,0:T(8,128)(2,1)} %get-tuple-element.70.refs_0_), kind=kOutput, calls=%fused_computation.14 | convolution fusion | flops 12888047616 | bytes 20971520 | tf_op jit(solution)/shard_map/dot_general | solution.py:461
  650.6 13.1 %fusion.18 = f32[1024,2048]{1,0:T(8,128)S(1)} fusion(bf16[2048,2048]{1,0:T(8,128)(2,1)} %all-gather.11.cloned.1.call-done, bf16[2048,2048]{1,0:T(8,128)(2,1)} %get-tuple-element.52), kind=kOutput, calls=%fused_computation.38 | convolution fusion | flops 8589934592 | bytes 20971520 | tf_op jit(solution)/shard_map/dot_general | solution.py:453
  679.6 26.4 %convert_reduce_fusion = (f32[2048]{0:T(1024)}, bf16[2048,2048]{1,0:T(8,128)(2,1)}) fusion(f32[2048,2048]{1,0:T(8,128)} %get-tuple-element.68, bf16[2048,2048]{1,0:T(8,128)(2,1)} %join_rows.1, bf16[2048,2048]{1,0:T(8,128)(2,1)} %all-gather.11.cloned.1.call-done), kind=kOutput, calls=%fused_computation.3 | convolution fusion | flops 17196644352 | bytes 41951232 | tf_op jit(solution)/shard_map/dot_general | solution.py:457
  706.1 11.8 %collective-permute-done.6 = bf16[512,2048]{1,0:T(8,128)(2,1)} collective-permute-done((bf16[512,2048]{1,0:T(8,128)(2,1)}, bf16[512,2048]{1,0:T(8,128)(2,1)}, u32[]{:S(2)}, u32[]{:S(2)}) %collective-permute-start.6) | collective-permute-done | bytes 2097184 | tf_op jit(solution)/shard_map/ppermute | solution.py:363
  725.9 15.4 %collective-permute-done.7 = bf16[256,2048]{1,0:T(8,128)(2,1)S(1)} collective-permute-done((bf16[256,2048]{1,0:T(8,128)(2,1)S(1)}, bf16[256,2048]{1,0:T(8,128)(2,1)S(1)}, u32[]{:S(2)}, u32[]{:S(2)}) %collective-permute-start.7) | collective-permute-done | bytes 1048608 | tf_op jit(solution)/shard_map/ppermute | solution.py:363
  744.5 22.1 %convolution_convert_fusion = bf16[2048,2048]{1,0:T(8,128)(2,1)} fusion(bf16[2048,2048]{1,0:T(8,128)(2,1)S(1)} %bitcast.66, bf16[2048,2048]{1,0:T(8,128)(2,1)} %get-tuple-element.71.refs_2_), kind=kOutput, calls=%fused_computation.12 | convolution fusion | flops 17184063488 | bytes 25165824 | tf_op jit(solution)/shard_map/dot_general | solution.py:461
  782.8 22.8 %product_nt.3 = bf16[1024,2048]{1,0:T(8,128)(2,1)} custom-call(bf16[2048,1536]{1,0:T(8,128)(2,1)} %get-tuple-element.70.refs_0_, bf16[2048,1536]{1,0:T(8,128)(2,1)} %all-gather.9.cloned.1.call-done.refs_1_, bf16[2048,2048]{1,0:T(8,128)(2,1)} %get-tuple-element.71.refs_2_, bf16[2048,2048]{1,0:T(8,128)(2,1)} %all-gather.7.cloned.1.call-done.refs_3_), custom_call_target="tpu_custom_call" | custom-call | flops 75161927680 | bytes 2097152 | tf_op jit(solution)/shard_map/product_nt/pallas_call | solution.py:515
  812.1 23.1 %product_nt.2 = f32[1024,2048]{1,0:T(8,128)} custom-call(bf16[2048,1536]{1,0:T(8,128)(2,1)} %get-tuple-element.70.refs_0_, bf16[2048,1536]{1,0:T(8,128)(2,1)} %all-gather.9.cloned.1.call-done.refs_1_, bf16[2048,2048]{1,0:T(8,128)(2,1)} %get-tuple-element.71.refs_2_, bf16[2048,2048]{1,0:T(8,128)(2,1)} %all-gather.7.cloned.1.call-done.refs_3_), custom_call_target="tpu_custom_call" | custom-call | flops 75161927680 | bytes 2097152 | tf_op jit(solution)/shard_map/product_nt/pallas_call | solution.py:515
  835.2 13.1 %collective-permute-done.10 = bf16[512,2048]{1,0:T(8,128)(2,1)S(1)} collective-permute-done((bf16[512,2048]{1,0:T(8,128)(2,1)S(1)}, bf16[512,2048]{1,0:T(8,128)(2,1)S(1)}, u32[]{:S(2)}, u32[]{:S(2)}) %collective-permute-start.10) | collective-permute-done | bytes 2097184 | tf_op jit(solution)/shard_map/ppermute | solution.py:363
  861.4 10.3 %collective-permute-done.11 = bf16[256,2048]{1,0:T(8,128)(2,1)} collective-permute-done((bf16[256,2048]{1,0:T(8,128)(2,1)S(1)}, bf16[256,2048]{1,0:T(8,128)(2,1)}, u32[]{:S(2)}, u32[]{:S(2)}) %collective-permute-start.11) | collective-permute-done | bytes 1048608 | tf_op jit(solution)/shard_map/ppermute | solution.py:363
  883.0 12.0 %collective-permute-done.13 = bf16[256,2048]{1,0:T(8,128)(2,1)S(1)} collective-permute-done((bf16[256,2048]{1,0:T(8,128)(2,1)}, bf16[256,2048]{1,0:T(8,128)(2,1)S(1)}, u32[]{:S(2)}, u32[]{:S(2)}) %collective-permute-start.13) | collective-permute-done | bytes 1048608 | tf_op jit(solution)/shard_map/ppermute | solution.py:363
  909.0 22.0 %all-to-all-start.3 = ((f32[32,1,640]{2,1,0:T(1,128)}), f32[32,1,640]{2,1,0:T(1,128)S(1)}, u32[]{:S(2)}, u32[]{:S(2)}) async-start(f32[32,1,640]{2,1,0:T(1,128)} %all_to_all.25), calls=%async_computation.5 | async-start | bytes 163840 | tf_op jit(solution)/shard_map/all_to_all | solution.py:726
  945.8 10.0 %all-to-all-done.4.x_ref = bf16[4,64,2048]{2,1,0:T(8,128)(2,1)S(1)} async-done(((bf16[4,64,2048]{2,1,0:T(8,128)(2,1)}), bf16[4,64,2048]{2,1,0:T(8,128)(2,1)S(1)}, u32[]{:S(2)}, u32[]{:S(2)}) %all-to-all-start.4) | async-done | bytes 1048608 | tf_op jit(solution)/shard_map/all_to_all | solution.py:449
  (240 shorter events, 174.2 us)
Async XLA Ops:
  7.2 174.9 %all-gather.5.cloned.1.call-start = ((), (), s32[]{:S(2)}) async-start(), calls=%async_computation.9 | async-start | bytes 2359296 | tf_op jit(solution)/shard_map/all_gather | solution.py:441
  7.9 181.0 %all-gather.7.cloned.1.call-start = ((), (), s32[]{:S(2)}) async-start(), calls=%async_computation.10 | async-start | bytes 9437184 | tf_op jit(solution)/shard_map/all_gather | solution.py:441
  41.3 469.4 %all-gather.9.cloned.1.call-start = ((), (), s32[]{:S(2)}) async-start(), calls=%async_computation.11 | async-start | bytes 7077888 | tf_op jit(solution)/shard_map/all_gather | solution.py:441
  43.4 560.8 %all-gather.11.cloned.1.call-start = ((), (), s32[]{:S(2)}) async-start(), calls=%async_computation.13 | async-start | bytes 9437184 | tf_op jit(solution)/shard_map/all_gather | solution.py:441
  43.5 47.7 %collective-permute-start = (bf16[512,2048]{1,0:T(8,128)(2,1)S(1)}, bf16[512,2048]{1,0:T(8,128)(2,1)}, u32[]{:S(2)}, u32[]{:S(2)}) collective-permute-start(bf16[512,2048]{1,0:T(8,128)(2,1)S(1)} %bitcast.55), channel_id=1, source_target_pairs={{0,1},{1,0},{2,3},{3,2},{4,5},{5,4},{6,7},{7,6},{8,9},{9,8},{10,11... | collective-permute-start | bytes 6291464 | tf_op jit(solution)/shard_map/ppermute | solution.py:363
  44.5 46.8 %collective-permute-start.1 = (bf16[512,2048]{1,0:T(8,128)(2,1)S(1)}, bf16[512,2048]{1,0:T(8,128)(2,1)}, u32[]{:S(2)}, u32[]{:S(2)}) collective-permute-start(bf16[512,2048]{1,0:T(8,128)(2,1)S(1)} %bitcast.56), channel_id=1, source_target_pairs={{0,2},{1,3},{2,0},{3,1},{4,6},{5,7},{6,4},{7,5},{8,10},{9,11},{10,... | collective-permute-start | bytes 6291464 | tf_op jit(solution)/shard_map/ppermute | solution.py:363
  91.3 537.3 %reduce-scatter.5.cloned.1.call-start = ((), (), s32[]{:S(2)}) async-start(), calls=%async_computation.12 | async-start | bytes 9437184 | tf_op jit(solution)/shard_map/reduce_scatter | solution.py:445
  99.3 70.5 %collective-permute-start.2 = (bf16[768,2048]{1,0:T(8,128)(2,1)}, bf16[768,2048]{1,0:T(8,128)(2,1)}, u32[]{:S(2)}, u32[]{:S(2)}) collective-permute-start(bf16[768,2048]{1,0:T(8,128)(2,1)} %get-tuple-element.99), channel_id=1, source_target_pairs={{0,2},{1,3},{2,0},{3,1},{4,6},{5,7},{6,4},{7,5},{8,10},{9,11},{10,... | collective-permute-start | bytes 9437192 | tf_op jit(solution)/shard_map/ppermute | solution.py:363
  99.8 70.2 %collective-permute-start.3 = (bf16[768,2048]{1,0:T(8,128)(2,1)}, bf16[768,2048]{1,0:T(8,128)(2,1)}, u32[]{:S(2)}, u32[]{:S(2)}) collective-permute-start(bf16[768,2048]{1,0:T(8,128)(2,1)} %get-tuple-element.98), channel_id=1, source_target_pairs={{0,1},{1,0},{2,3},{3,2},{4,5},{5,4},{6,7},{7,6},{8,9},{9,8},{10,11... | collective-permute-start | bytes 9437192 | tf_op jit(solution)/shard_map/ppermute | solution.py:363
  184.3 36.8 %collective-permute-start.5 = (bf16[256,2048]{1,0:T(8,128)(2,1)}, bf16[256,2048]{1,0:T(8,128)(2,1)}, u32[]{:S(2)}, u32[]{:S(2)}) collective-permute-start(bf16[256,2048]{1,0:T(8,128)(2,1)} %slice.136), channel_id=1, source_target_pairs={{0,1},{1,0},{2,3},{3,2},{4,5},{5,4},{6,7},{7,6},{8,9},{9,8},{10,11... | collective-permute-start | bytes 3145736 | tf_op jit(solution)/shard_map/ppermute | solution.py:363
  188.1 33.0 %collective-permute-start.4 = (bf16[256,2048]{1,0:T(8,128)(2,1)}, bf16[256,2048]{1,0:T(8,128)(2,1)}, u32[]{:S(2)}, u32[]{:S(2)}) collective-permute-start(bf16[256,2048]{1,0:T(8,128)(2,1)} %slice.135), channel_id=1, source_target_pairs={{0,2},{1,3},{2,0},{3,1},{4,6},{5,7},{6,4},{7,5},{8,10},{9,11},{10,... | collective-permute-start | bytes 3145736 | tf_op jit(solution)/shard_map/ppermute | solution.py:363
  500.2 267.6 %reduce-scatter.7.cloned.1.call-start = ((), (), s32[]{:S(2)}) async-start(), calls=%async_computation.14 | async-start | bytes 7077888 | tf_op jit(solution)/shard_map/reduce_scatter | solution.py:445
  650.6 280.5 %reduce-scatter.11.cloned.1.call-start = ((), (), s32[]{:S(2)}) async-start(), calls=%async_computation.16 | async-start | bytes 9437184 | tf_op jit(solution)/shard_map/reduce_scatter | solution.py:445
  677.8 40.1 %collective-permute-start.6 = (bf16[512,2048]{1,0:T(8,128)(2,1)}, bf16[512,2048]{1,0:T(8,128)(2,1)}, u32[]{:S(2)}, u32[]{:S(2)}) collective-permute-start(bf16[512,2048]{1,0:T(8,128)(2,1)} %get-tuple-element.94), channel_id=1, source_target_pairs={{0,2},{1,3},{2,0},{3,1},{4,6},{5,7},{6,4},{7,5},{8,10},{9,11},{10,... | collective-permute-start | bytes 6291464 | tf_op jit(solution)/shard_map/ppermute | solution.py:363
  679.1 44.5 %collective-permute-start.8 = (bf16[512,2048]{1,0:T(8,128)(2,1)}, bf16[512,2048]{1,0:T(8,128)(2,1)}, u32[]{:S(2)}, u32[]{:S(2)}) collective-permute-start(bf16[512,2048]{1,0:T(8,128)(2,1)} %get-tuple-element.95), channel_id=1, source_target_pairs={{0,1},{1,0},{2,3},{3,2},{4,5},{5,4},{6,7},{7,6},{8,9},{9,8},{10,11... | collective-permute-start | bytes 6291464 | tf_op jit(solution)/shard_map/ppermute | solution.py:363
  722.3 18.9 %collective-permute-start.7 = (bf16[256,2048]{1,0:T(8,128)(2,1)S(1)}, bf16[256,2048]{1,0:T(8,128)(2,1)S(1)}, u32[]{:S(2)}, u32[]{:S(2)}) collective-permute-start(bf16[256,2048]{1,0:T(8,128)(2,1)S(1)} %fusion.29), channel_id=1, source_target_pairs={{0,1},{1,0},{2,3},{3,2},{4,5},{5,4},{6,7},{7,6},{8,9},{9,8},{10,11... | collective-permute-start | bytes 3145736 | tf_op jit(solution)/shard_map/ppermute | solution.py:363
  743.7 39.0 %collective-permute-start.9 = (bf16[256,2048]{1,0:T(8,128)(2,1)}, bf16[256,2048]{1,0:T(8,128)(2,1)}, u32[]{:S(2)}, u32[]{:S(2)}) collective-permute-start(bf16[256,2048]{1,0:T(8,128)(2,1)} %get-tuple-element.91), channel_id=1, source_target_pairs={{0,2},{1,3},{2,0},{3,1},{4,6},{5,7},{6,4},{7,5},{8,10},{9,11},{10,... | collective-permute-start | bytes 3145736 | tf_op jit(solution)/shard_map/ppermute | solution.py:363
  771.3 171.0 %reduce-scatter.9.cloned.1.call-start = ((), (), s32[]{:S(2)}) async-start(), calls=%async_computation.15 | async-start | bytes 2359296 | tf_op jit(solution)/shard_map/reduce_scatter | solution.py:445
  809.6 38.7 %collective-permute-start.10 = (bf16[512,2048]{1,0:T(8,128)(2,1)S(1)}, bf16[512,2048]{1,0:T(8,128)(2,1)S(1)}, u32[]{:S(2)}, u32[]{:S(2)}) collective-permute-start(bf16[512,2048]{1,0:T(8,128)(2,1)S(1)} %get-tuple-element.92), channel_id=1, source_target_pairs={{0,2},{1,3},{2,0},{3,1},{4,6},{5,7},{6,4},{7,5},{8,10},{9,11},{10,... | collective-permute-start | bytes 6291464 | tf_op jit(solution)/shard_map/ppermute | solution.py:363
  811.4 47.7 %collective-permute-start.12 = (bf16[512,2048]{1,0:T(8,128)(2,1)}, bf16[512,2048]{1,0:T(8,128)(2,1)}, u32[]{:S(2)}, u32[]{:S(2)}) collective-permute-start(bf16[512,2048]{1,0:T(8,128)(2,1)} %get-tuple-element.93), channel_id=1, source_target_pairs={{0,1},{1,0},{2,3},{3,2},{4,5},{5,4},{6,7},{7,6},{8,9},{9,8},{10,11... | collective-permute-start | bytes 6291464 | tf_op jit(solution)/shard_map/ppermute | solution.py:363
  852.8 19.0 %collective-permute-start.11 = (bf16[256,2048]{1,0:T(8,128)(2,1)S(1)}, bf16[256,2048]{1,0:T(8,128)(2,1)}, u32[]{:S(2)}, u32[]{:S(2)}) collective-permute-start(bf16[256,2048]{1,0:T(8,128)(2,1)S(1)} %fusion.24), channel_id=1, source_target_pairs={{0,1},{1,0},{2,3},{3,2},{4,5},{5,4},{6,7},{7,6},{8,9},{9,8},{10,11... | collective-permute-start | bytes 3145736 | tf_op jit(solution)/shard_map/ppermute | solution.py:363
  876.9 18.1 %collective-permute-start.13 = (bf16[256,2048]{1,0:T(8,128)(2,1)}, bf16[256,2048]{1,0:T(8,128)(2,1)S(1)}, u32[]{:S(2)}, u32[]{:S(2)}) collective-permute-start(bf16[256,2048]{1,0:T(8,128)(2,1)} %get-tuple-element.89), channel_id=1, source_target_pairs={{0,2},{1,3},{2,0},{3,1},{4,6},{5,7},{6,4},{7,5},{8,10},{9,11},{10,... | collective-permute-start | bytes 3145736 | tf_op jit(solution)/shard_map/ppermute | solution.py:363
  909.0 29.7 %all-to-all-start.3 = ((f32[32,1,640]{2,1,0:T(1,128)}), f32[32,1,640]{2,1,0:T(1,128)S(1)}, u32[]{:S(2)}, u32[]{:S(2)}) async-start(f32[32,1,640]{2,1,0:T(1,128)} %all_to_all.25), calls=%async_computation.5 | async-start | bytes 163840 | tf_op jit(solution)/shard_map/all_to_all | solution.py:726
  938.7 17.1 %all-to-all-start.4 = ((bf16[4,64,2048]{2,1,0:T(8,128)(2,1)}), bf16[4,64,2048]{2,1,0:T(8,128)(2,1)S(1)}, u32[]{:S(2)}, u32[]{:S(2)}) async-start(bf16[4,64,2048]{2,1,0:T(8,128)(2,1)} %bitcast.69), calls=%async_computation.8 | async-start | bytes 2097152 | tf_op jit(solution)/shard_map/all_to_all | solution.py:449
  (41 other events, 870.6 us)
Sparse Core Ops, SparseCore 0:
  9.6 31.7 all-gather.4
  43.6 82.5 all-gather.6
  127.9 63.1 all-gather.8
  192.5 80.6 all-gather.10
  500.3 89.9 reduce-scatter.4
  650.7 70.2 reduce-scatter.6
  766.8 100.2 reduce-scatter.10
  869.4 37.4 reduce-scatter.8

commit v4 on v3

--- a/solution.py
+++ b/solution.py
@@ -255,63 +255,46 @@
     return arrays, places
 
 
-def norm_blocks(found, order, rows, gain, shift):
+def visit_blocks(body, found, order, rows, extra, outs, name):
     arrays, places = pick_rows(found, order, rows)
     width = arrays[0].shape[1]
 
     def kernel(*refs):
-        out = refs[-1]
         step = pl.program_id(0)
+        given = refs[len(arrays) : len(arrays) + len(extra)]
         for number, (which, block) in enumerate(places):
 
             @pl.when(step == number)
             def _(ref=refs[which], block=block):
-                x = ref[block * rows : (block + 1) * rows, :]
-                x, _ = standardise(x.astype(F32))
-                out[...] = (x * refs[-3][...] + refs[-2][...]).astype(BF)
+                results = body(ref[block * rows : (block + 1) * rows, :], *[g[...] for g in given])
+                for out, value in zip(refs[-outs:], results):
+                    out[...] = value
 
     once = pl.Buffered(1)
-    in_specs = [pl.BlockSpec(a.shape, lambda i: (0, 0), pipeline_mode=once) for a in arrays]
-    in_specs += [pl.BlockSpec((1, width), lambda i: (0, 0), pipeline_mode=once)] * 2
+    held = arrays + list(extra)
     size = len(order) * rows * width
     return pl.pallas_call(
         kernel,
         grid=(len(order),),
-        in_specs=in_specs,
-        out_specs=pl.BlockSpec((rows, width), lambda i: (i, 0)),
-        out_shape=jax.ShapeDtypeStruct((len(order) * rows, width), BF),
+        in_specs=[pl.BlockSpec(a.shape, lambda i: (0, 0), pipeline_mode=once) for a in held],
+        out_specs=[pl.BlockSpec((rows, width), lambda i: (i, 0))] * outs,
+        out_shape=[jax.ShapeDtypeStruct((len(order) * rows, width), BF)] * outs,
         compiler_params=pltpu.CompilerParams(vmem_limit_bytes=40 * 1024 * 1024),
         cost_estimate=pl.CostEstimate(flops=size * 10, bytes_accessed=4 * size, transcendentals=0),
-        name="norm_rows",
-    )(*arrays, gain[None, :], shift[None, :])
+        name=name,
+    )(*held)
+
+
+def norm_blocks(found, order, rows, gain, shift):
+    def body(x, gain, shift):
+        x, _ = standardise(x.astype(F32))
+        return (x * gain + shift).astype(BF), x.astype(BF)
+
+    return visit_blocks(body, found, order, rows, [gain[None, :], shift[None, :]], 2, "norm_rows")
 
 
 def join_blocks(found, order, rows):
-    arrays, places = pick_rows(found, order, rows)
-    width = arrays[0].shape[1]
-
-    def kernel(*refs):
-        out, arrived = refs[-2], refs[-1]
-        copies = []
-        for number, (which, block) in enumerate(places):
-            source = refs[which].at[pl.ds(block * rows, rows), :]
-            target = out.at[pl.ds(number * rows, rows), :]
-            copies.append(pltpu.make_async_copy(source, target, arrived.at[number]))
-        for copy in copies:
-            copy.start()
-        for copy in copies:
-            copy.wait()
-
-    size = len(order) * rows * width
-    return pl.pallas_call(
-        kernel,
-        in_specs=[pl.BlockSpec(memory_space=pl.ANY)] * len(arrays),
-        out_specs=pl.BlockSpec(memory_space=pl.ANY),
-        out_shape=jax.ShapeDtypeStruct((len(order) * rows, width), BF),
-        scratch_shapes=[pltpu.SemaphoreType.DMA((len(order),))],
-        cost_estimate=pl.CostEstimate(flops=size, bytes_accessed=4 * size, transcendentals=0),
-        name="join_rows",
-    )(*arrays)
+    return visit_blocks(lambda x: (x,), found, order, rows, [], 1, "join_rows")[0]
 
 
 def deal_columns(matrices, chunks):
@@ -389,7 +372,7 @@
             split_halves(send(first, offset=j), j, left)
         for j in range(1, size):
             split_halves(send(second, offset=j), j, right)
-        return left, right, first
+        return left, right, (right[1, 0][0],)
     one, two = send(first, offset=1), send(first, offset=2)
     split_halves(one, 1, left)
     split_halves(two, 2, left)
@@ -401,35 +384,31 @@
     right[2, 0], right[2, 1] = (far, half), (far, 2 * half)
     right[3, 0] = (send(near[half : 2 * half], offset=2), 0)
     right[3, 1] = (send(far[2 * half :], offset=1), 0)
-    return left, right, one
-
-
-def sum_cut(size):
-    return 4 if size == 4 else 2
-
-
-def sum_blocks(away, size):
-    away = away.astype(BF)
+    return left, right, (near, far)
+
+
+def sum_ranges(size):
+    if size == 4:
+        return (0, 4), [(4, 6), (6, 8)]
+    return (0, 2), [(2 * j, 2 * j + 2) for j in range(1, size)]
+
+
+def sum_send(pieces, size):
+    distances = (2, 1) if size == 4 else range(1, size)
+    return tuple(exchange(x.astype(BF), "ctx", size, j) for x, j in zip(pieces, distances))
+
+
+def sum_end(own, arrived, size):
     if size != 4:
-        blocks = away.reshape(size - 1, -1, away.shape[1])
-        arrived = tuple(exchange(blocks[j - 1], "ctx", size, j) for j in range(1, size))
-        return arrived, lambda own: (sum([x.astype(F32) for x in arrived], own), arrived)
-    half = away.shape[0] // 4
-    arrived = (
-        exchange(away[: 2 * half], "ctx", size, 2),
-        exchange(away[2 * half :], "ctx", size, 1),
-    )
-
-    def finish(own):
-        far, near = arrived[0].astype(F32), arrived[1].astype(F32)
-        top = exchange((own[2 * half : 3 * half] + far[half:]).astype(BF), "ctx", size, 1)
-        low = exchange((own[3 * half :] + near[half:]).astype(BF), "ctx", size, 2)
-        last = (top, low)
-        top = own[:half] + far[:half] + top.astype(F32)
-        low = own[half : 2 * half] + near[:half] + low.astype(F32)
-        return jnp.concatenate([top, low], axis=0), last
-
-    return arrived, finish
+        return sum([x.astype(F32) for x in arrived], own), arrived
+    half = own.shape[0] // 4
+    far, near = arrived[0].astype(F32), arrived[1].astype(F32)
+    top = exchange((own[2 * half : 3 * half] + far[half:]).astype(BF), "ctx", size, 1)
+    low = exchange((own[3 * half :] + near[half:]).astype(BF), "ctx", size, 2)
+    last = (top, low)
+    top = own[:half] + far[:half] + top.astype(F32)
+    low = own[half : 2 * half] + near[:half] + low.astype(F32)
+    return jnp.concatenate([top, low], axis=0), last
 
 
 def gather_small(value, devices):
@@ -605,9 +584,9 @@
         everything = everything.reshape(own_heads, C, HEAD, width)
         w_out_own = lax.dynamic_index_in_dim(everything, c, 1, keepdims=False)
         w_out_own = w_out_own.reshape(own_heads * HEAD, width)
-    both_rows = swap_ctx(deal_columns((w_up, w_qkv), (up_chunks, qkv_chunks)))
-    both_rows = both_rows.reshape(C * row_block, -1)
-    up_rows, qkv_rows = both_rows[:, :own_ff], both_rows[:, own_ff:]
+    up_rows = swap_ctx(deal_columns((w_up,), (up_chunks,))).reshape(C * row_block, -1)
+    qkv_send = deal_columns((w_qkv,), (qkv_chunks,))
+    qkv_rows = swap_ctx(after(qkv_send, *arrived)).reshape(C * row_block, -1)
     w_up_own = gather_dp(up_rows)
     w_qkv_own = gather_dp(qkv_rows)
 
@@ -640,8 +619,8 @@
         (gain, cosine, sine, first_place, block_place, slot_block, own_bias)
     )
     step = own_slots // 2
-    normed = norm_blocks(hidden_parts, half_blocks(C), step, gain, shift)
-    w_down_own = gather_dp(after(w_down, arrived))
+    normed, xhat_all = norm_blocks(hidden_parts, half_blocks(C), step, gain, shift)
+    w_down_own = gather_dp(after(w_down, up_rows))
     own_up_bias = lax.dynamic_index_in_dim(up_bias.reshape(N, C, ff_block), c, 1, keepdims=False)
     up = matmul(after(normed, w_out_own), w_up_own) + own_up_bias.reshape(-1)
     value, slope = gelu_pair(up)
@@ -653,22 +632,44 @@
     down_part = outer(active, grad_all).astype(BF)
     down_grad = scatter_dp(down_part).astype(F32)
 
-    qkv = matmul(after(normed, down_part), w_qkv_own) + own_bias
     d_attended = matmul_t(after(grad_all, down_part), w_out_own).astype(BF)
+
+    def column_grad(part, chunks):
+        own = scatter_dp(part)
+        return own, collect_columns(swap_ctx(own.reshape(C, row_block, -1)), chunks)
+
+    d_up = (matmul_t(after(grad_all, d_attended), w_down_own) * slope).astype(BF)
+    up_part = outer(normed, d_up).astype(BF)
+    up_rows_grad, up_grad = column_grad(up_part, up_chunks)
+
+    qkv = matmul(after(normed, up_part), w_qkv_own) + own_bias
     attended, d_qkv = attention(
         qkv, d_attended, cosine, sine, first_place, block_place, slot_block
     )
 
-    def column_grad(part, chunks):
-        own = scatter_dp(part)
-        return collect_columns(swap_ctx(own.reshape(C, row_block, -1)), chunks)
-
-    cut = sum_cut(C) * step
-
-    def out_rows(rows, attended):
-        return matmul(attended[rows], w_out_own) + matmul(active[rows], w_down_own)
-
-    out_part = outer(attended, after(grad_all, w_down_own))
+    near_range, away_ranges = sum_ranges(C)
+
+    def out_rows(half_range, dtype, attended):
+        pairs = [(active, w_down_own), (attended, w_out_own)]
+        return product("nn", pairs, (dtype,), row_range=[i * step for i in half_range])
+
+    out_away = [out_rows(r, BF, attended) for r in away_ranges]
+    out_arrived = sum_send(out_away, C)
+    out_near = out_rows(near_range, F32, after(attended, *out_away))
+    qkv_part = outer(after(normed, out_near, down_grad), d_qkv).astype(BF)
+    _, qkv_grad = column_grad(qkv_part, qkv_chunks)
+    out_sum, out_last = sum_end(after(out_near, qkv_part), out_arrived, C)
+    output = hidden_own.astype(F32) + out_sum + (out_bias + down_bias)
+    output = output.astype(BF).reshape(hidden_in.shape)
+
+    def normed_rows(half_range, dtype, d_qkv):
+        pairs = [(d_qkv, w_qkv_own), (d_up, w_up_own)]
+        return product("nt", pairs, (dtype,), row_range=[i * step for i in half_range])
+
+    d_away = [normed_rows(r, BF, after(d_qkv, qkv_part)) for r in away_ranges]
+    d_arrived = sum_send(d_away, C)
+    d_near = normed_rows(near_range, F32, after(d_qkv, up_rows_grad, *d_away, *out_last))
+    out_part = outer(after(attended, d_near), grad_all)
     if aligned:
         out_part = out_part.astype(BF)
         out_grad = scatter_dp(out_part).astype(F32)
@@ -681,38 +682,12 @@
             spread.reshape(heads * HEAD, width), ALL, scatter_dimension=0, tiled=True
         )
 
-    qkv_part = outer(after(normed, down_grad, out_part), d_qkv).astype(BF)
-    qkv_grad = column_grad(qkv_part, qkv_chunks)
-
-    out_away = out_rows(slice(cut, None), after(attended, qkv_part)).astype(BF)
-    out_arrived, finish = sum_blocks(out_away, C)
-    out_near = out_rows(slice(0, cut), after(attended, out_away))
-    grad_then = after(grad_all, out_near)
-    d_up = (matmul_t(grad_then, w_down_own) * slope).astype(BF)
-    up_part = outer(normed, d_up).astype(BF)
-    up_grad = column_grad(up_part, up_chunks)
-    out_sum, out_last = finish(after(out_near, d_up))
-    output = hidden_own.astype(F32) + out_sum + (out_bias + down_bias)
-    output = output.astype(BF).reshape(hidden_in.shape)
-
-    d_qkv_then, d_up_then = lax.optimization_barrier((d_qkv, d_up, up_part, qkv_grad) + out_last)[:2]
-
-    def normed_rows(row_range, dtype):
-        pairs = [(d_qkv_then, w_qkv_own), (d_up_then, w_up_own)]
-        return product("nt", pairs, (dtype,), row_range=row_range)
-
-    d_away = normed_rows((cut, slots), BF)
-    d_near = normed_rows((0, cut), F32)
-    d_normed, _ = sum_blocks(d_away, C)[1](d_near)
-    xhat, scale = standardise(hidden_own.astype(F32))
-    e = d_normed * gain
-    d_hidden = e - jnp.mean(e, axis=-1, keepdims=True)
-    d_hidden = (d_hidden - xhat * jnp.mean(e * xhat, axis=-1, keepdims=True)) * scale
-    grad_in = (grad_own.astype(F32) + d_hidden).astype(BF).reshape(hidden_in.shape)
-
     devices = N * C
-    gain_grad = jnp.sum(d_normed * xhat, axis=0)
-    shift_grad = jnp.sum(d_normed, axis=0)
+    gain_grad = shift_grad = 0.0
+    for r, piece in zip([near_range] + away_ranges, [d_near] + d_away):
+        piece = piece.astype(F32)
+        gain_grad += jnp.sum(piece * xhat_all[r[0] * step : r[1] * step].astype(F32), axis=0)
+        shift_grad += jnp.sum(piece, axis=0)
     bias_grad = jnp.sum(grad_own.astype(F32), axis=0)
     up_bias_grad = jnp.sum(d_up.astype(F32), axis=0).reshape(N, 1, ff_block)
     qkv_bias_grad = jnp.sum(d_qkv.astype(F32), axis=0).reshape(groups, 3, 2, HEAD)
@@ -722,9 +697,16 @@
     qkv_bias_grad = jnp.where(mine[None, None, None, :, None], qkv_bias_grad, 0.0)
     small = [gain_grad, shift_grad, qkv_bias_grad, bias_grad, up_bias_grad]
     small = jnp.concatenate([s.reshape(devices, -1) for s in small], axis=1)
-    small = after(small, grad_in)
     small = lax.all_to_all(small, ALL, split_axis=0, concat_axis=0, tiled=True)
     small = jnp.split(jnp.sum(small, axis=0), cuts[:4])
+
+    d_normed, _ = sum_end(d_near, d_arrived, C)
+    d_normed = after(d_normed, up_grad, *small)
+    xhat, scale = standardise(hidden_own.astype(F32))
+    e = d_normed * gain
+    d_hidden = e - jnp.mean(e, axis=-1, keepdims=True)
+    d_hidden = (d_hidden - xhat * jnp.mean(e * xhat, axis=-1, keepdims=True)) * scale
+    grad_in = (grad_own.astype(F32) + d_hidden).astype(BF).reshape(hidden_in.shape)
 
     return (
         output,

time: 982 us -> 750 us (0.76); the launches traced: 967 us -> 749 us
  Pallas kernels: 396 us -> 186 us
  matrix products: 202 us -> 162 us
  waiting for transfers between devices: 129 us -> 165 us
  other arithmetic: 65.1 us -> 75.5 us
    pallas_call x2, Pallas kernels: 267 us -> 25.2 us  [visit_blocks(): pl.pallas_call(kernel, grid=(len(order),), in_specs=[pl.BlockSpec(a.shape...]
    ppermute x14, waiting for transfers between devices: 106 us -> 154 us  [exchange(): return lax.ppermute(value, axis, [(i, i ^ offset) for i in range(size)])]
    pallas_call x2 -> x6, Pallas kernels: 45.9 us -> 87.1 us  [product(): pl.pallas_call(kernel, grid=(columns // wide, (high - low) // tall), in_s...]
    dot_general x6 -> x2, matrix products: 90.6 us -> 52.1 us  [matmul(): return jnp.dot(a, b, preferred_element_type=F32)]
    pallas_call x1, Pallas kernels: 74.2 us -> 64.2 us  [attention(): pl.pallas_call(attention_kernel, out_shape=[jax.ShapeDtypeStruct((slots,...]
    slice x4 -> x0, local copies, waits for them, and re-layouts: 9.83 us -> none  [the longest x2 6.64 us: sum_blocks(): away[:2 * half]]
  transfers between devices with their start and end apart: 25 -> 26, of which waited for: 10 -> 10; matrix products, arithmetic and copies ran while one was open for 29% -> 36% of each run, Pallas kernels for 41% -> 25%
where the time goes in v4:
time: 750 us; the launch traced here: 749 us
  Pallas kernels  186 us (25%)
  waiting for transfers between devices  165 us (22%)
  matrix products  162 us (22%)
  other arithmetic  75.5 us (10%)
  blocking collectives  65.3 us (9%)
  starting transfers between devices  42.8 us (6%)
  local copies, waits for them, and re-layouts  37.3 us (5%)
  between operations  15.4 us (2%)
    ppermute x14, waiting for transfers between devices, exchange(): return lax.ppermute(value, axis, [(i, i ^ offset) for i in range(size)])  154 us
    pallas_call x6, Pallas kernels, product(): pl.pallas_call(kernel, grid=(columns // wide, (high - low) // tall), in_s...  87.1 us
    dot_general x4, matrix products, outer(): lax.dot_general(a, b, (((0,), (0,)), ((), ())), preferred_element_type=F32)  73.8 us
    pallas_call x1, Pallas kernels, attention(): pl.pallas_call(attention_kernel, out_shape=[jax.ShapeDtypeStruct((slots,...  64.2 us
    dot_general x2, matrix products, matmul(): return jnp.dot(a, b, preferred_element_type=F32)  52.1 us
    all_to_all x1, blocking collectives, gather_small(): return lax.all_to_all(copies, ALL, split_axis=0, concat_axis=0, tiled=True)  45.3 us
    dot_general x2, matrix products, matmul_t(): lax.dot_general(a, b, (((1,), (1,)), ((), ())), preferred_element_type=F32)  35.9 us
    pallas_call x2, Pallas kernels, visit_blocks(): pl.pallas_call(kernel, grid=(len(order),), in_specs=[pl.BlockSpec(a.shape...  25.2 us
  transfers between devices with their start and end apart: 26, of which 10 were waited for; matrix products, arithmetic and copies ran while one was open for 36% of the time, Pallas kernels for 25%

profile of v4, /device:TPU:0, one launch (start us, length us, event | category | flops | bytes accessed | tf_op | source)
XLA Modules:
  0.0 749.4 jit_solution(5179388612290913811)
XLA Ops:
  10.3 20.0 %all_to_all.38 = bf16[4,64,2048]{2,1,0:T(8,128)(2,1)} all-to-all(bf16[4,64,2048]{2,1,0:T(8,128)(2,1)} %deal_columns.2), channel_id=1, replica_groups=mesh['dp'=8,'ctx'=4] {'ctx'}, dimensions={0} | all-to-all | bytes 2097152 | tf_op jit(solution)/shard_map/all_to_all | solution.py:428
  34.0 45.3 %all_to_all.39 = bf16[32,2,352]{2,1,0:T(2,128)(2,1)S(1)} all-to-all(bf16[32,2,352]{2,1,0:T(2,128)(2,1)S(1)} %reshape.297), channel_id=1, replica_groups=mesh['dp'=8,'ctx'=4] {'dp','ctx'}, dimensions={0} | all-to-all | bytes 90112 | tf_op jit(solution)/shard_map/all_to_all | solution.py:416
  91.6 64.5 %collective-permute-done.3.refs_4_.refs_1_ = bf16[768,2048]{1,0:T(8,128)(2,1)} collective-permute-done((bf16[768,2048]{1,0:T(8,128)(2,1)}, bf16[768,2048]{1,0:T(8,128)(2,1)}, u32[]{:S(2)}, u32[]{:S(2)}) %collective-permute-start.3) | collective-permute-done | bytes 3145760 | tf_op jit(solution)/shard_map/ppermute | solution.py:346
  200.5 14.0 %norm_rows.1 = (bf16[2048,2048]{1,0:T(8,128)(2,1)}, bf16[2048,2048]{1,0:T(8,128)(2,1)}) custom-call(bf16[512,2048]{1,0:T(8,128)(2,1)S(1)} %bitcast.55, bf16[512,2048]{1,0:T(8,128)(2,1)} %collective-permute-done.refs_1_, bf16[512,2048]{1,0:T(8,128)(2,1)} %collective-permute-done.1.refs_2_, bf16[768,2048]{1,0:T(8,128)(2,1)} %collective-permute-done.2.refs_3_.refs_2_, ...), custom_call_target="tpu_custom_call" | custom-call | flops 41943040 | bytes 16777216 | tf_op jit(solution)/shard_map/norm_rows/pallas_call | solution.py:276
  214.5 32.7 %multiply_add_fusion = (f32[2048,2048]{1,0:T(8,128)}, bf16[2048,2048]{1,0:T(8,128)(2,1)S(1)}) fusion(f32[2048]{0:T(1024)S(1)} %bitcast.74, bf16[2048,2048]{1,0:T(8,128)(2,1)} %get-tuple-element.69, bf16[2048,2048]{1,0:T(8,128)(2,1)} %all-gather.7.cloned.1.call-done.refs_3_), kind=kOutput, calls=%fused_computation.5 | convolution fusion | flops 17242783744 | bytes 41951232 | tf_op jit(solution)/shard_map/dot_general | solution.py:432
  247.2 11.2 %join_rows.1 = bf16[2048,2048]{1,0:T(8,128)(2,1)} custom-call(bf16[512,2048]{1,0:T(8,128)(2,1)S(1)} %bitcast.57, bf16[768,2048]{1,0:T(8,128)(2,1)} %collective-permute-done.3.refs_4_.refs_1_, bf16[768,2048]{1,0:T(8,128)(2,1)} %collective-permute-done.2.refs_3_.refs_2_, bf16[256,2048]{1,0:T(8,128)(2,1)} %collective-permute-done.4.refs_3_, ...), custom_call_target="tpu_custom_call" | custom-call | flops 41943040 | bytes 16777216 | tf_op jit(solution)/shard_map/join_rows/pallas_call | solution.py:276
  258.4 21.4 %convolution_convert_fusion.1 = bf16[2048,2048]{1,0:T(8,128)(2,1)} fusion(bf16[2048,2048]{1,0:T(8,128)(2,1)S(1)} %get-tuple-element.52.refs_0_, bf16[2048,2048]{1,0:T(8,128)(2,1)} %join_rows.1), kind=kOutput, calls=%fused_computation.13 | convolution fusion | flops 17184063488 | bytes 25165824 | tf_op jit(solution)/shard_map/dot_general | solution.py:440
  285.8 10.3 %convolution_convert_fusion.4.cot_ref = bf16[2048,512]{1,0:T(8,128)(2,1)} fusion(bf16[2048,2048]{1,0:T(8,128)(2,1)} %join_rows.1, bf16[512,2048]{1,0:T(8,128)(2,1)} %all-gather.5.cloned.1.call-done.refs_3_), kind=kOutput, calls=%fused_computation.42 | convolution fusion | flops 4296015872 | bytes 12582912 | tf_op jit(solution)/shard_map/dot_general | solution.py:436
  296.1 25.6 %convert_reduce_fusion = (f32[2048]{0:T(1024)S(1)}, bf16[2048,2048]{1,0:T(8,128)(2,1)}) fusion(f32[2048,2048]{1,0:T(8,128)} %get-tuple-element.61, bf16[2048,2048]{1,0:T(8,128)(2,1)} %join_rows.1, bf16[2048,2048]{1,0:T(8,128)(2,1)} %all-gather.9.cloned.1.call-done.refs_1_), kind=kOutput, calls=%fused_computation.3 | convolution fusion | flops 17196644352 | bytes 41951232 | tf_op jit(solution)/shard_map/dot_general | solution.py:436
  321.7 23.9 %convolution_convert_fusion = bf16[2048,2048]{1,0:T(8,128)(2,1)} fusion(bf16[2048,2048]{1,0:T(8,128)(2,1)} %get-tuple-element.69, bf16[2048,2048]{1,0:T(8,128)(2,1)} %get-tuple-element.111.refs_2_), kind=kOutput, calls=%fused_computation.12 | convolution fusion | flops 17184063488 | bytes 25165824 | tf_op jit(solution)/shard_map/dot_general | solution.py:440
  346.4 19.4 %convolution_add_fusion.qkv_ref = f32[2048,1536]{1,0:T(8,128)} fusion(bf16[2048,2048]{1,0:T(8,128)(2,1)} %get-tuple-element.69, bf16[2048,1536]{1,0:T(8,128)(2,1)} %all-gather.11.cloned.1.call-done.refs_1_, f32[1536]{0:T(1024)S(1)} %copy-done.30), kind=kOutput, calls=%fused_computation.10 | convolution fusion | flops 12888047616 | bytes 27269120 | tf_op jit(solution)/shard_map/dot_general | solution.py:432
  365.8 64.2 %attention.1 = (bf16[2048,512]{1,0:T(8,128)(2,1)}, bf16[2048,1536]{1,0:T(8,128)(2,1)}) custom-call(s32[16]{0:T(128)S(1)} %copy-done.6, s32[16]{0:T(128)S(1)} %copy-done.8, s32[16]{0:T(128)S(1)} %and_select_fusion.low_ref, f32[2048,1536]{1,0:T(8,128)} %convolution_add_fusion.qkv_ref, bf16[2048,512]{1,0:T(8,128)(2,1)} %convolution_convert_fusion.4.cot_ref, ...), custom_call_target="tpu_custom_call" | custom-call | flops 1073741824 | bytes 3145728 | tf_op jit(solution)/shard_map/attention/pallas_call | solution.py:229
  441.8 10.4 %product_nn.4 = bf16[512,2048]{1,0:T(8,128)(2,1)} custom-call(bf16[2048,2048]{1,0:T(8,128)(2,1)} %copy-done.43, bf16[2048,2048]{1,0:T(8,128)(2,1)} %all-gather.9.cloned.1.call-done.refs_1_, bf16[2048,512]{1,0:T(8,128)(2,1)} %get-tuple-element.76.refs_2_, bf16[512,2048]{1,0:T(8,128)(2,1)} %all-gather.5.cloned.1.call-done.refs_3_), custom_call_target="tpu_custom_call" | custom-call | flops 26843545600 | bytes 1048576 | tf_op jit(solution)/shard_map/product_nn/pallas_call | solution.py:494
  453.2 17.2 %product_nn.5 = f32[1024,2048]{1,0:T(8,128)} custom-call(bf16[2048,2048]{1,0:T(8,128)(2,1)} %copy-done.43, bf16[2048,2048]{1,0:T(8,128)(2,1)} %all-gather.9.cloned.1.call-done.refs_1_, bf16[2048,512]{1,0:T(8,128)(2,1)} %get-tuple-element.76.refs_2_, bf16[512,2048]{1,0:T(8,128)(2,1)} %all-gather.5.cloned.1.call-done.refs_3_), custom_call_target="tpu_custom_call" | custom-call | flops 53687091200 | bytes 2097152 | tf_op jit(solution)/shard_map/product_nn/pallas_call | solution.py:494
  472.2 15.3 %collective-permute-done.6 = bf16[512,2048]{1,0:T(8,128)(2,1)} collective-permute-done((bf16[512,2048]{1,0:T(8,128)(2,1)}, bf16[512,2048]{1,0:T(8,128)(2,1)}, u32[]{:S(2)}, u32[]{:S(2)}) %collective-permute-start.6) | collective-permute-done | bytes 2097184 | tf_op jit(solution)/shard_map/ppermute | solution.py:346
  505.4 19.1 %convolution_convert_fusion.2 = bf16[2048,1536]{1,0:T(8,128)(2,1)} fusion(bf16[2048,2048]{1,0:T(8,128)(2,1)} %get-tuple-element.69, bf16[2048,1536]{1,0:T(8,128)(2,1)} %get-tuple-element.73.refs_0_), kind=kOutput, calls=%fused_computation.14 | convolution fusion | flops 12888047616 | bytes 20971520 | tf_op jit(solution)/shard_map/dot_general | solution.py:440
  532.9 13.3 %product_nt.3 = bf16[512,2048]{1,0:T(8,128)(2,1)} custom-call(bf16[2048,1536]{1,0:T(8,128)(2,1)} %get-tuple-element.73.refs_0_, bf16[2048,1536]{1,0:T(8,128)(2,1)} %all-gather.11.cloned.1.call-done.refs_1_, bf16[2048,2048]{1,0:T(8,128)(2,1)} %get-tuple-element.111.refs_2_, bf16[2048,2048]{1,0:T(8,128)(2,1)} %all-gather.7.cloned.1.call-done.refs_3_), custom_call_target="tpu_custom_call" | custom-call | flops 37580963840 | bytes 1048576 | tf_op jit(solution)/shard_map/product_nt/pallas_call | solution.py:494
  547.6 14.8 %collective-permute-done.7 = bf16[256,2048]{1,0:T(8,128)(2,1)S(1)} collective-permute-done((bf16[256,2048]{1,0:T(8,128)(2,1)S(1)}, bf16[256,2048]{1,0:T(8,128)(2,1)S(1)}, u32[]{:S(2)}, u32[]{:S(2)}) %collective-permute-start.7) | collective-permute-done | bytes 1048608 | tf_op jit(solution)/shard_map/ppermute | solution.py:346
  569.1 13.3 %product_nt.4 = bf16[512,2048]{1,0:T(8,128)(2,1)} custom-call(bf16[2048,1536]{1,0:T(8,128)(2,1)} %get-tuple-element.73.refs_0_, bf16[2048,1536]{1,0:T(8,128)(2,1)} %all-gather.11.cloned.1.call-done.refs_1_, bf16[2048,2048]{1,0:T(8,128)(2,1)} %get-tuple-element.111.refs_2_, bf16[2048,2048]{1,0:T(8,128)(2,1)} %all-gather.7.cloned.1.call-done.refs_3_), custom_call_target="tpu_custom_call" | custom-call | flops 37580963840 | bytes 1048576 | tf_op jit(solution)/shard_map/product_nt/pallas_call | solution.py:494
  590.7 22.6 %collective-permute-done.9 = bf16[256,2048]{1,0:T(8,128)(2,1)S(1)} collective-permute-done((bf16[256,2048]{1,0:T(8,128)(2,1)S(1)}, bf16[256,2048]{1,0:T(8,128)(2,1)S(1)}, u32[]{:S(2)}, u32[]{:S(2)}) %collective-permute-start.9) | collective-permute-done | bytes 1048608 | tf_op jit(solution)/shard_map/ppermute | solution.py:346
  613.3 22.9 %product_nt.5 = f32[1024,2048]{1,0:T(8,128)} custom-call(bf16[2048,1536]{1,0:T(8,128)(2,1)} %get-tuple-element.73.refs_0_, bf16[2048,1536]{1,0:T(8,128)(2,1)} %all-gather.11.cloned.1.call-done.refs_1_, bf16[2048,2048]{1,0:T(8,128)(2,1)} %get-tuple-element.111.refs_2_, bf16[2048,2048]{1,0:T(8,128)(2,1)} %all-gather.7.cloned.1.call-done.refs_3_), custom_call_target="tpu_custom_call" | custom-call | flops 75161927680 | bytes 2097152 | tf_op jit(solution)/shard_map/product_nt/pallas_call | solution.py:494
  642.6 14.0 %all-to-all-start.4 = ((f32[32,1,640]{2,1,0:T(1,128)}), f32[32,1,640]{2,1,0:T(1,128)S(1)}, u32[]{:S(2)}, u32[]{:S(2)}) async-start(f32[32,1,640]{2,1,0:T(1,128)} %all_to_all.29), calls=%async_computation.6 | async-start | bytes 163840 | tf_op jit(solution)/shard_map/all_to_all | solution.py:700
  676.3 11.8 %collective-permute-done.11 = bf16[256,2048]{1,0:T(8,128)(2,1)S(1)} collective-permute-done((bf16[256,2048]{1,0:T(8,128)(2,1)S(1)}, bf16[256,2048]{1,0:T(8,128)(2,1)S(1)}, u32[]{:S(2)}, u32[]{:S(2)}) %collective-permute-start.11) | collective-permute-done | bytes 1048608 | tf_op jit(solution)/shard_map/ppermute | solution.py:346
  700.8 17.2 %collective-permute-done.13 = bf16[256,2048]{1,0:T(8,128)(2,1)} collective-permute-done((bf16[256,2048]{1,0:T(8,128)(2,1)}, bf16[256,2048]{1,0:T(8,128)(2,1)}, u32[]{:S(2)}, u32[]{:S(2)}) %collective-permute-start.13) | collective-permute-done | bytes 1048608 | tf_op jit(solution)/shard_map/ppermute | solution.py:346
  (255 shorter events, 189.6 us)
Async XLA Ops:
  7.3 207.2 %all-gather.5.cloned.1.call-start = ((), (), s32[]{:S(2)}) async-start(), calls=%async_computation.10 | async-start | bytes 2359296 | tf_op jit(solution)/shard_map/all_gather | solution.py:420
  8.0 206.5 %all-gather.7.cloned.1.call-start = ((), (), s32[]{:S(2)}) async-start(), calls=%async_computation.11 | async-start | bytes 9437184 | tf_op jit(solution)/shard_map/all_gather | solution.py:420
  30.3 265.8 %all-gather.9.cloned.1.call-start = ((), (), s32[]{:S(2)}) async-start(), calls=%async_computation.12 | async-start | bytes 9437184 | tf_op jit(solution)/shard_map/all_gather | solution.py:420
  31.1 48.4 %collective-permute-start.1 = (bf16[512,2048]{1,0:T(8,128)(2,1)S(1)}, bf16[512,2048]{1,0:T(8,128)(2,1)}, u32[]{:S(2)}, u32[]{:S(2)}) collective-permute-start(bf16[512,2048]{1,0:T(8,128)(2,1)S(1)} %bitcast.53), channel_id=1, source_target_pairs={{0,2},{1,3},{2,0},{3,1},{4,6},{5,7},{6,4},{7,5},{8,10},{9,11},{10,... | collective-permute-start | bytes 6291464 | tf_op jit(solution)/shard_map/ppermute | solution.py:346
  32.0 47.4 %collective-permute-start = (bf16[512,2048]{1,0:T(8,128)(2,1)S(1)}, bf16[512,2048]{1,0:T(8,128)(2,1)}, u32[]{:S(2)}, u32[]{:S(2)}) collective-permute-start(bf16[512,2048]{1,0:T(8,128)(2,1)S(1)} %bitcast.54), channel_id=1, source_target_pairs={{0,1},{1,0},{2,3},{3,2},{4,5},{5,4},{6,7},{7,6},{8,9},{9,8},{10,11... | collective-permute-start | bytes 6291464 | tf_op jit(solution)/shard_map/ppermute | solution.py:346
  85.5 70.6 %collective-permute-start.3 = (bf16[768,2048]{1,0:T(8,128)(2,1)}, bf16[768,2048]{1,0:T(8,128)(2,1)}, u32[]{:S(2)}, u32[]{:S(2)}) collective-permute-start(bf16[768,2048]{1,0:T(8,128)(2,1)} %get-tuple-element.98), channel_id=1, source_target_pairs={{0,1},{1,0},{2,3},{3,2},{4,5},{5,4},{6,7},{7,6},{8,9},{9,8},{10,11... | collective-permute-start | bytes 9437192 | tf_op jit(solution)/shard_map/ppermute | solution.py:346
  86.7 70.3 %collective-permute-start.2 = (bf16[768,2048]{1,0:T(8,128)(2,1)}, bf16[768,2048]{1,0:T(8,128)(2,1)}, u32[]{:S(2)}, u32[]{:S(2)}) collective-permute-start(bf16[768,2048]{1,0:T(8,128)(2,1)} %get-tuple-element.99), channel_id=1, source_target_pairs={{0,2},{1,3},{2,0},{3,1},{4,6},{5,7},{6,4},{7,5},{8,10},{9,11},{10,... | collective-permute-start | bytes 9437192 | tf_op jit(solution)/shard_map/ppermute | solution.py:346
  160.6 185.8 %all-gather.11.cloned.1.call-start = ((), (), s32[]{:S(2)}) async-start(), calls=%async_computation.13 | async-start | bytes 7077888 | tf_op jit(solution)/shard_map/all_gather | solution.py:420
  171.9 330.7 %reduce-scatter.5.cloned.1.call-start = ((), (), s32[]{:S(2)}) async-start(), calls=%async_computation.14 | async-start | bytes 9437184 | tf_op jit(solution)/shard_map/reduce_scatter | solution.py:424
  196.2 51.0 %collective-permute-start.4 = (bf16[256,2048]{1,0:T(8,128)(2,1)}, bf16[256,2048]{1,0:T(8,128)(2,1)}, u32[]{:S(2)}, u32[]{:S(2)}) collective-permute-start(bf16[256,2048]{1,0:T(8,128)(2,1)} %slice.106), channel_id=1, source_target_pairs={{0,2},{1,3},{2,0},{3,1},{4,6},{5,7},{6,4},{7,5},{8,10},{9,11},{10,... | collective-permute-start | bytes 3145736 | tf_op jit(solution)/shard_map/ppermute | solution.py:346
  200.0 47.2 %collective-permute-start.5 = (bf16[256,2048]{1,0:T(8,128)(2,1)}, bf16[256,2048]{1,0:T(8,128)(2,1)}, u32[]{:S(2)}, u32[]{:S(2)}) collective-permute-start(bf16[256,2048]{1,0:T(8,128)(2,1)} %slice.107), channel_id=1, source_target_pairs={{0,1},{1,0},{2,3},{3,2},{4,5},{5,4},{6,7},{7,6},{8,9},{9,8},{10,11... | collective-permute-start | bytes 3145736 | tf_op jit(solution)/shard_map/ppermute | solution.py:346
  279.8 244.8 %reduce-scatter.7.cloned.1.call-start = ((), (), s32[]{:S(2)}) async-start(), calls=%async_computation.15 | async-start | bytes 9437184 | tf_op jit(solution)/shard_map/reduce_scatter | solution.py:424
  345.6 379.0 %reduce-scatter.9.cloned.1.call-start = ((), (), s32[]{:S(2)}) async-start(), calls=%async_computation.16 | async-start | bytes 7077888 | tf_op jit(solution)/shard_map/reduce_scatter | solution.py:424
  440.0 47.4 %collective-permute-start.6 = (bf16[512,2048]{1,0:T(8,128)(2,1)}, bf16[512,2048]{1,0:T(8,128)(2,1)}, u32[]{:S(2)}, u32[]{:S(2)}) collective-permute-start(bf16[512,2048]{1,0:T(8,128)(2,1)} %product_nn.3), channel_id=1, source_target_pairs={{0,2},{1,3},{2,0},{3,1},{4,6},{5,7},{6,4},{7,5},{8,10},{9,11},{10,... | collective-permute-start | bytes 6291464 | tf_op jit(solution)/shard_map/ppermute | solution.py:346
  452.2 46.3 %collective-permute-start.8 = (bf16[512,2048]{1,0:T(8,128)(2,1)}, bf16[512,2048]{1,0:T(8,128)(2,1)}, u32[]{:S(2)}, u32[]{:S(2)}) collective-permute-start(bf16[512,2048]{1,0:T(8,128)(2,1)} %product_nn.4), channel_id=1, source_target_pairs={{0,1},{1,0},{2,3},{3,2},{4,5},{5,4},{6,7},{7,6},{8,9},{9,8},{10,11... | collective-permute-start | bytes 6291464 | tf_op jit(solution)/shard_map/ppermute | solution.py:346
  524.6 62.4 %all-to-all-start.3 = ((bf16[4,64,2048]{2,1,0:T(8,128)(2,1)}), bf16[4,64,2048]{2,1,0:T(8,128)(2,1)S(1)}, u32[]{:S(2)}, u32[]{:S(2)}) async-start(bf16[4,64,2048]{2,1,0:T(8,128)(2,1)} %bitcast.63), calls=%async_computation.5 | async-start | bytes 2097152 | tf_op jit(solution)/shard_map/all_to_all | solution.py:428
  530.8 31.6 %collective-permute-start.7 = (bf16[256,2048]{1,0:T(8,128)(2,1)S(1)}, bf16[256,2048]{1,0:T(8,128)(2,1)S(1)}, u32[]{:S(2)}, u32[]{:S(2)}) collective-permute-start(bf16[256,2048]{1,0:T(8,128)(2,1)S(1)} %fusion.23), channel_id=1, source_target_pairs={{0,1},{1,0},{2,3},{3,2},{4,5},{5,4},{6,7},{7,6},{8,9},{9,8},{10,11... | collective-permute-start | bytes 3145736 | tf_op jit(solution)/shard_map/ppermute | solution.py:346
  546.2 110.5 %collective-permute-start.10 = (bf16[512,2048]{1,0:T(8,128)(2,1)}, bf16[512,2048]{1,0:T(8,128)(2,1)}, u32[]{:S(2)}, u32[]{:S(2)}) collective-permute-start(bf16[512,2048]{1,0:T(8,128)(2,1)} %product_nt.3), channel_id=1, source_target_pairs={{0,2},{1,3},{2,0},{3,1},{4,6},{5,7},{6,4},{7,5},{8,10},{9,11},{10,... | collective-permute-start | bytes 6291464 | tf_op jit(solution)/shard_map/ppermute | solution.py:346
  567.6 45.7 %collective-permute-start.9 = (bf16[256,2048]{1,0:T(8,128)(2,1)S(1)}, bf16[256,2048]{1,0:T(8,128)(2,1)S(1)}, u32[]{:S(2)}, u32[]{:S(2)}) collective-permute-start(bf16[256,2048]{1,0:T(8,128)(2,1)S(1)} %get-tuple-element.97), channel_id=1, source_target_pairs={{0,2},{1,3},{2,0},{3,1},{4,6},{5,7},{6,4},{7,5},{8,10},{9,11},{10,... | collective-permute-start | bytes 3145736 | tf_op jit(solution)/shard_map/ppermute | solution.py:346
  582.4 91.6 %collective-permute-start.12 = (bf16[512,2048]{1,0:T(8,128)(2,1)}, bf16[512,2048]{1,0:T(8,128)(2,1)}, u32[]{:S(2)}, u32[]{:S(2)}) collective-permute-start(bf16[512,2048]{1,0:T(8,128)(2,1)} %product_nt.4), channel_id=1, source_target_pairs={{0,1},{1,0},{2,3},{3,2},{4,5},{5,4},{6,7},{7,6},{8,9},{9,8},{10,11... | collective-permute-start | bytes 6291464 | tf_op jit(solution)/shard_map/ppermute | solution.py:346
  642.6 56.4 %all-to-all-start.4 = ((f32[32,1,640]{2,1,0:T(1,128)}), f32[32,1,640]{2,1,0:T(1,128)S(1)}, u32[]{:S(2)}, u32[]{:S(2)}) async-start(f32[32,1,640]{2,1,0:T(1,128)} %all_to_all.29), calls=%async_computation.6 | async-start | bytes 163840 | tf_op jit(solution)/shard_map/all_to_all | solution.py:700
  656.6 76.6 %reduce-scatter.11.cloned.1.call-start = ((), (), s32[]{:S(2)}) async-start(), calls=%async_computation.17 | async-start | bytes 2359296 | tf_op jit(solution)/shard_map/reduce_scatter | solution.py:424
  662.8 25.4 %collective-permute-start.11 = (bf16[256,2048]{1,0:T(8,128)(2,1)S(1)}, bf16[256,2048]{1,0:T(8,128)(2,1)S(1)}, u32[]{:S(2)}, u32[]{:S(2)}) collective-permute-start(bf16[256,2048]{1,0:T(8,128)(2,1)S(1)} %fusion.18), channel_id=1, source_target_pairs={{0,1},{1,0},{2,3},{3,2},{4,5},{5,4},{6,7},{7,6},{8,9},{9,8},{10,11... | collective-permute-start | bytes 3145736 | tf_op jit(solution)/shard_map/ppermute | solution.py:346
  693.0 25.0 %collective-permute-start.13 = (bf16[256,2048]{1,0:T(8,128)(2,1)}, bf16[256,2048]{1,0:T(8,128)(2,1)}, u32[]{:S(2)}, u32[]{:S(2)}) collective-permute-start(bf16[256,2048]{1,0:T(8,128)(2,1)} %get-tuple-element.95), channel_id=1, source_target_pairs={{0,2},{1,3},{2,0},{3,1},{4,6},{5,7},{6,4},{7,5},{8,10},{9,11},{10,... | collective-permute-start | bytes 3145736 | tf_op jit(solution)/shard_map/ppermute | solution.py:346
  (48 other events, 779.2 us)
Sparse Core Ops, SparseCore 0:
  9.7 31.7 all-gather.4
  43.1 81.5 all-gather.6
  126.3 80.5 all-gather.8
  209.0 63.2 all-gather.10
  279.9 90.0 reduce-scatter.4
  372.1 87.9 reduce-scatter.6
  524.7 76.2 reduce-scatter.8
  674.2 35.6 reduce-scatter.10

commit v5 on v4

--- a/solution.py
+++ b/solution.py
@@ -372,7 +372,7 @@
             split_halves(send(first, offset=j), j, left)
         for j in range(1, size):
             split_halves(send(second, offset=j), j, right)
-        return left, right, (right[1, 0][0],)
+        return left, right
     one, two = send(first, offset=1), send(first, offset=2)
     split_halves(one, 1, left)
     split_halves(two, 2, left)
@@ -384,7 +384,7 @@
     right[2, 0], right[2, 1] = (far, half), (far, 2 * half)
     right[3, 0] = (send(near[half : 2 * half], offset=2), 0)
     right[3, 1] = (send(far[2 * half :], offset=1), 0)
-    return left, right, (near, far)
+    return left, right
 
 
 def sum_ranges(size):
@@ -402,12 +402,12 @@
     if size != 4:
         return sum([x.astype(F32) for x in arrived], own), arrived
     half = own.shape[0] // 4
-    far, near = arrived[0].astype(F32), arrived[1].astype(F32)
-    top = exchange((own[2 * half : 3 * half] + far[half:]).astype(BF), "ctx", size, 1)
-    low = exchange((own[3 * half :] + near[half:]).astype(BF), "ctx", size, 2)
-    last = (top, low)
-    top = own[:half] + far[:half] + top.astype(F32)
-    low = own[half : 2 * half] + near[:half] + low.astype(F32)
+    far, near = arrived
+    top = (own[2 * half : 3 * half] + far[half:].astype(F32)).astype(BF)
+    low = (own[3 * half :] + near[half:].astype(F32)).astype(BF)
+    last = (exchange(top, "ctx", size, 1), exchange(low, "ctx", size, 2))
+    top = own[:half] + far[:half].astype(F32) + last[0].astype(F32)
+    low = own[half : 2 * half] + near[:half].astype(F32) + last[1].astype(F32)
     return jnp.concatenate([top, low], axis=0), last
 
 
@@ -561,7 +561,7 @@
     cuts = [sum(sizes[:i]) for i in range(1, len(sizes))]
     small = jnp.concatenate([ln_gain, ln_bias, b_qkv, b_out, b_up, b_down])
     small = gather_small(small, N * C)
-    hidden_parts, grad_parts, arrived = gather_two(hidden_own, grad_own, C, (small,))
+    hidden_parts, grad_parts = gather_two(hidden_own, grad_own, C, (small,))
     pieces = jnp.split(small, cuts, axis=1)
     gain, shift, qkv_bias, out_bias, up_bias, down_bias = [p.reshape(-1).astype(F32) for p in pieces]
     qkv_chunks = [
@@ -586,9 +586,7 @@
         w_out_own = w_out_own.reshape(own_heads * HEAD, width)
     up_rows = swap_ctx(deal_columns((w_up,), (up_chunks,))).reshape(C * row_block, -1)
     qkv_send = deal_columns((w_qkv,), (qkv_chunks,))
-    qkv_rows = swap_ctx(after(qkv_send, *arrived)).reshape(C * row_block, -1)
     w_up_own = gather_dp(up_rows)
-    w_qkv_own = gather_dp(qkv_rows)
 
     half_block = jnp.array([j for j, _ in half_blocks(C)], jnp.int32) ^ c
     half_block = 2 * half_block + jnp.array([half for _, half in half_blocks(C)], jnp.int32)
@@ -606,12 +604,11 @@
     slot_block = jnp.argsort(block_place).astype(jnp.int32)
     first_place = jnp.take(first_all.reshape(-1, BLK), slot_block, axis=0)
     half = ROT // 2
-    frequency = 10000.0 ** (-jnp.arange(half, dtype=F32) * 2.0 / ROT)
+    lane = jnp.arange(PAIR, dtype=jnp.int32) % HEAD
+    frequency = 10000.0 ** (-(lane % half).astype(F32) * 2.0 / ROT)
+    frequency = jnp.where(lane < ROT, frequency, 0.0)
     angles = position_all.astype(F32)[:, None] * frequency
-    cosine, sine = jnp.cos(angles), jnp.sin(angles)
-    rest = jnp.zeros((slots, HEAD - ROT), F32)
-    cosine = jnp.concatenate([cosine, cosine, rest + 1.0] * 2, axis=1)
-    sine = jnp.concatenate([-sine, sine, rest] * 2, axis=1)
+    cosine, sine = jnp.cos(angles), jnp.sin(angles) * jnp.where(lane < half, -1.0, 1.0)
 
     own_bias = lax.dynamic_index_in_dim(qkv_bias.reshape(3, groups, 2, C, HEAD), c, 3, keepdims=False)
     own_bias = own_bias.transpose(1, 0, 2, 3).reshape(-1)
@@ -620,6 +617,8 @@
     )
     step = own_slots // 2
     normed, xhat_all = norm_blocks(hidden_parts, half_blocks(C), step, gain, shift)
+    qkv_rows = swap_ctx(after(qkv_send, normed)).reshape(C * row_block, -1)
+    w_qkv_own = gather_dp(qkv_rows)
     w_down_own = gather_dp(after(w_down, up_rows))
     own_up_bias = lax.dynamic_index_in_dim(up_bias.reshape(N, C, ff_block), c, 1, keepdims=False)
     up = matmul(after(normed, w_out_own), w_up_own) + own_up_bias.reshape(-1)
@@ -655,21 +654,7 @@
 
     out_away = [out_rows(r, BF, attended) for r in away_ranges]
     out_arrived = sum_send(out_away, C)
-    out_near = out_rows(near_range, F32, after(attended, *out_away))
-    qkv_part = outer(after(normed, out_near, down_grad), d_qkv).astype(BF)
-    _, qkv_grad = column_grad(qkv_part, qkv_chunks)
-    out_sum, out_last = sum_end(after(out_near, qkv_part), out_arrived, C)
-    output = hidden_own.astype(F32) + out_sum + (out_bias + down_bias)
-    output = output.astype(BF).reshape(hidden_in.shape)
-
-    def normed_rows(half_range, dtype, d_qkv):
-        pairs = [(d_qkv, w_qkv_own), (d_up, w_up_own)]
-        return product("nt", pairs, (dtype,), row_range=[i * step for i in half_range])
-
-    d_away = [normed_rows(r, BF, after(d_qkv, qkv_part)) for r in away_ranges]
-    d_arrived = sum_send(d_away, C)
-    d_near = normed_rows(near_range, F32, after(d_qkv, up_rows_grad, *d_away, *out_last))
-    out_part = outer(after(attended, d_near), grad_all)
+    out_part = outer(after(attended, *out_away), grad_all)
     if aligned:
         out_part = out_part.astype(BF)
         out_grad = scatter_dp(out_part).astype(F32)
@@ -681,6 +666,21 @@
         out_grad = lax.psum_scatter(
             spread.reshape(heads * HEAD, width), ALL, scatter_dimension=0, tiled=True
         )
+
+    qkv_part = outer(after(normed, down_grad, out_part), d_qkv).astype(BF)
+    _, qkv_grad = column_grad(qkv_part, qkv_chunks)
+    out_near = out_rows(near_range, F32, after(attended, qkv_part))
+
+    def normed_rows(half_range, dtype, d_qkv):
+        pairs = [(d_qkv, w_qkv_own), (d_up, w_up_own)]
+        return product("nt", pairs, (dtype,), row_range=[i * step for i in half_range])
+
+    d_away = [normed_rows(r, BF, after(d_qkv, out_near)) for r in away_ranges]
+    d_arrived = sum_send(d_away, C)
+    out_sum, out_last = sum_end(after(out_near, *d_away), out_arrived, C)
+    output = hidden_own.astype(F32) + out_sum + (out_bias + down_bias)
+    output = output.astype(BF).reshape(hidden_in.shape)
+    d_near = normed_rows(near_range, F32, after(d_qkv, up_rows_grad, *d_away, *out_arrived))
 
     devices = N * C
     gain_grad = shift_grad = 0.0

time: 750 us -> 703 us (0.937); the launches traced: 749 us -> 690 us
  waiting for transfers between devices: 165 us -> 112 us
  local copies, waits for them, and re-layouts: 37.3 us -> 21.2 us
  blocking collectives: 65.3 us -> 79.3 us
  starting transfers between devices: 42.8 us -> 31.2 us
  matrix products: 162 us -> 172 us
  other arithmetic: 75.5 us -> 67.4 us
    ppermute x14, waiting for transfers between devices: 154 us -> 77.1 us  [exchange(): return lax.ppermute(value, axis, [(i, i ^ offset) for i in range(size)])]
    all_to_all x1, waiting for transfers between devices: 0.01 us -> 17.1 us  [on_device(): small = lax.all_to_all(small, ALL, split_axis=0, concat_axis=0, tiled=True)]
    all_to_all x1 -> x2, blocking collectives: 20 us -> 34.1 us  [swap_ctx(): return lax.all_to_all(value, 'ctx', split_axis=0, concat_axis=0, tiled=True)]
    concatenate x2 -> x0, local copies, waits for them, and re-layouts: 10.9 us -> none  [the longest x1 5.54 us: on_device(): sine = jnp.concatenate([-sine, sine, rest] * 2, axis=1)]
    convert_element_type x6 -> x2, other arithmetic: 17.1 us -> 6.8 us  [sum_end(): top = (own[2 * half:3 * half] + far[half:].astype(F32)).astype(BF)]
    dot_general x2, matrix products: 35.9 us -> 45.8 us  [matmul_t(): lax.dot_general(a, b, (((1,), (1,)), ((), ())), preferred_element_type=F32)]
    all_to_all x3 -> x2, waiting for transfers between devices: 9.33 us -> 16.1 us  [swap_ctx(): return lax.all_to_all(value, 'ctx', split_axis=0, concat_axis=0, tiled=True)]
  transfers between devices with their start and end apart: 26 -> 25, of which waited for: 10 -> 7; matrix products, arithmetic and copies ran while one was open for 36% -> 37% of each run, Pallas kernels for 25% -> 27%
where the time goes in v5:
time: 703 us; the launch traced here: 690 us
  Pallas kernels  192 us (27%)
  matrix products  172 us (24%)
  waiting for transfers between devices  112 us (16%)
  blocking collectives  79.3 us (11%)
  other arithmetic  67.4 us (10%)
  starting transfers between devices  31.2 us (4%)
  local copies, waits for them, and re-layouts  21.2 us (3%)
  between operations  15.3 us (2%)
    pallas_call x6, Pallas kernels, product(): pl.pallas_call(kernel, grid=(columns // wide, (high - low) // tall), in_s...  86.9 us
    ppermute x14, waiting for transfers between devices, exchange(): return lax.ppermute(value, axis, [(i, i ^ offset) for i in range(size)])  77.1 us
    dot_general x4, matrix products, outer(): lax.dot_general(a, b, (((0,), (0,)), ((), ())), preferred_element_type=F32)  75.3 us
    pallas_call x1, Pallas kernels, attention(): pl.pallas_call(attention_kernel, out_shape=[jax.ShapeDtypeStruct((slots,...  70.7 us
    dot_general x2, matrix products, matmul(): return jnp.dot(a, b, preferred_element_type=F32)  50.8 us
    dot_general x2, matrix products, matmul_t(): lax.dot_general(a, b, (((1,), (1,)), ((), ())), preferred_element_type=F32)  45.8 us
    all_to_all x1, blocking collectives, gather_small(): return lax.all_to_all(copies, ALL, split_axis=0, concat_axis=0, tiled=True)  45.3 us
    all_to_all x2, blocking collectives, swap_ctx(): return lax.all_to_all(value, 'ctx', split_axis=0, concat_axis=0, tiled=True)  34.1 us
  transfers between devices with their start and end apart: 25, of which 7 were waited for; matrix products, arithmetic and copies ran while one was open for 37% of the time, Pallas kernels for 27%

profile of v5, /device:TPU:0, one launch (start us, length us, event | category | flops | bytes accessed | tf_op | source)
XLA Modules:
  0.0 690.4 jit_solution(8252192041585987949)
XLA Ops:
  10.3 20.0 %all_to_all.38 = bf16[4,64,2048]{2,1,0:T(8,128)(2,1)} all-to-all(bf16[4,64,2048]{2,1,0:T(8,128)(2,1)} %deal_columns.2), channel_id=1, replica_groups=mesh['dp'=8,'ctx'=4] {'ctx'}, dimensions={0} | all-to-all | bytes 2097152 | tf_op jit(solution)/shard_map/all_to_all | solution.py:428
  34.0 45.3 %all_to_all.39 = bf16[32,2,352]{2,1,0:T(2,128)(2,1)S(1)} all-to-all(bf16[32,2,352]{2,1,0:T(2,128)(2,1)S(1)} %reshape.321), channel_id=1, replica_groups=mesh['dp'=8,'ctx'=4] {'dp','ctx'}, dimensions={0} | all-to-all | bytes 90112 | tf_op jit(solution)/shard_map/all_to_all | solution.py:416
  104.3 51.8 %collective-permute-done.3.refs_4_.refs_1_ = bf16[768,2048]{1,0:T(8,128)(2,1)} collective-permute-done((bf16[768,2048]{1,0:T(8,128)(2,1)}, bf16[768,2048]{1,0:T(8,128)(2,1)}, u32[]{:S(2)}, u32[]{:S(2)}) %collective-permute-start.3) | collective-permute-done | bytes 3145760 | tf_op jit(solution)/shard_map/ppermute | solution.py:346
  157.1 13.6 %norm_rows.1 = (bf16[2048,2048]{1,0:T(8,128)(2,1)}, bf16[2048,2048]{1,0:T(8,128)(2,1)}) custom-call(bf16[512,2048]{1,0:T(8,128)(2,1)S(1)} %bitcast.55, bf16[512,2048]{1,0:T(8,128)(2,1)} %collective-permute-done.refs_1_, bf16[512,2048]{1,0:T(8,128)(2,1)} %collective-permute-done.1.refs_2_, bf16[768,2048]{1,0:T(8,128)(2,1)} %collective-permute-done.2.refs_3_.refs_2_, ...), custom_call_target="tpu_custom_call" | custom-call | flops 41943040 | bytes 16777216 | tf_op jit(solution)/shard_map/norm_rows/pallas_call | solution.py:276
  170.8 14.1 %all_to_all.40 = bf16[4,64,1536]{2,1,0:T(8,128)(2,1)} all-to-all(bf16[4,64,1536]{2,1,0:T(8,128)(2,1)S(1)} %copy-done.13), channel_id=1, replica_groups=mesh['dp'=8,'ctx'=4] {'ctx'}, dimensions={0} | all-to-all | bytes 1572864 | tf_op jit(solution)/shard_map/all_to_all | solution.py:428
  191.3 31.4 %multiply_add_fusion = (f32[2048,2048]{1,0:T(8,128)}, bf16[2048,2048]{1,0:T(8,128)(2,1)S(1)}) fusion(f32[2048]{0:T(1024)S(1)} %bitcast.72, bf16[2048,2048]{1,0:T(8,128)(2,1)} %get-tuple-element.69, bf16[2048,2048]{1,0:T(8,128)(2,1)} %all-gather.7.cloned.1.call-done.refs_3_), kind=kOutput, calls=%fused_computation.5 | convolution fusion | flops 17242783744 | bytes 41951232 | tf_op jit(solution)/shard_map/dot_general | solution.py:432
  222.8 11.2 %join_rows.1 = bf16[2048,2048]{1,0:T(8,128)(2,1)} custom-call(bf16[512,2048]{1,0:T(8,128)(2,1)S(1)} %bitcast.57, bf16[768,2048]{1,0:T(8,128)(2,1)} %collective-permute-done.3.refs_4_.refs_1_, bf16[768,2048]{1,0:T(8,128)(2,1)} %collective-permute-done.2.refs_3_.refs_2_, bf16[256,2048]{1,0:T(8,128)(2,1)} %collective-permute-done.4.refs_3_, ...), custom_call_target="tpu_custom_call" | custom-call | flops 41943040 | bytes 16777216 | tf_op jit(solution)/shard_map/join_rows/pallas_call | solution.py:276
  233.9 22.1 %convolution_convert_fusion.1 = bf16[2048,2048]{1,0:T(8,128)(2,1)} fusion(bf16[2048,2048]{1,0:T(8,128)(2,1)S(1)} %get-tuple-element.52.refs_0_, bf16[2048,2048]{1,0:T(8,128)(2,1)} %join_rows.1), kind=kOutput, calls=%fused_computation.13 | convolution fusion | flops 17184063488 | bytes 25165824 | tf_op jit(solution)/shard_map/dot_general | solution.py:440
  256.2 9.9 %convolution_convert_fusion.4.cot_ref = bf16[2048,512]{1,0:T(8,128)(2,1)} fusion(bf16[2048,2048]{1,0:T(8,128)(2,1)} %join_rows.1, bf16[512,2048]{1,0:T(8,128)(2,1)} %all-gather.5.cloned.1.call-done.refs_3_), kind=kOutput, calls=%fused_computation.42 | convolution fusion | flops 4296015872 | bytes 12582912 | tf_op jit(solution)/shard_map/dot_general | solution.py:436
  266.1 35.8 %convert_reduce_fusion = (f32[2048]{0:T(1024)S(1)}, bf16[2048,2048]{1,0:T(8,128)(2,1)}) fusion(f32[2048,2048]{1,0:T(8,128)} %get-tuple-element.61, bf16[2048,2048]{1,0:T(8,128)(2,1)} %join_rows.1, bf16[2048,2048]{1,0:T(8,128)(2,1)} %all-gather.9.cloned.1.call-done.refs_1_), kind=kOutput, calls=%fused_computation.3 | convolution fusion | flops 17196644352 | bytes 41951232 | tf_op jit(solution)/shard_map/dot_general | solution.py:436
  301.9 23.8 %convolution_convert_fusion = bf16[2048,2048]{1,0:T(8,128)(2,1)} fusion(bf16[2048,2048]{1,0:T(8,128)(2,1)} %get-tuple-element.69, bf16[2048,2048]{1,0:T(8,128)(2,1)} %get-tuple-element.110.refs_2_), kind=kOutput, calls=%fused_computation.12 | convolution fusion | flops 17184063488 | bytes 25165824 | tf_op jit(solution)/shard_map/dot_general | solution.py:440
  331.2 19.4 %convolution_add_fusion.qkv_ref = f32[2048,1536]{1,0:T(8,128)} fusion(bf16[2048,2048]{1,0:T(8,128)(2,1)} %get-tuple-element.69, bf16[2048,1536]{1,0:T(8,128)(2,1)} %all-gather.11.cloned.1.call-done.refs_1_, f32[1536]{0:T(1024)S(1)} %copy-done.27), kind=kOutput, calls=%fused_computation.10 | convolution fusion | flops 12888047616 | bytes 27269120 | tf_op jit(solution)/shard_map/dot_general | solution.py:432
  350.5 70.7 %attention.1 = (bf16[2048,512]{1,0:T(8,128)(2,1)}, bf16[2048,1536]{1,0:T(8,128)(2,1)}) custom-call(s32[16]{0:T(128)S(1)} %copy-done.7, s32[16]{0:T(128)S(1)} %copy-done.9, s32[16]{0:T(128)S(1)} %and_select_fusion.low_ref, f32[2048,1536]{1,0:T(8,128)} %convolution_add_fusion.qkv_ref, bf16[2048,512]{1,0:T(8,128)(2,1)} %convolution_convert_fusion.4.cot_ref, ...), custom_call_target="tpu_custom_call" | custom-call | flops 1073741824 | bytes 3145728 | tf_op jit(solution)/shard_map/attention/pallas_call | solution.py:229
  421.2 10.0 %product_nn.3 = bf16[512,2048]{1,0:T(8,128)(2,1)} custom-call(bf16[2048,2048]{1,0:T(8,128)(2,1)} %copy-done.37, bf16[2048,2048]{1,0:T(8,128)(2,1)} %all-gather.9.cloned.1.call-done.refs_1_, bf16[2048,512]{1,0:T(8,128)(2,1)} %get-tuple-element.71.refs_2_, bf16[512,2048]{1,0:T(8,128)(2,1)} %all-gather.5.cloned.1.call-done.refs_3_), custom_call_target="tpu_custom_call" | custom-call | flops 26843545600 | bytes 1048576 | tf_op jit(solution)/shard_map/product_nn/pallas_call | solution.py:494
  432.7 10.4 %product_nn.4 = bf16[512,2048]{1,0:T(8,128)(2,1)} custom-call(bf16[2048,2048]{1,0:T(8,128)(2,1)} %copy-done.37, bf16[2048,2048]{1,0:T(8,128)(2,1)} %all-gather.9.cloned.1.call-done.refs_1_, bf16[2048,512]{1,0:T(8,128)(2,1)} %get-tuple-element.71.refs_2_, bf16[512,2048]{1,0:T(8,128)(2,1)} %all-gather.5.cloned.1.call-done.refs_3_), custom_call_target="tpu_custom_call" | custom-call | flops 26843545600 | bytes 1048576 | tf_op jit(solution)/shard_map/product_nn/pallas_call | solution.py:494
  448.8 10.0 %convolution_convert_fusion.3 = bf16[512,2048]{1,0:T(8,128)(2,1)} fusion(bf16[2048,512]{1,0:T(8,128)(2,1)} %get-tuple-element.71.refs_2_, bf16[2048,2048]{1,0:T(8,128)(2,1)} %join_rows.1), kind=kOutput, calls=%fused_computation.41 | convolution fusion | flops 4296015872 | bytes 12582912 | tf_op jit(solution)/shard_map/dot_general | solution.py:440
  461.7 19.3 %convolution_convert_fusion.2 = bf16[2048,1536]{1,0:T(8,128)(2,1)} fusion(bf16[2048,2048]{1,0:T(8,128)(2,1)} %get-tuple-element.69, bf16[2048,1536]{1,0:T(8,128)(2,1)} %get-tuple-element.74.refs_0_), kind=kOutput, calls=%fused_computation.14 | convolution fusion | flops 12888047616 | bytes 20971520 | tf_op jit(solution)/shard_map/dot_general | solution.py:440
  481.0 17.2 %product_nn.5 = f32[1024,2048]{1,0:T(8,128)} custom-call(bf16[2048,2048]{1,0:T(8,128)(2,1)} %copy-done.37, bf16[2048,2048]{1,0:T(8,128)(2,1)} %all-gather.9.cloned.1.call-done.refs_1_, bf16[2048,512]{1,0:T(8,128)(2,1)} %get-tuple-element.71.refs_2_, bf16[512,2048]{1,0:T(8,128)(2,1)} %all-gather.5.cloned.1.call-done.refs_3_), custom_call_target="tpu_custom_call" | custom-call | flops 53687091200 | bytes 2097152 | tf_op jit(solution)/shard_map/product_nn/pallas_call | solution.py:494
  498.3 13.2 %product_nt.3 = bf16[512,2048]{1,0:T(8,128)(2,1)} custom-call(bf16[2048,1536]{1,0:T(8,128)(2,1)} %get-tuple-element.74.refs_0_, bf16[2048,1536]{1,0:T(8,128)(2,1)} %all-gather.11.cloned.1.call-done.refs_1_, bf16[2048,2048]{1,0:T(8,128)(2,1)} %get-tuple-element.110.refs_2_, bf16[2048,2048]{1,0:T(8,128)(2,1)} %all-gather.7.cloned.1.call-done.refs_3_), custom_call_target="tpu_custom_call" | custom-call | flops 37580963840 | bytes 1048576 | tf_op jit(solution)/shard_map/product_nt/pallas_call | solution.py:494
  512.3 13.4 %product_nt.4 = bf16[512,2048]{1,0:T(8,128)(2,1)} custom-call(bf16[2048,1536]{1,0:T(8,128)(2,1)} %get-tuple-element.74.refs_0_, bf16[2048,1536]{1,0:T(8,128)(2,1)} %all-gather.11.cloned.1.call-done.refs_1_, bf16[2048,2048]{1,0:T(8,128)(2,1)} %get-tuple-element.110.refs_2_, bf16[2048,2048]{1,0:T(8,128)(2,1)} %all-gather.7.cloned.1.call-done.refs_3_), custom_call_target="tpu_custom_call" | custom-call | flops 37580963840 | bytes 1048576 | tf_op jit(solution)/shard_map/product_nt/pallas_call | solution.py:494
  530.9 22.7 %product_nt.5 = f32[1024,2048]{1,0:T(8,128)} custom-call(bf16[2048,1536]{1,0:T(8,128)(2,1)} %get-tuple-element.74.refs_0_, bf16[2048,1536]{1,0:T(8,128)(2,1)} %all-gather.11.cloned.1.call-done.refs_1_, bf16[2048,2048]{1,0:T(8,128)(2,1)} %get-tuple-element.110.refs_2_, bf16[2048,2048]{1,0:T(8,128)(2,1)} %all-gather.7.cloned.1.call-done.refs_3_), custom_call_target="tpu_custom_call" | custom-call | flops 75161927680 | bytes 2097152 | tf_op jit(solution)/shard_map/product_nt/pallas_call | solution.py:494
  578.7 17.1 %all-to-all-done.4 = f32[32,1,640]{2,1,0:T(1,128)S(1)} async-done(((f32[32,1,640]{2,1,0:T(1,128)}), f32[32,1,640]{2,1,0:T(1,128)S(1)}, u32[]{:S(2)}, u32[]{:S(2)}) %all-to-all-start.4) | async-done | bytes 81952 | tf_op jit(solution)/shard_map/all_to_all | solution.py:700
  611.4 10.4 %all-to-all-done.3.x_ref = bf16[4,64,2048]{2,1,0:T(8,128)(2,1)S(1)} async-done(((bf16[4,64,2048]{2,1,0:T(8,128)(2,1)}), bf16[4,64,2048]{2,1,0:T(8,128)(2,1)S(1)}, u32[]{:S(2)}, u32[]{:S(2)}) %all-to-all-start.3) | async-done | bytes 1048608 | tf_op jit(solution)/shard_map/all_to_all | solution.py:428
  641.3 17.4 %collective-permute-done.13 = bf16[256,2048]{1,0:T(8,128)(2,1)S(1)} collective-permute-done((bf16[256,2048]{1,0:T(8,128)(2,1)S(1)}, bf16[256,2048]{1,0:T(8,128)(2,1)S(1)}, u32[]{:S(2)}, u32[]{:S(2)}) %collective-permute-start.13) | collective-permute-done | bytes 1048608 | tf_op jit(solution)/shard_map/ppermute | solution.py:346
  (230 shorter events, 144.7 us)
Async XLA Ops:
  7.3 184.1 %all-gather.5.cloned.1.call-start = ((), (), s32[]{:S(2)}) async-start(), calls=%async_computation.10 | async-start | bytes 2359296 | tf_op jit(solution)/shard_map/all_gather | solution.py:420
  8.0 183.3 %all-gather.7.cloned.1.call-start = ((), (), s32[]{:S(2)}) async-start(), calls=%async_computation.11 | async-start | bytes 9437184 | tf_op jit(solution)/shard_map/all_gather | solution.py:420
  30.3 235.8 %all-gather.9.cloned.1.call-start = ((), (), s32[]{:S(2)}) async-start(), calls=%async_computation.12 | async-start | bytes 9437184 | tf_op jit(solution)/shard_map/all_gather | solution.py:420
  31.1 300.1 %all-gather.11.cloned.1.call-start = ((), (), s32[]{:S(2)}) async-start(), calls=%async_computation.13 | async-start | bytes 7077888 | tf_op jit(solution)/shard_map/all_gather | solution.py:420
  31.1 48.4 %collective-permute-start.1 = (bf16[512,2048]{1,0:T(8,128)(2,1)S(1)}, bf16[512,2048]{1,0:T(8,128)(2,1)}, u32[]{:S(2)}, u32[]{:S(2)}) collective-permute-start(bf16[512,2048]{1,0:T(8,128)(2,1)S(1)} %bitcast.53), channel_id=1, source_target_pairs={{0,2},{1,3},{2,0},{3,1},{4,6},{5,7},{6,4},{7,5},{8,10},{9,11},{10,... | collective-permute-start | bytes 6291464 | tf_op jit(solution)/shard_map/ppermute | solution.py:346
  32.1 47.4 %collective-permute-start = (bf16[512,2048]{1,0:T(8,128)(2,1)S(1)}, bf16[512,2048]{1,0:T(8,128)(2,1)}, u32[]{:S(2)}, u32[]{:S(2)}) collective-permute-start(bf16[512,2048]{1,0:T(8,128)(2,1)S(1)} %bitcast.54), channel_id=1, source_target_pairs={{0,1},{1,0},{2,3},{3,2},{4,5},{5,4},{6,7},{7,6},{8,9},{9,8},{10,11... | collective-permute-start | bytes 6291464 | tf_op jit(solution)/shard_map/ppermute | solution.py:346
  85.6 70.6 %collective-permute-start.3 = (bf16[768,2048]{1,0:T(8,128)(2,1)}, bf16[768,2048]{1,0:T(8,128)(2,1)}, u32[]{:S(2)}, u32[]{:S(2)}) collective-permute-start(bf16[768,2048]{1,0:T(8,128)(2,1)} %get-tuple-element.98), channel_id=1, source_target_pairs={{0,1},{1,0},{2,3},{3,2},{4,5},{5,4},{6,7},{7,6},{8,9},{9,8},{10,11... | collective-permute-start | bytes 9437192 | tf_op jit(solution)/shard_map/ppermute | solution.py:346
  86.8 70.3 %collective-permute-start.2 = (bf16[768,2048]{1,0:T(8,128)(2,1)}, bf16[768,2048]{1,0:T(8,128)(2,1)}, u32[]{:S(2)}, u32[]{:S(2)}) collective-permute-start(bf16[768,2048]{1,0:T(8,128)(2,1)} %get-tuple-element.99), channel_id=1, source_target_pairs={{0,2},{1,3},{2,0},{3,1},{4,6},{5,7},{6,4},{7,5},{8,10},{9,11},{10,... | collective-permute-start | bytes 9437192 | tf_op jit(solution)/shard_map/ppermute | solution.py:346
  184.8 274.1 %reduce-scatter.5.cloned.1.call-start = ((), (), s32[]{:S(2)}) async-start(), calls=%async_computation.14 | async-start | bytes 9437184 | tf_op jit(solution)/shard_map/reduce_scatter | solution.py:424
  187.5 35.2 %collective-permute-start.4 = (bf16[256,2048]{1,0:T(8,128)(2,1)}, bf16[256,2048]{1,0:T(8,128)(2,1)}, u32[]{:S(2)}, u32[]{:S(2)}) collective-permute-start(bf16[256,2048]{1,0:T(8,128)(2,1)} %slice.106), channel_id=1, source_target_pairs={{0,2},{1,3},{2,0},{3,1},{4,6},{5,7},{6,4},{7,5},{8,10},{9,11},{10,... | collective-permute-start | bytes 3145736 | tf_op jit(solution)/shard_map/ppermute | solution.py:346
  190.8 32.0 %collective-permute-start.5 = (bf16[256,2048]{1,0:T(8,128)(2,1)}, bf16[256,2048]{1,0:T(8,128)(2,1)}, u32[]{:S(2)}, u32[]{:S(2)}) collective-permute-start(bf16[256,2048]{1,0:T(8,128)(2,1)} %slice.107), channel_id=1, source_target_pairs={{0,1},{1,0},{2,3},{3,2},{4,5},{5,4},{6,7},{7,6},{8,9},{9,8},{10,11... | collective-permute-start | bytes 3145736 | tf_op jit(solution)/shard_map/ppermute | solution.py:346
  256.1 274.8 %reduce-scatter.7.cloned.1.call-start = ((), (), s32[]{:S(2)}) async-start(), calls=%async_computation.15 | async-start | bytes 9437184 | tf_op jit(solution)/shard_map/reduce_scatter | solution.py:424
  325.8 282.0 %reduce-scatter.11.cloned.1.call-start = ((), (), s32[]{:S(2)}) async-start(), calls=%async_computation.17 | async-start | bytes 2359296 | tf_op jit(solution)/shard_map/reduce_scatter | solution.py:424
  431.2 95.1 %collective-permute-start.6 = (bf16[512,2048]{1,0:T(8,128)(2,1)}, bf16[512,2048]{1,0:T(8,128)(2,1)}, u32[]{:S(2)}, u32[]{:S(2)}) collective-permute-start(bf16[512,2048]{1,0:T(8,128)(2,1)} %product_nn.3), channel_id=1, source_target_pairs={{0,2},{1,3},{2,0},{3,1},{4,6},{5,7},{6,4},{7,5},{8,10},{9,11},{10,... | collective-permute-start | bytes 6291464 | tf_op jit(solution)/shard_map/ppermute | solution.py:346
  443.1 87.8 %collective-permute-start.8 = (bf16[512,2048]{1,0:T(8,128)(2,1)}, bf16[512,2048]{1,0:T(8,128)(2,1)}, u32[]{:S(2)}, u32[]{:S(2)}) collective-permute-start(bf16[512,2048]{1,0:T(8,128)(2,1)} %product_nn.4), channel_id=1, source_target_pairs={{0,1},{1,0},{2,3},{3,2},{4,5},{5,4},{6,7},{7,6},{8,9},{9,8},{10,11... | collective-permute-start | bytes 6291464 | tf_op jit(solution)/shard_map/ppermute | solution.py:346
  458.9 206.0 %reduce-scatter.9.cloned.1.call-start = ((), (), s32[]{:S(2)}) async-start(), calls=%async_computation.16 | async-start | bytes 7077888 | tf_op jit(solution)/shard_map/reduce_scatter | solution.py:424
  511.4 61.7 %collective-permute-start.10 = (bf16[512,2048]{1,0:T(8,128)(2,1)}, bf16[512,2048]{1,0:T(8,128)(2,1)S(1)}, u32[]{:S(2)}, u32[]{:S(2)}) collective-permute-start(bf16[512,2048]{1,0:T(8,128)(2,1)} %product_nt.3), channel_id=1, source_target_pairs={{0,2},{1,3},{2,0},{3,1},{4,6},{5,7},{6,4},{7,5},{8,10},{9,11},{10,... | collective-permute-start | bytes 6291464 | tf_op jit(solution)/shard_map/ppermute | solution.py:346
  525.7 99.8 %collective-permute-start.12 = (bf16[512,2048]{1,0:T(8,128)(2,1)}, bf16[512,2048]{1,0:T(8,128)(2,1)}, u32[]{:S(2)}, u32[]{:S(2)}) collective-permute-start(bf16[512,2048]{1,0:T(8,128)(2,1)} %product_nt.4), channel_id=1, source_target_pairs={{0,1},{1,0},{2,3},{3,2},{4,5},{5,4},{6,7},{7,6},{8,9},{9,8},{10,11... | collective-permute-start | bytes 6291464 | tf_op jit(solution)/shard_map/ppermute | solution.py:346
  529.5 70.0 %collective-permute-start.7 = (bf16[256,2048]{1,0:T(8,128)(2,1)}, bf16[256,2048]{1,0:T(8,128)(2,1)S(1)}, u32[]{:S(2)}, u32[]{:S(2)}) collective-permute-start(bf16[256,2048]{1,0:T(8,128)(2,1)} %add_convert_fusion.1), channel_id=1, source_target_pairs={{0,1},{1,0},{2,3},{3,2},{4,5},{5,4},{6,7},{7,6},{8,9},{9,8},{10,11... | collective-permute-start | bytes 3145736 | tf_op jit(solution)/shard_map/ppermute | solution.py:346
  564.3 31.4 %all-to-all-start.4 = ((f32[32,1,640]{2,1,0:T(1,128)}), f32[32,1,640]{2,1,0:T(1,128)S(1)}, u32[]{:S(2)}, u32[]{:S(2)}) async-start(f32[32,1,640]{2,1,0:T(1,128)} %all_to_all.29), calls=%async_computation.6 | async-start | bytes 163840 | tf_op jit(solution)/shard_map/all_to_all | solution.py:700
  576.9 48.6 %collective-permute-start.11 = (bf16[256,2048]{1,0:T(8,128)(2,1)}, bf16[256,2048]{1,0:T(8,128)(2,1)}, u32[]{:S(2)}, u32[]{:S(2)}) collective-permute-start(bf16[256,2048]{1,0:T(8,128)(2,1)} %fusion.18), channel_id=1, source_target_pairs={{0,1},{1,0},{2,3},{3,2},{4,5},{5,4},{6,7},{7,6},{8,9},{9,8},{10,11... | collective-permute-start | bytes 3145736 | tf_op jit(solution)/shard_map/ppermute | solution.py:346
  595.7 26.0 %all-to-all-start.3 = ((bf16[4,64,2048]{2,1,0:T(8,128)(2,1)}), bf16[4,64,2048]{2,1,0:T(8,128)(2,1)S(1)}, u32[]{:S(2)}, u32[]{:S(2)}) async-start(bf16[4,64,2048]{2,1,0:T(8,128)(2,1)} %bitcast.61), calls=%async_computation.5 | async-start | bytes 2097152 | tf_op jit(solution)/shard_map/all_to_all | solution.py:428
  604.9 32.0 %collective-permute-start.9 = (bf16[256,2048]{1,0:T(8,128)(2,1)}, bf16[256,2048]{1,0:T(8,128)(2,1)S(1)}, u32[]{:S(2)}, u32[]{:S(2)}) collective-permute-start(bf16[256,2048]{1,0:T(8,128)(2,1)} %get-tuple-element.97), channel_id=1, source_target_pairs={{0,2},{1,3},{2,0},{3,1},{4,6},{5,7},{6,4},{7,5},{8,10},{9,11},{10,... | collective-permute-start | bytes 3145736 | tf_op jit(solution)/shard_map/ppermute | solution.py:346
  629.4 29.3 %collective-permute-start.13 = (bf16[256,2048]{1,0:T(8,128)(2,1)S(1)}, bf16[256,2048]{1,0:T(8,128)(2,1)S(1)}, u32[]{:S(2)}, u32[]{:S(2)}) collective-permute-start(bf16[256,2048]{1,0:T(8,128)(2,1)S(1)} %get-tuple-element.95), channel_id=1, source_target_pairs={{0,2},{1,3},{2,0},{3,1},{4,6},{5,7},{6,4},{7,5},{8,10},{9,11},{10,... | collective-permute-start | bytes 3145736 | tf_op jit(solution)/shard_map/ppermute | solution.py:346
  (39 other events, 607.4 us)
Sparse Core Ops, SparseCore 0:
  9.7 31.7 all-gather.4
  43.1 81.5 all-gather.6
  126.3 80.5 all-gather.8
  208.4 63.2 all-gather.10
  273.9 88.2 reduce-scatter.4
  364.3 87.9 reduce-scatter.6
  459.0 38.4 reduce-scatter.10
  526.5 75.1 reduce-scatter.8

commit v6 on v5

--- a/solution.py
+++ b/solution.py
@@ -400,15 +400,16 @@
 
 def sum_end(own, arrived, size):
     if size != 4:
-        return sum([x.astype(F32) for x in arrived], own), arrived
+        return sum([x.astype(F32) for x in arrived], own), arrived, arrived
     half = own.shape[0] // 4
     far, near = arrived
     top = (own[2 * half : 3 * half] + far[half:].astype(F32)).astype(BF)
     low = (own[3 * half :] + near[half:].astype(F32)).astype(BF)
+    sent = (top, low)
     last = (exchange(top, "ctx", size, 1), exchange(low, "ctx", size, 2))
     top = own[:half] + far[:half].astype(F32) + last[0].astype(F32)
     low = own[half : 2 * half] + near[:half].astype(F32) + last[1].astype(F32)
-    return jnp.concatenate([top, low], axis=0), last
+    return jnp.concatenate([top, low], axis=0), last, sent
 
 
 def gather_small(value, devices):
@@ -617,8 +618,6 @@
     )
     step = own_slots // 2
     normed, xhat_all = norm_blocks(hidden_parts, half_blocks(C), step, gain, shift)
-    qkv_rows = swap_ctx(after(qkv_send, normed)).reshape(C * row_block, -1)
-    w_qkv_own = gather_dp(qkv_rows)
     w_down_own = gather_dp(after(w_down, up_rows))
     own_up_bias = lax.dynamic_index_in_dim(up_bias.reshape(N, C, ff_block), c, 1, keepdims=False)
     up = matmul(after(normed, w_out_own), w_up_own) + own_up_bias.reshape(-1)
@@ -628,10 +627,9 @@
         for key in ((3, 0), (3, 1)):
             grad_parts[key] = (after(grad_parts[key][0], active), grad_parts[key][1])
     grad_all = join_blocks(grad_parts, half_blocks(C), step)
-    down_part = outer(active, grad_all).astype(BF)
-    down_grad = scatter_dp(down_part).astype(F32)
-
-    d_attended = matmul_t(after(grad_all, down_part), w_out_own).astype(BF)
+    qkv_rows = swap_ctx(after(qkv_send, grad_all)).reshape(C * row_block, -1)
+    w_qkv_own = gather_dp(qkv_rows)
+    d_attended = matmul_t(grad_all, w_out_own).astype(BF)
 
     def column_grad(part, chunks):
         own = scatter_dp(part)
@@ -641,7 +639,11 @@
     up_part = outer(normed, d_up).astype(BF)
     up_rows_grad, up_grad = column_grad(up_part, up_chunks)
 
-    qkv = matmul(after(normed, up_part), w_qkv_own) + own_bias
+    down_part = outer(after(active, up_part), grad_all).astype(BF)
+    down_rows = scatter_dp(down_part)
+
+
+    qkv = matmul(after(normed, down_part), w_qkv_own) + own_bias
     attended, d_qkv = attention(
         qkv, d_attended, cosine, sine, first_place, block_place, slot_block
     )
@@ -652,12 +654,14 @@
         pairs = [(active, w_down_own), (attended, w_out_own)]
         return product("nn", pairs, (dtype,), row_range=[i * step for i in half_range])
 
-    out_away = [out_rows(r, BF, attended) for r in away_ranges]
+    out_away = [out_rows(r, BF, attended) for r in away_ranges[:1]]
+    attended_then = after(attended, up_grad, *out_away)
+    out_away += [out_rows(r, BF, attended_then) for r in away_ranges[1:]]
     out_arrived = sum_send(out_away, C)
     out_part = outer(after(attended, *out_away), grad_all)
     if aligned:
         out_part = out_part.astype(BF)
-        out_grad = scatter_dp(out_part).astype(F32)
+        out_grad = scatter_dp(out_part)
     else:
         spread = jnp.zeros((own_heads, C, HEAD, width), F32)
         spread = lax.dynamic_update_index_in_dim(
@@ -667,7 +671,7 @@
             spread.reshape(heads * HEAD, width), ALL, scatter_dimension=0, tiled=True
         )
 
-    qkv_part = outer(after(normed, down_grad, out_part), d_qkv).astype(BF)
+    qkv_part = outer(after(normed, up_rows_grad, out_part), d_qkv).astype(BF)
     _, qkv_grad = column_grad(qkv_part, qkv_chunks)
     out_near = out_rows(near_range, F32, after(attended, qkv_part))
 
@@ -677,10 +681,13 @@
 
     d_away = [normed_rows(r, BF, after(d_qkv, out_near)) for r in away_ranges]
     d_arrived = sum_send(d_away, C)
-    out_sum, out_last = sum_end(after(out_near, *d_away), out_arrived, C)
+    d_near = normed_rows(near_range, F32, after(d_qkv, *d_away, *out_arrived))
+    out_sum, _, _ = sum_end(after(out_near, d_near), out_arrived, C)
     output = hidden_own.astype(F32) + out_sum + (out_bias + down_bias)
     output = output.astype(BF).reshape(hidden_in.shape)
-    d_near = normed_rows(near_range, F32, after(d_qkv, up_rows_grad, *d_away, *out_arrived))
+
+    down_grad = after(down_rows, d_near).astype(F32)
+    out_grad = after(out_grad, d_near).astype(F32)
 
     devices = N * C
     gain_grad = shift_grad = 0.0
@@ -697,11 +704,12 @@
     qkv_bias_grad = jnp.where(mine[None, None, None, :, None], qkv_bias_grad, 0.0)
     small = [gain_grad, shift_grad, qkv_bias_grad, bias_grad, up_bias_grad]
     small = jnp.concatenate([s.reshape(devices, -1) for s in small], axis=1)
+    d_normed, _, d_sent = sum_end(d_near, d_arrived, C)
+    small = after(small, *d_sent)
     small = lax.all_to_all(small, ALL, split_axis=0, concat_axis=0, tiled=True)
     small = jnp.split(jnp.sum(small, axis=0), cuts[:4])
 
-    d_normed, _ = sum_end(d_near, d_arrived, C)
-    d_normed = after(d_normed, up_grad, *small)
+    d_normed = after(d_normed, down_rows, *small)
     xhat, scale = standardise(hidden_own.astype(F32))
     e = d_normed * gain
     d_hidden = e - jnp.mean(e, axis=-1, keepdims=True)

time: 703 us -> 675 us (0.960)
  blocking collectives: 79.3 us -> 33.6 us
  waiting for transfers between devices: 112 us -> 132 us
  matrix products: 172 us -> 164 us
    all_to_all x1 -> x0, blocking collectives: 45.3 us -> none  [gather_small(): return lax.all_to_all(copies, ALL, split_axis=0, concat_axis=0, tiled=True)]
    all_to_all x0 -> x1, waiting for transfers between devices: none -> 34.4 us  [gather_small(): return lax.all_to_all(copies, ALL, split_axis=0, concat_axis=0, tiled=True)]
    ppermute x14, waiting for transfers between devices: 77.1 us -> 96.5 us  [exchange(): return lax.ppermute(value, axis, [(i, i ^ offset) for i in range(size)])]
    all_to_all x1, waiting for transfers between devices: 17.1 us -> 0.13 us  [on_device(): small = lax.all_to_all(small, ALL, split_axis=0, concat_axis=0, tiled=True)]
    all_to_all x2, waiting for transfers between devices: 16.1 us -> 0.01 us  [swap_ctx(): return lax.all_to_all(value, 'ctx', split_axis=0, concat_axis=0, tiled=True)]
    dot_general x2, matrix products: 45.8 us -> 35.6 us  [matmul_t(): lax.dot_general(a, b, (((1,), (1,)), ((), ())), preferred_element_type=F32)]
  transfers between devices with their start and end apart: 25 -> 26, of which waited for: 7 -> 6; matrix products, arithmetic and copies ran while one was open for 37% -> 38% of each run, Pallas kernels for 27% -> 29%
where the time goes in v6:
time: 675 us; the launch traced here: 662 us
  Pallas kernels  192 us (28%)
  matrix products  164 us (24%)
  waiting for transfers between devices  132 us (20%)
  other arithmetic  68.2 us (10%)
  starting transfers between devices  34.9 us (5%)
  blocking collectives  33.6 us (5%)
  local copies, waits for them, and re-layouts  21.4 us (3%)
  between operations  15 us (2%)
    ppermute x14, waiting for transfers between devices, exchange(): return lax.ppermute(value, axis, [(i, i ^ offset) for i in range(size)])  96.5 us
    pallas_call x6, Pallas kernels, product(): pl.pallas_call(kernel, grid=(columns // wide, (high - low) // tall), in_s...  87.9 us
    dot_general x4, matrix products, outer(): lax.dot_general(a, b, (((0,), (0,)), ((), ())), preferred_element_type=F32)  76.5 us
    pallas_call x1, Pallas kernels, attention(): pl.pallas_call(attention_kernel, out_shape=[jax.ShapeDtypeStruct((slots,...  72.8 us
    dot_general x2, matrix products, matmul(): return jnp.dot(a, b, preferred_element_type=F32)  51.8 us
    dot_general x2, matrix products, matmul_t(): lax.dot_general(a, b, (((1,), (1,)), ((), ())), preferred_element_type=F32)  35.6 us
    all_to_all x1, waiting for transfers between devices, gather_small(): return lax.all_to_all(copies, ALL, split_axis=0, concat_axis=0, tiled=True)  34.4 us
    all_to_all x2, blocking collectives, swap_ctx(): return lax.all_to_all(value, 'ctx', split_axis=0, concat_axis=0, tiled=True)  33.6 us
  transfers between devices with their start and end apart: 26, of which 6 were waited for; matrix products, arithmetic and copies ran while one was open for 38% of the time, Pallas kernels for 29%

profile of v6, /device:TPU:0, one launch (start us, length us, event | category | flops | bytes accessed | tf_op | source)
XLA Modules:
  0.0 662.0 jit_solution(1411343209812282275)
XLA Ops:
  10.3 20.0 %all_to_all.38 = bf16[4,64,2048]{2,1,0:T(8,128)(2,1)} all-to-all(bf16[4,64,2048]{2,1,0:T(8,128)(2,1)} %deal_columns.2), channel_id=1, replica_groups=mesh['dp'=8,'ctx'=4] {'ctx'}, dimensions={0} | all-to-all | bytes 2097152 | tf_op jit(solution)/shard_map/all_to_all | solution.py:429
  44.9 34.4 %all-to-all-done = bf16[32,2,352]{2,1,0:T(2,128)(2,1)S(1)} async-done(((bf16[32,2,352]{2,1,0:T(2,128)(2,1)}), bf16[32,2,352]{2,1,0:T(2,128)(2,1)S(1)}, u32[]{:S(2)}, u32[]{:S(2)}) %all-to-all-start) | async-done | bytes 45088 | tf_op jit(solution)/shard_map/all_to_all | solution.py:417
  100.1 56.0 %collective-permute-done.3.refs_4_.refs_1_ = bf16[768,2048]{1,0:T(8,128)(2,1)} collective-permute-done((bf16[768,2048]{1,0:T(8,128)(2,1)}, bf16[768,2048]{1,0:T(8,128)(2,1)}, u32[]{:S(2)}, u32[]{:S(2)}) %collective-permute-start.3) | collective-permute-done | bytes 3145760 | tf_op jit(solution)/shard_map/ppermute | solution.py:346
  162.5 13.6 %norm_rows.1 = (bf16[2048,2048]{1,0:T(8,128)(2,1)}, bf16[2048,2048]{1,0:T(8,128)(2,1)}) custom-call(bf16[512,2048]{1,0:T(8,128)(2,1)S(1)} %bitcast.55, bf16[512,2048]{1,0:T(8,128)(2,1)} %collective-permute-done.refs_1_, bf16[512,2048]{1,0:T(8,128)(2,1)} %collective-permute-done.1.refs_2_, bf16[768,2048]{1,0:T(8,128)(2,1)} %collective-permute-done.2.refs_3_.refs_2_, ...), custom_call_target="tpu_custom_call" | custom-call | flops 41943040 | bytes 16777216 | tf_op jit(solution)/shard_map/norm_rows/pallas_call | solution.py:276
  176.1 32.4 %multiply_add_fusion = (f32[2048,2048]{1,0:T(8,128)}, bf16[2048,2048]{1,0:T(8,128)(2,1)}) fusion(f32[2048]{0:T(1024)S(1)} %bitcast.72, bf16[2048,2048]{1,0:T(8,128)(2,1)} %get-tuple-element.74, bf16[2048,2048]{1,0:T(8,128)(2,1)} %all-gather.7.cloned.1.call-done.refs_3_), kind=kOutput, calls=%fused_computation.5 | convolution fusion | flops 17242783744 | bytes 41951232 | tf_op jit(solution)/shard_map/dot_general | solution.py:433
  208.5 8.2 %join_rows.1 = bf16[2048,2048]{1,0:T(8,128)(2,1)} custom-call(bf16[512,2048]{1,0:T(8,128)(2,1)S(1)} %bitcast.57, bf16[768,2048]{1,0:T(8,128)(2,1)} %collective-permute-done.3.refs_4_.refs_1_, bf16[768,2048]{1,0:T(8,128)(2,1)} %collective-permute-done.2.refs_3_.refs_2_, bf16[256,2048]{1,0:T(8,128)(2,1)} %collective-permute-done.4.refs_3_, ...), custom_call_target="tpu_custom_call" | custom-call | flops 41943040 | bytes 16777216 | tf_op jit(solution)/shard_map/join_rows/pallas_call | solution.py:276
  216.7 13.6 %all_to_all.39 = bf16[4,64,1536]{2,1,0:T(8,128)(2,1)} all-to-all(bf16[4,64,1536]{2,1,0:T(8,128)(2,1)S(1)} %copy-done.13), channel_id=1, replica_groups=mesh['dp'=8,'ctx'=4] {'ctx'}, dimensions={0} | all-to-all | bytes 1572864 | tf_op jit(solution)/shard_map/all_to_all | solution.py:429
  230.4 9.9 %convolution_convert_fusion.4.cot_ref = bf16[2048,512]{1,0:T(8,128)(2,1)} fusion(bf16[2048,2048]{1,0:T(8,128)(2,1)} %join_rows.1, bf16[512,2048]{1,0:T(8,128)(2,1)} %all-gather.5.cloned.1.call-done.refs_3_), kind=kOutput, calls=%fused_computation.42 | convolution fusion | flops 4296015872 | bytes 12582912 | tf_op jit(solution)/shard_map/dot_general | solution.py:437
  240.3 25.8 %convert_reduce_fusion = (f32[2048]{0:T(1024)S(1)}, bf16[2048,2048]{1,0:T(8,128)(2,1)}) fusion(f32[2048,2048]{1,0:T(8,128)} %get-tuple-element.64, bf16[2048,2048]{1,0:T(8,128)(2,1)} %join_rows.1, bf16[2048,2048]{1,0:T(8,128)(2,1)} %all-gather.9.cloned.1.call-done.refs_1_), kind=kOutput, calls=%fused_computation.3 | convolution fusion | flops 17196644352 | bytes 41951232 | tf_op jit(solution)/shard_map/dot_general | solution.py:437
  266.1 23.9 %convolution_convert_fusion.1 = bf16[2048,2048]{1,0:T(8,128)(2,1)} fusion(bf16[2048,2048]{1,0:T(8,128)(2,1)} %get-tuple-element.74, bf16[2048,2048]{1,0:T(8,128)(2,1)} %get-tuple-element.118.refs_2_), kind=kOutput, calls=%fused_computation.13 | convolution fusion | flops 17184063488 | bytes 25165824 | tf_op jit(solution)/shard_map/dot_general | solution.py:441
  290.0 24.2 %convolution_convert_fusion = bf16[2048,2048]{1,0:T(8,128)(2,1)} fusion(bf16[2048,2048]{1,0:T(8,128)(2,1)} %get-tuple-element.65.refs_0_, bf16[2048,2048]{1,0:T(8,128)(2,1)} %join_rows.1), kind=kOutput, calls=%fused_computation.12 | convolution fusion | flops 17184063488 | bytes 25165824 | tf_op jit(solution)/shard_map/dot_general | solution.py:441
  321.0 19.4 %convolution_add_fusion.qkv_ref = f32[2048,1536]{1,0:T(8,128)} fusion(bf16[2048,2048]{1,0:T(8,128)(2,1)} %get-tuple-element.74, bf16[2048,1536]{1,0:T(8,128)(2,1)} %all-gather.11.cloned.1.call-done.refs_1_, f32[1536]{0:T(1024)S(1)} %copy-done.28), kind=kOutput, calls=%fused_computation.10 | convolution fusion | flops 12888047616 | bytes 27269120 | tf_op jit(solution)/shard_map/dot_general | solution.py:433
  340.4 72.8 %attention.1 = (bf16[2048,512]{1,0:T(8,128)(2,1)}, bf16[2048,1536]{1,0:T(8,128)(2,1)}) custom-call(s32[16]{0:T(128)S(1)} %copy-done.8, s32[16]{0:T(128)S(1)} %copy-done.10, s32[16]{0:T(128)S(1)} %and_select_fusion.low_ref, f32[2048,1536]{1,0:T(8,128)} %convolution_add_fusion.qkv_ref, bf16[2048,512]{1,0:T(8,128)(2,1)} %convolution_convert_fusion.4.cot_ref, ...), custom_call_target="tpu_custom_call" | custom-call | flops 1073741824 | bytes 3145728 | tf_op jit(solution)/shard_map/attention/pallas_call | solution.py:229
  416.9 10.3 %product_nn.3 = bf16[512,2048]{1,0:T(8,128)(2,1)} custom-call(bf16[2048,2048]{1,0:T(8,128)(2,1)} %get-tuple-element.65.refs_0_, bf16[2048,2048]{1,0:T(8,128)(2,1)} %all-gather.9.cloned.1.call-done.refs_1_, bf16[2048,512]{1,0:T(8,128)(2,1)} %get-tuple-element.76.refs_2_, bf16[512,2048]{1,0:T(8,128)(2,1)} %all-gather.5.cloned.1.call-done.refs_3_), custom_call_target="tpu_custom_call" | custom-call | flops 26843545600 | bytes 1048576 | tf_op jit(solution)/shard_map/product_nn/pallas_call | solution.py:495
  437.3 10.2 %product_nn.4 = bf16[512,2048]{1,0:T(8,128)(2,1)} custom-call(bf16[2048,2048]{1,0:T(8,128)(2,1)} %get-tuple-element.65.refs_0_, bf16[2048,2048]{1,0:T(8,128)(2,1)} %all-gather.9.cloned.1.call-done.refs_1_, bf16[2048,512]{1,0:T(8,128)(2,1)} %get-tuple-element.76.refs_2_, bf16[512,2048]{1,0:T(8,128)(2,1)} %all-gather.5.cloned.1.call-done.refs_3_), custom_call_target="tpu_custom_call" | custom-call | flops 26843545600 | bytes 1048576 | tf_op jit(solution)/shard_map/product_nn/pallas_call | solution.py:495
  449.0 9.2 %convolution_convert_fusion.3 = bf16[512,2048]{1,0:T(8,128)(2,1)} fusion(bf16[2048,512]{1,0:T(8,128)(2,1)S(1)} %copy-done.38, bf16[2048,2048]{1,0:T(8,128)(2,1)} %join_rows.1), kind=kOutput, calls=%fused_computation.41 | convolution fusion | flops 4296015872 | bytes 12582912 | tf_op jit(solution)/shard_map/dot_general | solution.py:441
  458.2 19.2 %convolution_convert_fusion.2 = bf16[2048,1536]{1,0:T(8,128)(2,1)} fusion(bf16[2048,2048]{1,0:T(8,128)(2,1)} %get-tuple-element.74, bf16[2048,1536]{1,0:T(8,128)(2,1)} %get-tuple-element.78.refs_0_), kind=kOutput, calls=%fused_computation.14 | convolution fusion | flops 12888047616 | bytes 20971520 | tf_op jit(solution)/shard_map/dot_general | solution.py:441
  477.5 17.7 %product_nn.5 = f32[1024,2048]{1,0:T(8,128)} custom-call(bf16[2048,2048]{1,0:T(8,128)(2,1)} %get-tuple-element.65.refs_0_, bf16[2048,2048]{1,0:T(8,128)(2,1)} %all-gather.9.cloned.1.call-done.refs_1_, bf16[2048,512]{1,0:T(8,128)(2,1)} %get-tuple-element.76.refs_2_, bf16[512,2048]{1,0:T(8,128)(2,1)} %all-gather.5.cloned.1.call-done.refs_3_), custom_call_target="tpu_custom_call" | custom-call | flops 53687091200 | bytes 2097152 | tf_op jit(solution)/shard_map/product_nn/pallas_call | solution.py:495
  495.2 13.3 %product_nt.3 = bf16[512,2048]{1,0:T(8,128)(2,1)} custom-call(bf16[2048,1536]{1,0:T(8,128)(2,1)} %get-tuple-element.78.refs_0_, bf16[2048,1536]{1,0:T(8,128)(2,1)} %all-gather.11.cloned.1.call-done.refs_1_, bf16[2048,2048]{1,0:T(8,128)(2,1)} %get-tuple-element.118.refs_2_, bf16[2048,2048]{1,0:T(8,128)(2,1)} %all-gather.7.cloned.1.call-done.refs_3_), custom_call_target="tpu_custom_call" | custom-call | flops 37580963840 | bytes 1048576 | tf_op jit(solution)/shard_map/product_nt/pallas_call | solution.py:495
  509.0 13.4 %product_nt.4 = bf16[512,2048]{1,0:T(8,128)(2,1)} custom-call(bf16[2048,1536]{1,0:T(8,128)(2,1)} %get-tuple-element.78.refs_0_, bf16[2048,1536]{1,0:T(8,128)(2,1)} %all-gather.11.cloned.1.call-done.refs_1_, bf16[2048,2048]{1,0:T(8,128)(2,1)} %get-tuple-element.118.refs_2_, bf16[2048,2048]{1,0:T(8,128)(2,1)} %all-gather.7.cloned.1.call-done.refs_3_), custom_call_target="tpu_custom_call" | custom-call | flops 37580963840 | bytes 1048576 | tf_op jit(solution)/shard_map/product_nt/pallas_call | solution.py:495
  526.9 23.2 %product_nt.5 = f32[1024,2048]{1,0:T(8,128)} custom-call(bf16[2048,1536]{1,0:T(8,128)(2,1)} %get-tuple-element.78.refs_0_, bf16[2048,1536]{1,0:T(8,128)(2,1)} %all-gather.11.cloned.1.call-done.refs_1_, bf16[2048,2048]{1,0:T(8,128)(2,1)} %get-tuple-element.118.refs_2_, bf16[2048,2048]{1,0:T(8,128)(2,1)} %all-gather.7.cloned.1.call-done.refs_3_), custom_call_target="tpu_custom_call" | custom-call | flops 75161927680 | bytes 2097152 | tf_op jit(solution)/shard_map/product_nt/pallas_call | solution.py:495
  571.2 22.6 %collective-permute-done.11 = bf16[256,2048]{1,0:T(8,128)(2,1)} collective-permute-done((bf16[256,2048]{1,0:T(8,128)(2,1)}, bf16[256,2048]{1,0:T(8,128)(2,1)}, u32[]{:S(2)}, u32[]{:S(2)}) %collective-permute-start.11) | collective-permute-done | bytes 1048608 | tf_op jit(solution)/shard_map/ppermute | solution.py:346
  602.9 7.2 %all-to-all-start.4 = ((f32[32,1,640]{2,1,0:T(1,128)}), f32[32,1,640]{2,1,0:T(1,128)S(1)}, u32[]{:S(2)}, u32[]{:S(2)}) async-start(f32[32,1,640]{2,1,0:T(1,128)} %all_to_all.29), calls=%async_computation.6 | async-start | bytes 163840 | tf_op jit(solution)/shard_map/all_to_all | solution.py:709
  634.5 11.8 %collective-permute-done.9 = bf16[256,2048]{1,0:T(8,128)(2,1)} collective-permute-done((bf16[256,2048]{1,0:T(8,128)(2,1)}, bf16[256,2048]{1,0:T(8,128)(2,1)}, u32[]{:S(2)}, u32[]{:S(2)}) %collective-permute-start.9) | collective-permute-done | bytes 1048608 | tf_op jit(solution)/shard_map/ppermute | solution.py:346
  (233 shorter events, 135.0 us)
Async XLA Ops:
  7.3 168.8 %all-gather.5.cloned.1.call-start = ((), (), s32[]{:S(2)}) async-start(), calls=%async_computation.10 | async-start | bytes 2359296 | tf_op jit(solution)/shard_map/all_gather | solution.py:421
  8.0 168.1 %all-gather.7.cloned.1.call-start = ((), (), s32[]{:S(2)}) async-start(), calls=%async_computation.11 | async-start | bytes 9437184 | tf_op jit(solution)/shard_map/all_gather | solution.py:421
  30.3 210.0 %all-gather.9.cloned.1.call-start = ((), (), s32[]{:S(2)}) async-start(), calls=%async_computation.12 | async-start | bytes 9437184 | tf_op jit(solution)/shard_map/all_gather | solution.py:421
  31.1 48.4 %collective-permute-start.1 = (bf16[512,2048]{1,0:T(8,128)(2,1)S(1)}, bf16[512,2048]{1,0:T(8,128)(2,1)}, u32[]{:S(2)}, u32[]{:S(2)}) collective-permute-start(bf16[512,2048]{1,0:T(8,128)(2,1)S(1)} %bitcast.53), channel_id=1, source_target_pairs={{0,2},{1,3},{2,0},{3,1},{4,6},{5,7},{6,4},{7,5},{8,10},{9,11},{10,... | collective-permute-start | bytes 6291464 | tf_op jit(solution)/shard_map/ppermute | solution.py:346
  32.1 47.4 %collective-permute-start = (bf16[512,2048]{1,0:T(8,128)(2,1)S(1)}, bf16[512,2048]{1,0:T(8,128)(2,1)}, u32[]{:S(2)}, u32[]{:S(2)}) collective-permute-start(bf16[512,2048]{1,0:T(8,128)(2,1)S(1)} %bitcast.54), channel_id=1, source_target_pairs={{0,1},{1,0},{2,3},{3,2},{4,5},{5,4},{6,7},{7,6},{8,9},{9,8},{10,11... | collective-permute-start | bytes 6291464 | tf_op jit(solution)/shard_map/ppermute | solution.py:346
  34.7 44.6 %all-to-all-start = ((bf16[32,2,352]{2,1,0:T(2,128)(2,1)}), bf16[32,2,352]{2,1,0:T(2,128)(2,1)S(1)}, u32[]{:S(2)}, u32[]{:S(2)}) async-start(bf16[32,2,352]{2,1,0:T(2,128)(2,1)} %reshape.321), calls=%async_computation | async-start | bytes 98304 | tf_op jit(solution)/shard_map/all_to_all | solution.py:417
  40.6 280.4 %all-gather.11.cloned.1.call-start = ((), (), s32[]{:S(2)}) async-start(), calls=%async_computation.13 | async-start | bytes 7077888 | tf_op jit(solution)/shard_map/all_gather | solution.py:421
  85.5 70.6 %collective-permute-start.3 = (bf16[768,2048]{1,0:T(8,128)(2,1)}, bf16[768,2048]{1,0:T(8,128)(2,1)}, u32[]{:S(2)}, u32[]{:S(2)}) collective-permute-start(bf16[768,2048]{1,0:T(8,128)(2,1)} %get-tuple-element.106), channel_id=1, source_target_pairs={{0,1},{1,0},{2,3},{3,2},{4,5},{5,4},{6,7},{7,6},{8,9},{9,8},{10,11... | collective-permute-start | bytes 9437192 | tf_op jit(solution)/shard_map/ppermute | solution.py:346
  86.8 72.9 %collective-permute-start.2 = (bf16[768,2048]{1,0:T(8,128)(2,1)}, bf16[768,2048]{1,0:T(8,128)(2,1)}, u32[]{:S(2)}, u32[]{:S(2)}) collective-permute-start(bf16[768,2048]{1,0:T(8,128)(2,1)} %get-tuple-element.107), channel_id=1, source_target_pairs={{0,2},{1,3},{2,0},{3,1},{4,6},{5,7},{6,4},{7,5},{8,10},{9,11},{10,... | collective-permute-start | bytes 9437192 | tf_op jit(solution)/shard_map/ppermute | solution.py:346
  158.4 50.2 %collective-permute-start.4 = (bf16[256,2048]{1,0:T(8,128)(2,1)}, bf16[256,2048]{1,0:T(8,128)(2,1)}, u32[]{:S(2)}, u32[]{:S(2)}) collective-permute-start(bf16[256,2048]{1,0:T(8,128)(2,1)} %slice.106), channel_id=1, source_target_pairs={{0,2},{1,3},{2,0},{3,1},{4,6},{5,7},{6,4},{7,5},{8,10},{9,11},{10,... | collective-permute-start | bytes 3145736 | tf_op jit(solution)/shard_map/ppermute | solution.py:346
  161.9 46.6 %collective-permute-start.5 = (bf16[256,2048]{1,0:T(8,128)(2,1)}, bf16[256,2048]{1,0:T(8,128)(2,1)}, u32[]{:S(2)}, u32[]{:S(2)}) collective-permute-start(bf16[256,2048]{1,0:T(8,128)(2,1)} %slice.107), channel_id=1, source_target_pairs={{0,1},{1,0},{2,3},{3,2},{4,5},{5,4},{6,7},{7,6},{8,9},{9,8},{10,11... | collective-permute-start | bytes 3145736 | tf_op jit(solution)/shard_map/ppermute | solution.py:346
  230.4 182.9 %reduce-scatter.5.cloned.1.call-start = ((), (), s32[]{:S(2)}) async-start(), calls=%async_computation.14 | async-start | bytes 9437184 | tf_op jit(solution)/shard_map/reduce_scatter | solution.py:425
  290.0 269.4 %reduce-scatter.7.cloned.1.call-start = ((), (), s32[]{:S(2)}) async-start(), calls=%async_computation.15 | async-start | bytes 9437184 | tf_op jit(solution)/shard_map/reduce_scatter | solution.py:425
  413.3 20.4 %all-to-all-start.3 = ((bf16[4,64,2048]{2,1,0:T(8,128)(2,1)}), bf16[4,64,2048]{2,1,0:T(8,128)(2,1)S(1)}, u32[]{:S(2)}, u32[]{:S(2)}) async-start(bf16[4,64,2048]{2,1,0:T(8,128)(2,1)} %bitcast.61), calls=%async_computation.4 | async-start | bytes 2097152 | tf_op jit(solution)/shard_map/all_to_all | solution.py:429
  416.8 202.8 %reduce-scatter.11.cloned.1.call-start = ((), (), s32[]{:S(2)}) async-start(), calls=%async_computation.17 | async-start | bytes 2359296 | tf_op jit(solution)/shard_map/reduce_scatter | solution.py:425
  431.8 95.1 %collective-permute-start.6 = (bf16[512,2048]{1,0:T(8,128)(2,1)}, bf16[512,2048]{1,0:T(8,128)(2,1)}, u32[]{:S(2)}, u32[]{:S(2)}) collective-permute-start(bf16[512,2048]{1,0:T(8,128)(2,1)} %product_nn.3), channel_id=1, source_target_pairs={{0,2},{1,3},{2,0},{3,1},{4,6},{5,7},{6,4},{7,5},{8,10},{9,11},{10,... | collective-permute-start | bytes 6291464 | tf_op jit(solution)/shard_map/ppermute | solution.py:346
  447.5 79.4 %collective-permute-start.7 = (bf16[512,2048]{1,0:T(8,128)(2,1)}, bf16[512,2048]{1,0:T(8,128)(2,1)}, u32[]{:S(2)}, u32[]{:S(2)}) collective-permute-start(bf16[512,2048]{1,0:T(8,128)(2,1)} %product_nn.4), channel_id=1, source_target_pairs={{0,1},{1,0},{2,3},{3,2},{4,5},{5,4},{6,7},{7,6},{8,9},{9,8},{10,11... | collective-permute-start | bytes 6291464 | tf_op jit(solution)/shard_map/ppermute | solution.py:346
  477.5 153.4 %reduce-scatter.9.cloned.1.call-start = ((), (), s32[]{:S(2)}) async-start(), calls=%async_computation.16 | async-start | bytes 7077888 | tf_op jit(solution)/shard_map/reduce_scatter | solution.py:425
  508.5 41.6 %collective-permute-start.10 = (bf16[512,2048]{1,0:T(8,128)(2,1)}, bf16[512,2048]{1,0:T(8,128)(2,1)S(1)}, u32[]{:S(2)}, u32[]{:S(2)}) collective-permute-start(bf16[512,2048]{1,0:T(8,128)(2,1)} %product_nt.3), channel_id=1, source_target_pairs={{0,2},{1,3},{2,0},{3,1},{4,6},{5,7},{6,4},{7,5},{8,10},{9,11},{10,... | collective-permute-start | bytes 6291464 | tf_op jit(solution)/shard_map/ppermute | solution.py:346
  522.4 48.8 %collective-permute-start.12 = (bf16[512,2048]{1,0:T(8,128)(2,1)}, bf16[512,2048]{1,0:T(8,128)(2,1)S(1)}, u32[]{:S(2)}, u32[]{:S(2)}) collective-permute-start(bf16[512,2048]{1,0:T(8,128)(2,1)} %product_nt.4), channel_id=1, source_target_pairs={{0,1},{1,0},{2,3},{3,2},{4,5},{5,4},{6,7},{7,6},{8,9},{9,8},{10,11... | collective-permute-start | bytes 6291464 | tf_op jit(solution)/shard_map/ppermute | solution.py:346
  554.4 39.4 %collective-permute-start.11 = (bf16[256,2048]{1,0:T(8,128)(2,1)}, bf16[256,2048]{1,0:T(8,128)(2,1)}, u32[]{:S(2)}, u32[]{:S(2)}) collective-permute-start(bf16[256,2048]{1,0:T(8,128)(2,1)} %fusion.18), channel_id=1, source_target_pairs={{0,1},{1,0},{2,3},{3,2},{4,5},{5,4},{6,7},{7,6},{8,9},{9,8},{10,11... | collective-permute-start | bytes 3145736 | tf_op jit(solution)/shard_map/ppermute | solution.py:346
  559.4 50.8 %collective-permute-start.8 = (bf16[256,2048]{1,0:T(8,128)(2,1)}, bf16[256,2048]{1,0:T(8,128)(2,1)}, u32[]{:S(2)}, u32[]{:S(2)}) collective-permute-start(bf16[256,2048]{1,0:T(8,128)(2,1)} %add_convert_fusion.1), channel_id=1, source_target_pairs={{0,1},{1,0},{2,3},{3,2},{4,5},{5,4},{6,7},{7,6},{8,9},{9,8},{10,11... | collective-permute-start | bytes 3145736 | tf_op jit(solution)/shard_map/ppermute | solution.py:346
  599.1 22.3 %collective-permute-start.13 = (bf16[256,2048]{1,0:T(8,128)(2,1)}, bf16[256,2048]{1,0:T(8,128)(2,1)}, u32[]{:S(2)}, u32[]{:S(2)}) collective-permute-start(bf16[256,2048]{1,0:T(8,128)(2,1)} %get-tuple-element.103), channel_id=1, source_target_pairs={{0,2},{1,3},{2,0},{3,1},{4,6},{5,7},{6,4},{7,5},{8,10},{9,11},{10,... | collective-permute-start | bytes 3145736 | tf_op jit(solution)/shard_map/ppermute | solution.py:346
  615.8 30.5 %collective-permute-start.9 = (bf16[256,2048]{1,0:T(8,128)(2,1)}, bf16[256,2048]{1,0:T(8,128)(2,1)}, u32[]{:S(2)}, u32[]{:S(2)}) collective-permute-start(bf16[256,2048]{1,0:T(8,128)(2,1)} %get-tuple-element.105), channel_id=1, source_target_pairs={{0,2},{1,3},{2,0},{3,1},{4,6},{5,7},{6,4},{7,5},{8,10},{9,11},{10,... | collective-permute-start | bytes 3145736 | tf_op jit(solution)/shard_map/ppermute | solution.py:346
  (41 other events, 742.1 us)
Sparse Core Ops, SparseCore 0:
  9.7 31.7 all-gather.4
  43.1 81.5 all-gather.6
  126.3 80.5 all-gather.8
  230.5 64.4 all-gather.10
  297.2 88.2 reduce-scatter.4
  387.6 87.9 reduce-scatter.6
  477.9 39.2 reduce-scatter.10
  519.5 68.4 reduce-scatter.8

commit v7 on v6

--- a/solution.py
+++ b/solution.py
@@ -398,15 +398,15 @@
     return tuple(exchange(x.astype(BF), "ctx", size, j) for x, j in zip(pieces, distances))
 
 
-def sum_end(own, arrived, size):
+def sum_end(own, arrived, size, together=False):
     if size != 4:
         return sum([x.astype(F32) for x in arrived], own), arrived, arrived
     half = own.shape[0] // 4
     far, near = arrived
     top = (own[2 * half : 3 * half] + far[half:].astype(F32)).astype(BF)
     low = (own[3 * half :] + near[half:].astype(F32)).astype(BF)
-    sent = (top, low)
-    last = (exchange(top, "ctx", size, 1), exchange(low, "ctx", size, 2))
+    sent = lax.optimization_barrier((top, low)) if together else (top, low)
+    last = (exchange(sent[0], "ctx", size, 1), exchange(sent[1], "ctx", size, 2))
     top = own[:half] + far[:half].astype(F32) + last[0].astype(F32)
     low = own[half : 2 * half] + near[:half].astype(F32) + last[1].astype(F32)
     return jnp.concatenate([top, low], axis=0), last, sent
@@ -585,8 +585,9 @@
         everything = everything.reshape(own_heads, C, HEAD, width)
         w_out_own = lax.dynamic_index_in_dim(everything, c, 1, keepdims=False)
         w_out_own = w_out_own.reshape(own_heads * HEAD, width)
-    up_rows = swap_ctx(deal_columns((w_up,), (up_chunks,))).reshape(C * row_block, -1)
-    qkv_send = deal_columns((w_qkv,), (qkv_chunks,))
+    both_rows = swap_ctx(deal_columns((w_up, w_qkv), (up_chunks, qkv_chunks)))
+    both_rows = both_rows.reshape(C * row_block, -1)
+    up_rows, qkv_rows = both_rows[:, :own_ff], both_rows[:, own_ff:]
     w_up_own = gather_dp(up_rows)
 
     half_block = jnp.array([j for j, _ in half_blocks(C)], jnp.int32) ^ c
@@ -627,7 +628,6 @@
         for key in ((3, 0), (3, 1)):
             grad_parts[key] = (after(grad_parts[key][0], active), grad_parts[key][1])
     grad_all = join_blocks(grad_parts, half_blocks(C), step)
-    qkv_rows = swap_ctx(after(qkv_send, grad_all)).reshape(C * row_block, -1)
     w_qkv_own = gather_dp(qkv_rows)
     d_attended = matmul_t(grad_all, w_out_own).astype(BF)
 
@@ -704,12 +704,12 @@
     qkv_bias_grad = jnp.where(mine[None, None, None, :, None], qkv_bias_grad, 0.0)
     small = [gain_grad, shift_grad, qkv_bias_grad, bias_grad, up_bias_grad]
     small = jnp.concatenate([s.reshape(devices, -1) for s in small], axis=1)
-    d_normed, _, d_sent = sum_end(d_near, d_arrived, C)
+    d_normed, _, d_sent = sum_end(d_near, d_arrived, C, True)
     small = after(small, *d_sent)
     small = lax.all_to_all(small, ALL, split_axis=0, concat_axis=0, tiled=True)
     small = jnp.split(jnp.sum(small, axis=0), cuts[:4])
 
-    d_normed = after(d_normed, down_rows, *small)
+    d_normed = after(d_normed, down_rows, qkv_grad, *small)
     xhat, scale = standardise(hidden_own.astype(F32))
     e = d_normed * gain
     d_hidden = e - jnp.mean(e, axis=-1, keepdims=True)

time: 675 us -> 677 us (level)
  waiting for transfers between devices: 132 us -> 148 us
    all_to_all x1, waiting for transfers between devices: 0.13 us -> 24.3 us  [on_device(): small = lax.all_to_all(small, ALL, split_axis=0, concat_axis=0, tiled=True)]
    ppermute x14, waiting for transfers between devices: 96.5 us -> 80.9 us  [exchange(): return lax.ppermute(value, axis, [(i, i ^ offset) for i in range(size)])]
    all_to_all x2 -> x1, blocking collectives: 33.6 us -> 27.9 us  [swap_ctx(): return lax.all_to_all(value, 'ctx', split_axis=0, concat_axis=0, tiled=True)]
  transfers between devices with their start and end apart: 26 -> 26, of which waited for: 6 -> 6; matrix products, arithmetic and copies ran while one was open for 38% -> 37% of each run, Pallas kernels for 29% -> 27%
where the time goes in v7:
time: 677 us; the launch traced here: 669 us
  Pallas kernels  186 us (27%)
  matrix products  163 us (24%)
  waiting for transfers between devices  148 us (22%)
  other arithmetic  69.2 us (10%)
  starting transfers between devices  34.5 us (5%)
  blocking collectives  27.9 us (4%)
  local copies, waits for them, and re-layouts  24 us (4%)
  between operations  15.3 us (2%)
    pallas_call x6, Pallas kernels, product(): pl.pallas_call(kernel, grid=(columns // wide, (high - low) // tall), in_s...  87.4 us
    ppermute x14, waiting for transfers between devices, exchange(): return lax.ppermute(value, axis, [(i, i ^ offset) for i in range(size)])  80.9 us
    dot_general x4, matrix products, outer(): lax.dot_general(a, b, (((0,), (0,)), ((), ())), preferred_element_type=F32)  76.3 us
    pallas_call x1, Pallas kernels, attention(): pl.pallas_call(attention_kernel, out_shape=[jax.ShapeDtypeStruct((slots,...  68.5 us
    dot_general x2, matrix products, matmul(): return jnp.dot(a, b, preferred_element_type=F32)  51.9 us
    all_to_all x1, waiting for transfers between devices, gather_small(): return lax.all_to_all(copies, ALL, split_axis=0, concat_axis=0, tiled=True)  36.2 us
    dot_general x2, matrix products, matmul_t(): lax.dot_general(a, b, (((1,), (1,)), ((), ())), preferred_element_type=F32)  35 us
    all_to_all x1, blocking collectives, swap_ctx(): return lax.all_to_all(value, 'ctx', split_axis=0, concat_axis=0, tiled=True)  27.9 us
  transfers between devices with their start and end apart: 26, of which 6 were waited for; matrix products, arithmetic and copies ran while one was open for 37% of the time, Pallas kernels for 27%

profile of v7, /device:TPU:0, one launch (start us, length us, event | category | flops | bytes accessed | tf_op | source)
XLA Modules:
  0.0 668.7 jit_solution(15962771593211775472)
XLA Ops:
  11.1 27.9 %all_to_all.33 = bf16[4,64,3584]{2,1,0:T(8,128)(2,1)S(1)} all-to-all(bf16[4,64,3584]{2,1,0:T(8,128)(2,1)} %deal_columns.1), channel_id=1, replica_groups=mesh['dp'=8,'ctx'=4] {'ctx'}, dimensions={0} | all-to-all | bytes 3670016 | tf_op jit(solution)/shard_map/all_to_all | solution.py:429
  53.5 36.2 %all-to-all-done = bf16[32,2,352]{2,1,0:T(2,128)(2,1)S(1)} async-done(((bf16[32,2,352]{2,1,0:T(2,128)(2,1)}), bf16[32,2,352]{2,1,0:T(2,128)(2,1)S(1)}, u32[]{:S(2)}, u32[]{:S(2)}) %all-to-all-start) | async-done | bytes 45088 | tf_op jit(solution)/shard_map/all_to_all | solution.py:417
  112.6 53.8 %collective-permute-done.3.refs_4_.refs_1_ = bf16[768,2048]{1,0:T(8,128)(2,1)} collective-permute-done((bf16[768,2048]{1,0:T(8,128)(2,1)}, bf16[768,2048]{1,0:T(8,128)(2,1)}, u32[]{:S(2)}, u32[]{:S(2)}) %collective-permute-start.3) | collective-permute-done | bytes 3145760 | tf_op jit(solution)/shard_map/ppermute | solution.py:346
  172.9 13.8 %norm_rows.1 = (bf16[2048,2048]{1,0:T(8,128)(2,1)}, bf16[2048,2048]{1,0:T(8,128)(2,1)}) custom-call(bf16[512,2048]{1,0:T(8,128)(2,1)S(1)} %bitcast.54, bf16[512,2048]{1,0:T(8,128)(2,1)} %collective-permute-done.refs_1_, bf16[512,2048]{1,0:T(8,128)(2,1)} %collective-permute-done.1.refs_2_, bf16[768,2048]{1,0:T(8,128)(2,1)} %collective-permute-done.2.refs_3_.refs_2_, ...), custom_call_target="tpu_custom_call" | custom-call | flops 41943040 | bytes 16777216 | tf_op jit(solution)/shard_map/norm_rows/pallas_call | solution.py:276
  186.8 32.5 %multiply_add_fusion = (f32[2048,2048]{1,0:T(8,128)}, bf16[2048,2048]{1,0:T(8,128)(2,1)}) fusion(f32[2048]{0:T(1024)S(1)} %bitcast.71, bf16[2048,2048]{1,0:T(8,128)(2,1)} %get-tuple-element.74, bf16[2048,2048]{1,0:T(8,128)(2,1)} %all-gather.7.cloned.1.call-done.refs_3_), kind=kOutput, calls=%fused_computation.5 | convolution fusion | flops 17242783744 | bytes 41951232 | tf_op jit(solution)/shard_map/dot_general | solution.py:433
  219.3 8.3 %join_rows.1 = bf16[2048,2048]{1,0:T(8,128)(2,1)} custom-call(bf16[512,2048]{1,0:T(8,128)(2,1)S(1)} %bitcast.56, bf16[768,2048]{1,0:T(8,128)(2,1)} %collective-permute-done.3.refs_4_.refs_1_, bf16[768,2048]{1,0:T(8,128)(2,1)} %collective-permute-done.2.refs_3_.refs_2_, bf16[256,2048]{1,0:T(8,128)(2,1)} %collective-permute-done.4.refs_3_, ...), custom_call_target="tpu_custom_call" | custom-call | flops 41943040 | bytes 16777216 | tf_op jit(solution)/shard_map/join_rows/pallas_call | solution.py:276
  227.6 9.2 %convolution_convert_fusion.4.cot_ref = bf16[2048,512]{1,0:T(8,128)(2,1)} fusion(bf16[2048,2048]{1,0:T(8,128)(2,1)} %join_rows.1, bf16[512,2048]{1,0:T(8,128)(2,1)S(1)} %copy-done.38), kind=kOutput, calls=%fused_computation.42 | convolution fusion | flops 4296015872 | bytes 12582912 | tf_op jit(solution)/shard_map/dot_general | solution.py:437
  236.8 25.8 %convert_reduce_fusion = (f32[2048]{0:T(1024)S(1)}, bf16[2048,2048]{1,0:T(8,128)(2,1)}) fusion(f32[2048,2048]{1,0:T(8,128)} %get-tuple-element.65, bf16[2048,2048]{1,0:T(8,128)(2,1)} %join_rows.1, bf16[2048,2048]{1,0:T(8,128)(2,1)} %all-gather.9.cloned.1.call-done.refs_1_), kind=kOutput, calls=%fused_computation.3 | convolution fusion | flops 17196644352 | bytes 41951232 | tf_op jit(solution)/shard_map/dot_general | solution.py:437
  262.6 23.9 %convolution_convert_fusion.1 = bf16[2048,2048]{1,0:T(8,128)(2,1)} fusion(bf16[2048,2048]{1,0:T(8,128)(2,1)} %get-tuple-element.74, bf16[2048,2048]{1,0:T(8,128)(2,1)} %get-tuple-element.122.refs_2_), kind=kOutput, calls=%fused_computation.13 | convolution fusion | flops 17184063488 | bytes 25165824 | tf_op jit(solution)/shard_map/dot_general | solution.py:441
  286.6 24.0 %convolution_convert_fusion = bf16[2048,2048]{1,0:T(8,128)(2,1)} fusion(bf16[2048,2048]{1,0:T(8,128)(2,1)} %get-tuple-element.66.refs_0_, bf16[2048,2048]{1,0:T(8,128)(2,1)} %join_rows.1), kind=kOutput, calls=%fused_computation.12 | convolution fusion | flops 17184063488 | bytes 25165824 | tf_op jit(solution)/shard_map/dot_general | solution.py:441
  315.3 19.4 %convolution_add_fusion.qkv_ref = f32[2048,1536]{1,0:T(8,128)} fusion(bf16[2048,2048]{1,0:T(8,128)(2,1)} %get-tuple-element.74, bf16[2048,1536]{1,0:T(8,128)(2,1)} %all-gather.11.cloned.1.call-done.refs_1_, f32[1536]{0:T(1024)S(1)} %copy-done.28), kind=kOutput, calls=%fused_computation.10 | convolution fusion | flops 12888047616 | bytes 27269120 | tf_op jit(solution)/shard_map/dot_general | solution.py:433
  334.7 68.5 %attention.1 = (bf16[2048,512]{1,0:T(8,128)(2,1)}, bf16[2048,1536]{1,0:T(8,128)(2,1)}) custom-call(s32[16]{0:T(128)S(1)} %copy-done.8, s32[16]{0:T(128)S(1)} %copy-done.10, s32[16]{0:T(128)S(1)} %and_select_fusion.low_ref, f32[2048,1536]{1,0:T(8,128)} %convolution_add_fusion.qkv_ref, bf16[2048,512]{1,0:T(8,128)(2,1)} %convolution_convert_fusion.4.cot_ref, ...), custom_call_target="tpu_custom_call" | custom-call | flops 1073741824 | bytes 3145728 | tf_op jit(solution)/shard_map/attention/pallas_call | solution.py:229
  403.1 10.1 %product_nn.3 = bf16[512,2048]{1,0:T(8,128)(2,1)} custom-call(bf16[2048,2048]{1,0:T(8,128)(2,1)} %get-tuple-element.66.refs_0_, bf16[2048,2048]{1,0:T(8,128)(2,1)} %all-gather.9.cloned.1.call-done.refs_1_, bf16[2048,512]{1,0:T(8,128)(2,1)} %get-tuple-element.76.refs_2_, bf16[512,2048]{1,0:T(8,128)(2,1)} %all-gather.5.cloned.1.call-done.refs_3_), custom_call_target="tpu_custom_call" | custom-call | flops 26843545600 | bytes 1048576 | tf_op jit(solution)/shard_map/product_nn/pallas_call | solution.py:495
  433.3 10.1 %product_nn.4 = bf16[512,2048]{1,0:T(8,128)(2,1)} custom-call(bf16[2048,2048]{1,0:T(8,128)(2,1)} %get-tuple-element.66.refs_0_, bf16[2048,2048]{1,0:T(8,128)(2,1)} %all-gather.9.cloned.1.call-done.refs_1_, bf16[2048,512]{1,0:T(8,128)(2,1)} %get-tuple-element.76.refs_2_, bf16[512,2048]{1,0:T(8,128)(2,1)} %all-gather.5.cloned.1.call-done.refs_3_), custom_call_target="tpu_custom_call" | custom-call | flops 26843545600 | bytes 1048576 | tf_op jit(solution)/shard_map/product_nn/pallas_call | solution.py:495
  445.7 9.2 %convolution_convert_fusion.3 = bf16[512,2048]{1,0:T(8,128)(2,1)} fusion(bf16[2048,512]{1,0:T(8,128)(2,1)S(1)} %copy-done.39, bf16[2048,2048]{1,0:T(8,128)(2,1)} %join_rows.1), kind=kOutput, calls=%fused_computation.41 | convolution fusion | flops 4296015872 | bytes 12582912 | tf_op jit(solution)/shard_map/dot_general | solution.py:441
  454.9 19.2 %convolution_convert_fusion.2 = bf16[2048,1536]{1,0:T(8,128)(2,1)} fusion(bf16[2048,2048]{1,0:T(8,128)(2,1)} %get-tuple-element.74, bf16[2048,1536]{1,0:T(8,128)(2,1)} %get-tuple-element.78.refs_0_), kind=kOutput, calls=%fused_computation.14 | convolution fusion | flops 12888047616 | bytes 20971520 | tf_op jit(solution)/shard_map/dot_general | solution.py:441
  474.4 17.3 %product_nn.5 = f32[1024,2048]{1,0:T(8,128)} custom-call(bf16[2048,2048]{1,0:T(8,128)(2,1)} %get-tuple-element.66.refs_0_, bf16[2048,2048]{1,0:T(8,128)(2,1)} %all-gather.9.cloned.1.call-done.refs_1_, bf16[2048,512]{1,0:T(8,128)(2,1)} %get-tuple-element.76.refs_2_, bf16[512,2048]{1,0:T(8,128)(2,1)} %all-gather.5.cloned.1.call-done.refs_3_), custom_call_target="tpu_custom_call" | custom-call | flops 53687091200 | bytes 2097152 | tf_op jit(solution)/shard_map/product_nn/pallas_call | solution.py:495
  491.7 13.3 %product_nt.3 = bf16[512,2048]{1,0:T(8,128)(2,1)} custom-call(bf16[2048,1536]{1,0:T(8,128)(2,1)} %get-tuple-element.78.refs_0_, bf16[2048,1536]{1,0:T(8,128)(2,1)} %all-gather.11.cloned.1.call-done.refs_1_, bf16[2048,2048]{1,0:T(8,128)(2,1)} %get-tuple-element.122.refs_2_, bf16[2048,2048]{1,0:T(8,128)(2,1)} %all-gather.7.cloned.1.call-done.refs_3_), custom_call_target="tpu_custom_call" | custom-call | flops 37580963840 | bytes 1048576 | tf_op jit(solution)/shard_map/product_nt/pallas_call | solution.py:495
  505.0 13.4 %product_nt.4 = bf16[512,2048]{1,0:T(8,128)(2,1)} custom-call(bf16[2048,1536]{1,0:T(8,128)(2,1)} %get-tuple-element.78.refs_0_, bf16[2048,1536]{1,0:T(8,128)(2,1)} %all-gather.11.cloned.1.call-done.refs_1_, bf16[2048,2048]{1,0:T(8,128)(2,1)} %get-tuple-element.122.refs_2_, bf16[2048,2048]{1,0:T(8,128)(2,1)} %all-gather.7.cloned.1.call-done.refs_3_), custom_call_target="tpu_custom_call" | custom-call | flops 37580963840 | bytes 1048576 | tf_op jit(solution)/shard_map/product_nt/pallas_call | solution.py:495
  522.6 23.3 %product_nt.5 = f32[1024,2048]{1,0:T(8,128)} custom-call(bf16[2048,1536]{1,0:T(8,128)(2,1)} %get-tuple-element.78.refs_0_, bf16[2048,1536]{1,0:T(8,128)(2,1)} %all-gather.11.cloned.1.call-done.refs_1_, bf16[2048,2048]{1,0:T(8,128)(2,1)} %get-tuple-element.122.refs_2_, bf16[2048,2048]{1,0:T(8,128)(2,1)} %all-gather.7.cloned.1.call-done.refs_3_), custom_call_target="tpu_custom_call" | custom-call | flops 75161927680 | bytes 2097152 | tf_op jit(solution)/shard_map/product_nt/pallas_call | solution.py:495
  556.3 11.0 %collective-permute-done.11 = bf16[512,2048]{1,0:T(8,128)(2,1)} collective-permute-done((bf16[512,2048]{1,0:T(8,128)(2,1)}, bf16[512,2048]{1,0:T(8,128)(2,1)}, u32[]{:S(2)}, u32[]{:S(2)}) %collective-permute-start.11) | collective-permute-done | bytes 2097184 | tf_op jit(solution)/shard_map/ppermute | solution.py:346
  574.6 6.4 all-to-all-start.4
  584.7 24.3 %all-to-all-done.4 = f32[32,1,640]{2,1,0:T(1,128)S(1)} async-done(((f32[32,1,640]{2,1,0:T(1,128)}), f32[32,1,640]{2,1,0:T(1,128)S(1)}, u32[]{:S(2)}, u32[]{:S(2)}) %all-to-all-start.4) | async-done | bytes 81952 | tf_op jit(solution)/shard_map/all_to_all | solution.py:709
  629.4 16.0 %collective-permute-done.9 = bf16[256,2048]{1,0:T(8,128)(2,1)} collective-permute-done((bf16[256,2048]{1,0:T(8,128)(2,1)}, bf16[256,2048]{1,0:T(8,128)(2,1)}, u32[]{:S(2)}, u32[]{:S(2)}) %collective-permute-start.9) | collective-permute-done | bytes 1048608 | tf_op jit(solution)/shard_map/ppermute | solution.py:346
  (234 shorter events, 136.6 us)
Async XLA Ops:
  7.2 179.6 %all-gather.5.cloned.1.call-start = ((), (), s32[]{:S(2)}) async-start(), calls=%async_computation.9 | async-start | bytes 2359296 | tf_op jit(solution)/shard_map/all_gather | solution.py:421
  7.9 178.8 %all-gather.7.cloned.1.call-start = ((), (), s32[]{:S(2)}) async-start(), calls=%async_computation.10 | async-start | bytes 9437184 | tf_op jit(solution)/shard_map/all_gather | solution.py:421
  41.3 195.5 %all-gather.9.cloned.1.call-start = ((), (), s32[]{:S(2)}) async-start(), calls=%async_computation.11 | async-start | bytes 9437184 | tf_op jit(solution)/shard_map/all_gather | solution.py:421
  42.1 47.8 %collective-permute-start.1 = (bf16[512,2048]{1,0:T(8,128)(2,1)S(1)}, bf16[512,2048]{1,0:T(8,128)(2,1)}, u32[]{:S(2)}, u32[]{:S(2)}) collective-permute-start(bf16[512,2048]{1,0:T(8,128)(2,1)S(1)} %bitcast.52), channel_id=1, source_target_pairs={{0,2},{1,3},{2,0},{3,1},{4,6},{5,7},{6,4},{7,5},{8,10},{9,11},{10,... | collective-permute-start | bytes 6291464 | tf_op jit(solution)/shard_map/ppermute | solution.py:346
  43.0 46.9 %collective-permute-start = (bf16[512,2048]{1,0:T(8,128)(2,1)S(1)}, bf16[512,2048]{1,0:T(8,128)(2,1)}, u32[]{:S(2)}, u32[]{:S(2)}) collective-permute-start(bf16[512,2048]{1,0:T(8,128)(2,1)S(1)} %bitcast.53), channel_id=1, source_target_pairs={{0,1},{1,0},{2,3},{3,2},{4,5},{5,4},{6,7},{7,6},{8,9},{9,8},{10,11... | collective-permute-start | bytes 6291464 | tf_op jit(solution)/shard_map/ppermute | solution.py:346
  46.0 43.7 %all-to-all-start = ((bf16[32,2,352]{2,1,0:T(2,128)(2,1)}), bf16[32,2,352]{2,1,0:T(2,128)(2,1)S(1)}, u32[]{:S(2)}, u32[]{:S(2)}) async-start(bf16[32,2,352]{2,1,0:T(2,128)(2,1)} %reshape.317), calls=%async_computation | async-start | bytes 98304 | tf_op jit(solution)/shard_map/all_to_all | solution.py:417
  51.5 263.8 %all-gather.11.cloned.1.call-start = ((), (), s32[]{:S(2)}) async-start(), calls=%async_computation.12 | async-start | bytes 7077888 | tf_op jit(solution)/shard_map/all_gather | solution.py:421
  95.8 70.6 %collective-permute-start.3 = (bf16[768,2048]{1,0:T(8,128)(2,1)}, bf16[768,2048]{1,0:T(8,128)(2,1)}, u32[]{:S(2)}, u32[]{:S(2)}) collective-permute-start(bf16[768,2048]{1,0:T(8,128)(2,1)} %get-tuple-element.110), channel_id=1, source_target_pairs={{0,1},{1,0},{2,3},{3,2},{4,5},{5,4},{6,7},{7,6},{8,9},{9,8},{10,11... | collective-permute-start | bytes 9437192 | tf_op jit(solution)/shard_map/ppermute | solution.py:346
  97.1 72.8 %collective-permute-start.2 = (bf16[768,2048]{1,0:T(8,128)(2,1)}, bf16[768,2048]{1,0:T(8,128)(2,1)}, u32[]{:S(2)}, u32[]{:S(2)}) collective-permute-start(bf16[768,2048]{1,0:T(8,128)(2,1)} %get-tuple-element.111), channel_id=1, source_target_pairs={{0,2},{1,3},{2,0},{3,1},{4,6},{5,7},{6,4},{7,5},{8,10},{9,11},{10,... | collective-permute-start | bytes 9437192 | tf_op jit(solution)/shard_map/ppermute | solution.py:346
  112.5 300.7 %reduce-scatter.5.cloned.1.call-start = ((), (), s32[]{:S(2)}) async-start(), calls=%async_computation.13 | async-start | bytes 9437184 | tf_op jit(solution)/shard_map/reduce_scatter | solution.py:425
  168.7 50.6 %collective-permute-start.4 = (bf16[256,2048]{1,0:T(8,128)(2,1)}, bf16[256,2048]{1,0:T(8,128)(2,1)}, u32[]{:S(2)}, u32[]{:S(2)}) collective-permute-start(bf16[256,2048]{1,0:T(8,128)(2,1)} %slice.115), channel_id=1, source_target_pairs={{0,2},{1,3},{2,0},{3,1},{4,6},{5,7},{6,4},{7,5},{8,10},{9,11},{10,... | collective-permute-start | bytes 3145736 | tf_op jit(solution)/shard_map/ppermute | solution.py:346
  172.3 47.0 %collective-permute-start.5 = (bf16[256,2048]{1,0:T(8,128)(2,1)}, bf16[256,2048]{1,0:T(8,128)(2,1)}, u32[]{:S(2)}, u32[]{:S(2)}) collective-permute-start(bf16[256,2048]{1,0:T(8,128)(2,1)} %slice.116), channel_id=1, source_target_pairs={{0,1},{1,0},{2,3},{3,2},{4,5},{5,4},{6,7},{7,6},{8,9},{9,8},{10,11... | collective-permute-start | bytes 3145736 | tf_op jit(solution)/shard_map/ppermute | solution.py:346
  286.5 295.4 %reduce-scatter.7.cloned.1.call-start = ((), (), s32[]{:S(2)}) async-start(), calls=%async_computation.14 | async-start | bytes 9437184 | tf_op jit(solution)/shard_map/reduce_scatter | solution.py:425
  416.7 206.5 %reduce-scatter.11.cloned.1.call-start = ((), (), s32[]{:S(2)}) async-start(), calls=%async_computation.16 | async-start | bytes 2359296 | tf_op jit(solution)/shard_map/reduce_scatter | solution.py:425
  421.6 101.0 %collective-permute-start.6 = (bf16[512,2048]{1,0:T(8,128)(2,1)}, bf16[512,2048]{1,0:T(8,128)(2,1)}, u32[]{:S(2)}, u32[]{:S(2)}) collective-permute-start(bf16[512,2048]{1,0:T(8,128)(2,1)} %product_nn.3), channel_id=1, source_target_pairs={{0,2},{1,3},{2,0},{3,1},{4,6},{5,7},{6,4},{7,5},{8,10},{9,11},{10,... | collective-permute-start | bytes 6291464 | tf_op jit(solution)/shard_map/ppermute | solution.py:346
  443.5 79.1 %collective-permute-start.7 = (bf16[512,2048]{1,0:T(8,128)(2,1)}, bf16[512,2048]{1,0:T(8,128)(2,1)}, u32[]{:S(2)}, u32[]{:S(2)}) collective-permute-start(bf16[512,2048]{1,0:T(8,128)(2,1)} %product_nn.4), channel_id=1, source_target_pairs={{0,1},{1,0},{2,3},{3,2},{4,5},{5,4},{6,7},{7,6},{8,9},{9,8},{10,11... | collective-permute-start | bytes 6291464 | tf_op jit(solution)/shard_map/ppermute | solution.py:346
  474.1 151.0 %reduce-scatter.9.cloned.1.call-start = ((), (), s32[]{:S(2)}) async-start(), calls=%async_computation.15 | async-start | bytes 7077888 | tf_op jit(solution)/shard_map/reduce_scatter | solution.py:425
  505.0 51.2 %collective-permute-start.10 = (bf16[512,2048]{1,0:T(8,128)(2,1)}, bf16[512,2048]{1,0:T(8,128)(2,1)S(1)}, u32[]{:S(2)}, u32[]{:S(2)}) collective-permute-start(bf16[512,2048]{1,0:T(8,128)(2,1)} %product_nt.3), channel_id=1, source_target_pairs={{0,2},{1,3},{2,0},{3,1},{4,6},{5,7},{6,4},{7,5},{8,10},{9,11},{10,... | collective-permute-start | bytes 6291464 | tf_op jit(solution)/shard_map/ppermute | solution.py:346
  518.4 48.9 %collective-permute-start.11 = (bf16[512,2048]{1,0:T(8,128)(2,1)}, bf16[512,2048]{1,0:T(8,128)(2,1)}, u32[]{:S(2)}, u32[]{:S(2)}) collective-permute-start(bf16[512,2048]{1,0:T(8,128)(2,1)} %product_nt.4), channel_id=1, source_target_pairs={{0,1},{1,0},{2,3},{3,2},{4,5},{5,4},{6,7},{7,6},{8,9},{9,8},{10,11... | collective-permute-start | bytes 6291464 | tf_op jit(solution)/shard_map/ppermute | solution.py:346
  554.6 54.5 %collective-permute-start.8 = (bf16[256,2048]{1,0:T(8,128)(2,1)}, bf16[256,2048]{1,0:T(8,128)(2,1)}, u32[]{:S(2)}, u32[]{:S(2)}) collective-permute-start(bf16[256,2048]{1,0:T(8,128)(2,1)} %add_convert_fusion.1), channel_id=1, source_target_pairs={{0,1},{1,0},{2,3},{3,2},{4,5},{5,4},{6,7},{7,6},{8,9},{9,8},{10,11... | collective-permute-start | bytes 3145736 | tf_op jit(solution)/shard_map/ppermute | solution.py:346
  572.0 45.2 %collective-permute-start.12 = (bf16[256,2048]{1,0:T(8,128)(2,1)}, bf16[256,2048]{1,0:T(8,128)(2,1)S(1)}, u32[]{:S(2)}, u32[]{:S(2)}) collective-permute-start(bf16[256,2048]{1,0:T(8,128)(2,1)} %get-tuple-element.80), channel_id=1, source_target_pairs={{0,1},{1,0},{2,3},{3,2},{4,5},{5,4},{6,7},{7,6},{8,9},{9,8},{10,11... | collective-permute-start | bytes 3145736 | tf_op jit(solution)/shard_map/ppermute | solution.py:346
  572.4 44.8 %collective-permute-start.13 = (bf16[256,2048]{1,0:T(8,128)(2,1)}, bf16[256,2048]{1,0:T(8,128)(2,1)}, u32[]{:S(2)}, u32[]{:S(2)}) collective-permute-start(bf16[256,2048]{1,0:T(8,128)(2,1)} %get-tuple-element.81), channel_id=1, source_target_pairs={{0,2},{1,3},{2,0},{3,1},{4,6},{5,7},{6,4},{7,5},{8,10},{9,11},{10,... | collective-permute-start | bytes 3145736 | tf_op jit(solution)/shard_map/ppermute | solution.py:346
  574.6 34.3 %all-to-all-start.4 = ((f32[32,1,640]{2,1,0:T(1,128)}), f32[32,1,640]{2,1,0:T(1,128)S(1)}, u32[]{:S(2)}, u32[]{:S(2)}) async-start(f32[32,1,640]{2,1,0:T(1,128)} %all_to_all.26), calls=%async_computation.7 | async-start | bytes 163840 | tf_op jit(solution)/shard_map/all_to_all | solution.py:709
  614.9 30.5 %collective-permute-start.9 = (bf16[256,2048]{1,0:T(8,128)(2,1)}, bf16[256,2048]{1,0:T(8,128)(2,1)}, u32[]{:S(2)}, u32[]{:S(2)}) collective-permute-start(bf16[256,2048]{1,0:T(8,128)(2,1)} %get-tuple-element.109), channel_id=1, source_target_pairs={{0,2},{1,3},{2,0},{3,1},{4,6},{5,7},{6,4},{7,5},{8,10},{9,11},{10,... | collective-permute-start | bytes 3145736 | tf_op jit(solution)/shard_map/ppermute | solution.py:346
  (42 other events, 781.4 us)
Sparse Core Ops, SparseCore 0:
  9.6 31.7 all-gather.4
  43.6 82.3 all-gather.6
  127.6 80.6 all-gather.8
  210.4 63.2 all-gather.10
  286.7 90.4 reduce-scatter.4
  379.3 87.9 reduce-scatter.6
  474.3 35.8 reduce-scatter.10
  512.5 68.6 reduce-scatter.8

commit v8 on v7

--- a/solution.py
+++ b/solution.py
@@ -398,14 +398,14 @@
     return tuple(exchange(x.astype(BF), "ctx", size, j) for x, j in zip(pieces, distances))
 
 
-def sum_end(own, arrived, size, together=False):
+def sum_end(own, arrived, size):
     if size != 4:
         return sum([x.astype(F32) for x in arrived], own), arrived, arrived
     half = own.shape[0] // 4
     far, near = arrived
     top = (own[2 * half : 3 * half] + far[half:].astype(F32)).astype(BF)
     low = (own[3 * half :] + near[half:].astype(F32)).astype(BF)
-    sent = lax.optimization_barrier((top, low)) if together else (top, low)
+    sent = lax.optimization_barrier((top, low))
     last = (exchange(sent[0], "ctx", size, 1), exchange(sent[1], "ctx", size, 2))
     top = own[:half] + far[:half].astype(F32) + last[0].astype(F32)
     low = own[half : 2 * half] + near[:half].astype(F32) + last[1].astype(F32)
@@ -654,11 +654,9 @@
         pairs = [(active, w_down_own), (attended, w_out_own)]
         return product("nn", pairs, (dtype,), row_range=[i * step for i in half_range])
 
-    out_away = [out_rows(r, BF, attended) for r in away_ranges[:1]]
-    attended_then = after(attended, up_grad, *out_away)
-    out_away += [out_rows(r, BF, attended_then) for r in away_ranges[1:]]
-    out_arrived = sum_send(out_away, C)
-    out_part = outer(after(attended, *out_away), grad_all)
+    qkv_part = outer(after(normed, up_rows_grad), d_qkv).astype(BF)
+    _, qkv_grad = column_grad(qkv_part, qkv_chunks)
+    out_part = outer(after(attended, qkv_part), grad_all)
     if aligned:
         out_part = out_part.astype(BF)
         out_grad = scatter_dp(out_part)
@@ -671,9 +669,12 @@
             spread.reshape(heads * HEAD, width), ALL, scatter_dimension=0, tiled=True
         )
 
-    qkv_part = outer(after(normed, up_rows_grad, out_part), d_qkv).astype(BF)
-    _, qkv_grad = column_grad(qkv_part, qkv_chunks)
-    out_near = out_rows(near_range, F32, after(attended, qkv_part))
+    attended_first = after(attended, out_part)
+    out_away = [out_rows(r, BF, attended_first) for r in away_ranges[:1]]
+    attended_then = after(attended, up_grad, *out_away)
+    out_away += [out_rows(r, BF, attended_then) for r in away_ranges[1:]]
+    out_arrived = sum_send(out_away, C)
+    out_near = out_rows(near_range, F32, after(attended, *out_away))
 
     def normed_rows(half_range, dtype, d_qkv):
         pairs = [(d_qkv, w_qkv_own), (d_up, w_up_own)]
@@ -704,12 +705,12 @@
     qkv_bias_grad = jnp.where(mine[None, None, None, :, None], qkv_bias_grad, 0.0)
     small = [gain_grad, shift_grad, qkv_bias_grad, bias_grad, up_bias_grad]
     small = jnp.concatenate([s.reshape(devices, -1) for s in small], axis=1)
-    d_normed, _, d_sent = sum_end(d_near, d_arrived, C, True)
+    d_normed, _, d_sent = sum_end(d_near, d_arrived, C)
     small = after(small, *d_sent)
     small = lax.all_to_all(small, ALL, split_axis=0, concat_axis=0, tiled=True)
     small = jnp.split(jnp.sum(small, axis=0), cuts[:4])
 
-    d_normed = after(d_normed, down_rows, qkv_grad, *small)
+    d_normed = after(d_normed, down_rows, *small)
     xhat, scale = standardise(hidden_own.astype(F32))
     e = d_normed * gain
     d_hidden = e - jnp.mean(e, axis=-1, keepdims=True)

time: 677 us -> 650 us (0.960)
  the two profiles are of different devices: /device:TPU:0 before, /device:TPU:20 now
where the time goes in v8:
time: 650 us; the launch traced here: 638 us
  Pallas kernels  184 us (28%)
  matrix products  165 us (25%)
  waiting for transfers between devices  124 us (19%)
  other arithmetic  63.1 us (10%)
  starting transfers between devices  35.3 us (5%)
  local copies, waits for them, and re-layouts  25.9 us (4%)
  blocking collectives  25.9 us (4%)
  between operations  15.2 us (2%)
    pallas_call x6, Pallas kernels, product(): pl.pallas_call(kernel, grid=(columns // wide, (high - low) // tall), in_s...  87.7 us
    ppermute x14, waiting for transfers between devices, exchange(): return lax.ppermute(value, axis, [(i, i ^ offset) for i in range(size)])  77.4 us
    dot_general x4, matrix products, outer(): lax.dot_general(a, b, (((0,), (0,)), ((), ())), preferred_element_type=F32)  77.4 us
    pallas_call x1, Pallas kernels, attention(): pl.pallas_call(attention_kernel, out_shape=[jax.ShapeDtypeStruct((slots,...  66.1 us
    dot_general x2, matrix products, matmul(): return jnp.dot(a, b, preferred_element_type=F32)  51.8 us
    all_to_all x1, waiting for transfers between devices, gather_small(): return lax.all_to_all(copies, ALL, split_axis=0, concat_axis=0, tiled=True)  36.2 us
    dot_general x2, matrix products, matmul_t(): lax.dot_general(a, b, (((1,), (1,)), ((), ())), preferred_element_type=F32)  35.4 us
    all_to_all x1, blocking collectives, swap_ctx(): return lax.all_to_all(value, 'ctx', split_axis=0, concat_axis=0, tiled=True)  25.9 us
  transfers between devices with their start and end apart: 26, of which 6 were waited for; matrix products, arithmetic and copies ran while one was open for 39% of the time, Pallas kernels for 28%

profile of v8, /device:TPU:20, one launch (start us, length us, event | category | flops | bytes accessed | tf_op | source)
XLA Modules:
  0.0 638.2 jit_solution(1426971915213059720)
XLA Ops:
  11.1 25.9 %all_to_all.33 = bf16[4,64,3584]{2,1,0:T(8,128)(2,1)S(1)} all-to-all(bf16[4,64,3584]{2,1,0:T(8,128)(2,1)} %deal_columns.1), channel_id=1, replica_groups=mesh['dp'=8,'ctx'=4] {'ctx'}, dimensions={0} | all-to-all | bytes 3670016 | tf_op jit(solution)/shard_map/all_to_all | solution.py:429
  52.1 36.2 %all-to-all-done = bf16[32,2,352]{2,1,0:T(2,128)(2,1)S(1)} async-done(((bf16[32,2,352]{2,1,0:T(2,128)(2,1)}), bf16[32,2,352]{2,1,0:T(2,128)(2,1)S(1)}, u32[]{:S(2)}, u32[]{:S(2)}) %all-to-all-start) | async-done | bytes 45088 | tf_op jit(solution)/shard_map/all_to_all | solution.py:417
  111.3 53.7 %collective-permute-done.3.refs_4_.refs_1_ = bf16[768,2048]{1,0:T(8,128)(2,1)} collective-permute-done((bf16[768,2048]{1,0:T(8,128)(2,1)}, bf16[768,2048]{1,0:T(8,128)(2,1)}, u32[]{:S(2)}, u32[]{:S(2)}) %collective-permute-start.3) | collective-permute-done | bytes 3145760 | tf_op jit(solution)/shard_map/ppermute | solution.py:346
  171.7 13.7 %norm_rows.1 = (bf16[2048,2048]{1,0:T(8,128)(2,1)}, bf16[2048,2048]{1,0:T(8,128)(2,1)}) custom-call(bf16[512,2048]{1,0:T(8,128)(2,1)S(1)} %bitcast.54, bf16[512,2048]{1,0:T(8,128)(2,1)} %collective-permute-done.refs_1_, bf16[512,2048]{1,0:T(8,128)(2,1)} %collective-permute-done.1.refs_2_, bf16[768,2048]{1,0:T(8,128)(2,1)} %collective-permute-done.2.refs_3_.refs_2_, ...), custom_call_target="tpu_custom_call" | custom-call | flops 41943040 | bytes 16777216 | tf_op jit(solution)/shard_map/norm_rows/pallas_call | solution.py:276
  185.4 32.4 %multiply_add_fusion = (f32[2048,2048]{1,0:T(8,128)}, bf16[2048,2048]{1,0:T(8,128)(2,1)}) fusion(f32[2048]{0:T(1024)S(1)} %bitcast.70, bf16[2048,2048]{1,0:T(8,128)(2,1)} %get-tuple-element.75, bf16[2048,2048]{1,0:T(8,128)(2,1)} %all-gather.7.cloned.1.call-done.refs_3_), kind=kOutput, calls=%fused_computation.5 | convolution fusion | flops 17242783744 | bytes 41951232 | tf_op jit(solution)/shard_map/dot_general | solution.py:433
  217.8 8.3 %join_rows.1 = bf16[2048,2048]{1,0:T(8,128)(2,1)} custom-call(bf16[512,2048]{1,0:T(8,128)(2,1)S(1)} %bitcast.56, bf16[768,2048]{1,0:T(8,128)(2,1)} %collective-permute-done.3.refs_4_.refs_1_, bf16[768,2048]{1,0:T(8,128)(2,1)} %collective-permute-done.2.refs_3_.refs_2_, bf16[256,2048]{1,0:T(8,128)(2,1)} %collective-permute-done.4.refs_3_, ...), custom_call_target="tpu_custom_call" | custom-call | flops 41943040 | bytes 16777216 | tf_op jit(solution)/shard_map/join_rows/pallas_call | solution.py:276
  226.1 9.3 %convolution_convert_fusion.4.cot_ref = bf16[2048,512]{1,0:T(8,128)(2,1)} fusion(bf16[2048,2048]{1,0:T(8,128)(2,1)} %join_rows.1, bf16[512,2048]{1,0:T(8,128)(2,1)S(1)} %copy-done.36), kind=kOutput, calls=%fused_computation.42 | convolution fusion | flops 4296015872 | bytes 12582912 | tf_op jit(solution)/shard_map/dot_general | solution.py:437
  235.4 26.1 %convert_reduce_fusion = (f32[2048]{0:T(1024)S(1)}, bf16[2048,2048]{1,0:T(8,128)(2,1)}) fusion(f32[2048,2048]{1,0:T(8,128)} %get-tuple-element.68, bf16[2048,2048]{1,0:T(8,128)(2,1)} %join_rows.1, bf16[2048,2048]{1,0:T(8,128)(2,1)} %all-gather.9.cloned.1.call-done.refs_1_), kind=kOutput, calls=%fused_computation.3 | convolution fusion | flops 17196644352 | bytes 41951232 | tf_op jit(solution)/shard_map/dot_general | solution.py:437
  261.5 23.8 %convolution_convert_fusion.1 = bf16[2048,2048]{1,0:T(8,128)(2,1)} fusion(bf16[2048,2048]{1,0:T(8,128)(2,1)} %get-tuple-element.75, bf16[2048,2048]{1,0:T(8,128)(2,1)} %get-tuple-element.130.refs_2_), kind=kOutput, calls=%fused_computation.13 | convolution fusion | flops 17184063488 | bytes 25165824 | tf_op jit(solution)/shard_map/dot_general | solution.py:441
  285.4 23.9 %convolution_convert_fusion = bf16[2048,2048]{1,0:T(8,128)(2,1)} fusion(bf16[2048,2048]{1,0:T(8,128)(2,1)} %get-tuple-element.69.refs_0_, bf16[2048,2048]{1,0:T(8,128)(2,1)} %join_rows.1), kind=kOutput, calls=%fused_computation.12 | convolution fusion | flops 17184063488 | bytes 25165824 | tf_op jit(solution)/shard_map/dot_general | solution.py:441
  310.2 19.4 %convolution_add_fusion.qkv_ref = f32[2048,1536]{1,0:T(8,128)} fusion(bf16[2048,2048]{1,0:T(8,128)(2,1)} %get-tuple-element.75, bf16[2048,1536]{1,0:T(8,128)(2,1)} %all-gather.11.cloned.1.call-done.refs_1_, f32[1536]{0:T(1024)S(1)} %copy-done.26), kind=kOutput, calls=%fused_computation.10 | convolution fusion | flops 12888047616 | bytes 27269120 | tf_op jit(solution)/shard_map/dot_general | solution.py:433
  329.6 66.1 %attention.1 = (bf16[2048,512]{1,0:T(8,128)(2,1)}, bf16[2048,1536]{1,0:T(8,128)(2,1)}) custom-call(s32[16]{0:T(128)S(1)} %copy-done.8, s32[16]{0:T(128)S(1)} %copy-done.10, s32[16]{0:T(128)S(1)} %and_select_fusion.low_ref, f32[2048,1536]{1,0:T(8,128)} %convolution_add_fusion.qkv_ref, bf16[2048,512]{1,0:T(8,128)(2,1)} %convolution_convert_fusion.4.cot_ref, ...), custom_call_target="tpu_custom_call" | custom-call | flops 1073741824 | bytes 3145728 | tf_op jit(solution)/shard_map/attention/pallas_call | solution.py:229
  395.7 19.6 %convolution_convert_fusion.2 = bf16[2048,1536]{1,0:T(8,128)(2,1)} fusion(bf16[2048,2048]{1,0:T(8,128)(2,1)} %get-tuple-element.75, bf16[2048,1536]{1,0:T(8,128)(2,1)} %get-tuple-element.82.refs_0_), kind=kOutput, calls=%fused_computation.14 | convolution fusion | flops 12888047616 | bytes 20971520 | tf_op jit(solution)/shard_map/dot_general | solution.py:441
  430.8 10.0 %convolution_convert_fusion.3 = bf16[512,2048]{1,0:T(8,128)(2,1)} fusion(bf16[2048,512]{1,0:T(8,128)(2,1)} %get-tuple-element.80.refs_2_, bf16[2048,2048]{1,0:T(8,128)(2,1)} %join_rows.1), kind=kOutput, calls=%fused_computation.41 | convolution fusion | flops 4296015872 | bytes 12582912 | tf_op jit(solution)/shard_map/dot_general | solution.py:441
  440.9 10.2 %product_nn.3 = bf16[512,2048]{1,0:T(8,128)(2,1)} custom-call(bf16[2048,2048]{1,0:T(8,128)(2,1)} %get-tuple-element.69.refs_0_, bf16[2048,2048]{1,0:T(8,128)(2,1)} %all-gather.9.cloned.1.call-done.refs_1_, bf16[2048,512]{1,0:T(8,128)(2,1)} %get-tuple-element.80.refs_2_, bf16[512,2048]{1,0:T(8,128)(2,1)} %all-gather.5.cloned.1.call-done.refs_3_), custom_call_target="tpu_custom_call" | custom-call | flops 26843545600 | bytes 1048576 | tf_op jit(solution)/shard_map/product_nn/pallas_call | solution.py:495
  454.9 10.0 %product_nn.4 = bf16[512,2048]{1,0:T(8,128)(2,1)} custom-call(bf16[2048,2048]{1,0:T(8,128)(2,1)} %get-tuple-element.69.refs_0_, bf16[2048,2048]{1,0:T(8,128)(2,1)} %all-gather.9.cloned.1.call-done.refs_1_, bf16[2048,512]{1,0:T(8,128)(2,1)} %get-tuple-element.80.refs_2_, bf16[512,2048]{1,0:T(8,128)(2,1)} %all-gather.5.cloned.1.call-done.refs_3_), custom_call_target="tpu_custom_call" | custom-call | flops 26843545600 | bytes 1048576 | tf_op jit(solution)/shard_map/product_nn/pallas_call | solution.py:495
  466.8 17.2 %product_nn.5 = f32[1024,2048]{1,0:T(8,128)} custom-call(bf16[2048,2048]{1,0:T(8,128)(2,1)} %get-tuple-element.69.refs_0_, bf16[2048,2048]{1,0:T(8,128)(2,1)} %all-gather.9.cloned.1.call-done.refs_1_, bf16[2048,512]{1,0:T(8,128)(2,1)} %get-tuple-element.80.refs_2_, bf16[512,2048]{1,0:T(8,128)(2,1)} %all-gather.5.cloned.1.call-done.refs_3_), custom_call_target="tpu_custom_call" | custom-call | flops 53687091200 | bytes 2097152 | tf_op jit(solution)/shard_map/product_nn/pallas_call | solution.py:495
  484.0 13.4 %product_nt.3 = bf16[512,2048]{1,0:T(8,128)(2,1)} custom-call(bf16[2048,1536]{1,0:T(8,128)(2,1)} %get-tuple-element.82.refs_0_, bf16[2048,1536]{1,0:T(8,128)(2,1)} %all-gather.11.cloned.1.call-done.refs_1_, bf16[2048,2048]{1,0:T(8,128)(2,1)} %get-tuple-element.130.refs_2_, bf16[2048,2048]{1,0:T(8,128)(2,1)} %all-gather.7.cloned.1.call-done.refs_3_), custom_call_target="tpu_custom_call" | custom-call | flops 37580963840 | bytes 1048576 | tf_op jit(solution)/shard_map/product_nt/pallas_call | solution.py:495
  498.8 13.3 %product_nt.4 = bf16[512,2048]{1,0:T(8,128)(2,1)} custom-call(bf16[2048,1536]{1,0:T(8,128)(2,1)} %get-tuple-element.82.refs_0_, bf16[2048,1536]{1,0:T(8,128)(2,1)} %all-gather.11.cloned.1.call-done.refs_1_, bf16[2048,2048]{1,0:T(8,128)(2,1)} %get-tuple-element.130.refs_2_, bf16[2048,2048]{1,0:T(8,128)(2,1)} %all-gather.7.cloned.1.call-done.refs_3_), custom_call_target="tpu_custom_call" | custom-call | flops 37580963840 | bytes 1048576 | tf_op jit(solution)/shard_map/product_nt/pallas_call | solution.py:495
  516.6 23.7 %product_nt.5 = f32[1024,2048]{1,0:T(8,128)} custom-call(bf16[2048,1536]{1,0:T(8,128)(2,1)} %get-tuple-element.82.refs_0_, bf16[2048,1536]{1,0:T(8,128)(2,1)} %all-gather.11.cloned.1.call-done.refs_1_, bf16[2048,2048]{1,0:T(8,128)(2,1)} %get-tuple-element.130.refs_2_, bf16[2048,2048]{1,0:T(8,128)(2,1)} %all-gather.7.cloned.1.call-done.refs_3_), custom_call_target="tpu_custom_call" | custom-call | flops 75161927680 | bytes 2097152 | tf_op jit(solution)/shard_map/product_nt/pallas_call | solution.py:495
  545.9 13.7 %collective-permute-done.11 = bf16[512,2048]{1,0:T(8,128)(2,1)} collective-permute-done((bf16[512,2048]{1,0:T(8,128)(2,1)}, bf16[512,2048]{1,0:T(8,128)(2,1)}, u32[]{:S(2)}, u32[]{:S(2)}) %collective-permute-start.11) | collective-permute-done | bytes 2097184 | tf_op jit(solution)/shard_map/ppermute | solution.py:346
  567.1 6.8 %all-to-all-start.3 = ((f32[32,1,640]{2,1,0:T(1,128)}), f32[32,1,640]{2,1,0:T(1,128)S(1)}, u32[]{:S(2)}, u32[]{:S(2)}) async-start(f32[32,1,640]{2,1,0:T(1,128)} %all_to_all.25), calls=%async_computation.5 | async-start | bytes 163840 | tf_op jit(solution)/shard_map/all_to_all | solution.py:710
  583.2 9.1 %all-to-all-done.3 = f32[32,1,640]{2,1,0:T(1,128)S(1)} async-done(((f32[32,1,640]{2,1,0:T(1,128)}), f32[32,1,640]{2,1,0:T(1,128)S(1)}, u32[]{:S(2)}, u32[]{:S(2)}) %all-to-all-start.3) | async-done | bytes 81952 | tf_op jit(solution)/shard_map/all_to_all | solution.py:710
  612.6 6.1 collective-permute-done.9
  (227 shorter events, 131.1 us)
Async XLA Ops:
  7.2 178.2 %all-gather.5.cloned.1.call-start = ((), (), s32[]{:S(2)}) async-start(), calls=%async_computation.9 | async-start | bytes 2359296 | tf_op jit(solution)/shard_map/all_gather | solution.py:421
  7.9 177.5 %all-gather.7.cloned.1.call-start = ((), (), s32[]{:S(2)}) async-start(), calls=%async_computation.10 | async-start | bytes 9437184 | tf_op jit(solution)/shard_map/all_gather | solution.py:421
  39.4 196.0 %all-gather.9.cloned.1.call-start = ((), (), s32[]{:S(2)}) async-start(), calls=%async_computation.11 | async-start | bytes 9437184 | tf_op jit(solution)/shard_map/all_gather | solution.py:421
  40.1 48.3 %collective-permute-start.1 = (bf16[512,2048]{1,0:T(8,128)(2,1)S(1)}, bf16[512,2048]{1,0:T(8,128)(2,1)}, u32[]{:S(2)}, u32[]{:S(2)}) collective-permute-start(bf16[512,2048]{1,0:T(8,128)(2,1)S(1)} %bitcast.52), channel_id=1, source_target_pairs={{0,2},{1,3},{2,0},{3,1},{4,6},{5,7},{6,4},{7,5},{8,10},{9,11},{10,... | collective-permute-start | bytes 6291464 | tf_op jit(solution)/shard_map/ppermute | solution.py:346
  41.3 47.1 %collective-permute-start = (bf16[512,2048]{1,0:T(8,128)(2,1)S(1)}, bf16[512,2048]{1,0:T(8,128)(2,1)}, u32[]{:S(2)}, u32[]{:S(2)}) collective-permute-start(bf16[512,2048]{1,0:T(8,128)(2,1)S(1)} %bitcast.53), channel_id=1, source_target_pairs={{0,1},{1,0},{2,3},{3,2},{4,5},{5,4},{6,7},{7,6},{8,9},{9,8},{10,11... | collective-permute-start | bytes 6291464 | tf_op jit(solution)/shard_map/ppermute | solution.py:346
  44.6 43.7 %all-to-all-start = ((bf16[32,2,352]{2,1,0:T(2,128)(2,1)}), bf16[32,2,352]{2,1,0:T(2,128)(2,1)S(1)}, u32[]{:S(2)}, u32[]{:S(2)}) async-start(bf16[32,2,352]{2,1,0:T(2,128)(2,1)} %reshape.317), calls=%async_computation | async-start | bytes 98304 | tf_op jit(solution)/shard_map/all_to_all | solution.py:417
  50.1 260.0 %all-gather.11.cloned.1.call-start = ((), (), s32[]{:S(2)}) async-start(), calls=%async_computation.12 | async-start | bytes 7077888 | tf_op jit(solution)/shard_map/all_gather | solution.py:421
  94.4 70.6 %collective-permute-start.3 = (bf16[768,2048]{1,0:T(8,128)(2,1)}, bf16[768,2048]{1,0:T(8,128)(2,1)}, u32[]{:S(2)}, u32[]{:S(2)}) collective-permute-start(bf16[768,2048]{1,0:T(8,128)(2,1)} %get-tuple-element.118), channel_id=1, source_target_pairs={{0,1},{1,0},{2,3},{3,2},{4,5},{5,4},{6,7},{7,6},{8,9},{9,8},{10,11... | collective-permute-start | bytes 9437192 | tf_op jit(solution)/shard_map/ppermute | solution.py:346
  95.0 73.1 %collective-permute-start.2 = (bf16[768,2048]{1,0:T(8,128)(2,1)}, bf16[768,2048]{1,0:T(8,128)(2,1)}, u32[]{:S(2)}, u32[]{:S(2)}) collective-permute-start(bf16[768,2048]{1,0:T(8,128)(2,1)} %get-tuple-element.119), channel_id=1, source_target_pairs={{0,2},{1,3},{2,0},{3,1},{4,6},{5,7},{6,4},{7,5},{8,10},{9,11},{10,... | collective-permute-start | bytes 9437192 | tf_op jit(solution)/shard_map/ppermute | solution.py:346
  111.2 284.5 %reduce-scatter.5.cloned.1.call-start = ((), (), s32[]{:S(2)}) async-start(), calls=%async_computation.13 | async-start | bytes 9437184 | tf_op jit(solution)/shard_map/reduce_scatter | solution.py:425
  167.3 50.5 %collective-permute-start.4 = (bf16[256,2048]{1,0:T(8,128)(2,1)}, bf16[256,2048]{1,0:T(8,128)(2,1)}, u32[]{:S(2)}, u32[]{:S(2)}) collective-permute-start(bf16[256,2048]{1,0:T(8,128)(2,1)} %slice.115), channel_id=1, source_target_pairs={{0,2},{1,3},{2,0},{3,1},{4,6},{5,7},{6,4},{7,5},{8,10},{9,11},{10,... | collective-permute-start | bytes 3145736 | tf_op jit(solution)/shard_map/ppermute | solution.py:346
  170.4 47.4 %collective-permute-start.5 = (bf16[256,2048]{1,0:T(8,128)(2,1)}, bf16[256,2048]{1,0:T(8,128)(2,1)}, u32[]{:S(2)}, u32[]{:S(2)}) collective-permute-start(bf16[256,2048]{1,0:T(8,128)(2,1)} %slice.116), channel_id=1, source_target_pairs={{0,1},{1,0},{2,3},{3,2},{4,5},{5,4},{6,7},{7,6},{8,9},{9,8},{10,11... | collective-permute-start | bytes 3145736 | tf_op jit(solution)/shard_map/ppermute | solution.py:346
  285.3 293.0 %reduce-scatter.7.cloned.1.call-start = ((), (), s32[]{:S(2)}) async-start(), calls=%async_computation.14 | async-start | bytes 9437184 | tf_op jit(solution)/shard_map/reduce_scatter | solution.py:425
  309.3 294.9 %reduce-scatter.9.cloned.1.call-start = ((), (), s32[]{:S(2)}) async-start(), calls=%async_computation.15 | async-start | bytes 7077888 | tf_op jit(solution)/shard_map/reduce_scatter | solution.py:425
  430.8 194.3 %reduce-scatter.11.cloned.1.call-start = ((), (), s32[]{:S(2)}) async-start(), calls=%async_computation.16 | async-start | bytes 2359296 | tf_op jit(solution)/shard_map/reduce_scatter | solution.py:425
  451.1 65.5 %collective-permute-start.6 = (bf16[512,2048]{1,0:T(8,128)(2,1)}, bf16[512,2048]{1,0:T(8,128)(2,1)}, u32[]{:S(2)}, u32[]{:S(2)}) collective-permute-start(bf16[512,2048]{1,0:T(8,128)(2,1)} %product_nn.3), channel_id=1, source_target_pairs={{0,2},{1,3},{2,0},{3,1},{4,6},{5,7},{6,4},{7,5},{8,10},{9,11},{10,... | collective-permute-start | bytes 6291464 | tf_op jit(solution)/shard_map/ppermute | solution.py:346
  464.9 51.7 %collective-permute-start.7 = (bf16[512,2048]{1,0:T(8,128)(2,1)}, bf16[512,2048]{1,0:T(8,128)(2,1)S(1)}, u32[]{:S(2)}, u32[]{:S(2)}) collective-permute-start(bf16[512,2048]{1,0:T(8,128)(2,1)} %product_nn.4), channel_id=1, source_target_pairs={{0,1},{1,0},{2,3},{3,2},{4,5},{5,4},{6,7},{7,6},{8,9},{9,8},{10,11... | collective-permute-start | bytes 6291464 | tf_op jit(solution)/shard_map/ppermute | solution.py:346
  497.3 48.6 %collective-permute-start.10 = (bf16[512,2048]{1,0:T(8,128)(2,1)}, bf16[512,2048]{1,0:T(8,128)(2,1)}, u32[]{:S(2)}, u32[]{:S(2)}) collective-permute-start(bf16[512,2048]{1,0:T(8,128)(2,1)} %product_nt.3), channel_id=1, source_target_pairs={{0,2},{1,3},{2,0},{3,1},{4,6},{5,7},{6,4},{7,5},{8,10},{9,11},{10,... | collective-permute-start | bytes 6291464 | tf_op jit(solution)/shard_map/ppermute | solution.py:346
  512.1 47.5 %collective-permute-start.11 = (bf16[512,2048]{1,0:T(8,128)(2,1)}, bf16[512,2048]{1,0:T(8,128)(2,1)}, u32[]{:S(2)}, u32[]{:S(2)}) collective-permute-start(bf16[512,2048]{1,0:T(8,128)(2,1)} %product_nt.4), channel_id=1, source_target_pairs={{0,1},{1,0},{2,3},{3,2},{4,5},{5,4},{6,7},{7,6},{8,9},{9,8},{10,11... | collective-permute-start | bytes 6291464 | tf_op jit(solution)/shard_map/ppermute | solution.py:346
  564.5 29.5 %collective-permute-start.12 = (bf16[256,2048]{1,0:T(8,128)(2,1)}, bf16[256,2048]{1,0:T(8,128)(2,1)S(1)}, u32[]{:S(2)}, u32[]{:S(2)}) collective-permute-start(bf16[256,2048]{1,0:T(8,128)(2,1)} %get-tuple-element.86), channel_id=1, source_target_pairs={{0,1},{1,0},{2,3},{3,2},{4,5},{5,4},{6,7},{7,6},{8,9},{9,8},{10,11... | collective-permute-start | bytes 3145736 | tf_op jit(solution)/shard_map/ppermute | solution.py:346
  565.1 29.0 %collective-permute-start.13 = (bf16[256,2048]{1,0:T(8,128)(2,1)}, bf16[256,2048]{1,0:T(8,128)(2,1)}, u32[]{:S(2)}, u32[]{:S(2)}) collective-permute-start(bf16[256,2048]{1,0:T(8,128)(2,1)} %get-tuple-element.87), channel_id=1, source_target_pairs={{0,2},{1,3},{2,0},{3,1},{4,6},{5,7},{6,4},{7,5},{8,10},{9,11},{10,... | collective-permute-start | bytes 3145736 | tf_op jit(solution)/shard_map/ppermute | solution.py:346
  567.1 25.2 %all-to-all-start.3 = ((f32[32,1,640]{2,1,0:T(1,128)}), f32[32,1,640]{2,1,0:T(1,128)S(1)}, u32[]{:S(2)}, u32[]{:S(2)}) async-start(f32[32,1,640]{2,1,0:T(1,128)} %all_to_all.25), calls=%async_computation.5 | async-start | bytes 163840 | tf_op jit(solution)/shard_map/all_to_all | solution.py:710
  581.1 31.5 %collective-permute-start.8 = (bf16[256,2048]{1,0:T(8,128)(2,1)}, bf16[256,2048]{1,0:T(8,128)(2,1)}, u32[]{:S(2)}, u32[]{:S(2)}) collective-permute-start(bf16[256,2048]{1,0:T(8,128)(2,1)} %get-tuple-element.84), channel_id=1, source_target_pairs={{0,1},{1,0},{2,3},{3,2},{4,5},{5,4},{6,7},{7,6},{8,9},{9,8},{10,11... | collective-permute-start | bytes 3145736 | tf_op jit(solution)/shard_map/ppermute | solution.py:346
  582.6 36.1 %collective-permute-start.9 = (bf16[256,2048]{1,0:T(8,128)(2,1)}, bf16[256,2048]{1,0:T(8,128)(2,1)}, u32[]{:S(2)}, u32[]{:S(2)}) collective-permute-start(bf16[256,2048]{1,0:T(8,128)(2,1)} %get-tuple-element.85), channel_id=1, source_target_pairs={{0,2},{1,3},{2,0},{3,1},{4,6},{5,7},{6,4},{7,5},{8,10},{9,11},{10,... | collective-permute-start | bytes 3145736 | tf_op jit(solution)/shard_map/ppermute | solution.py:346
  (39 other events, 744.4 us)
Sparse Core Ops, SparseCore 0:
  9.6 29.6 all-gather.4
  41.4 81.2 all-gather.6
  124.4 80.7 all-gather.8
  207.3 63.3 all-gather.10
  285.5 87.3 reduce-scatter.4
  374.9 87.9 reduce-scatter.6
  465.2 68.1 reduce-scatter.8
  535.7 30.3 reduce-scatter.10
